TPU v7x, 32 devices: a whole 2x2x4 slice. The times are simulated.
32 devices in a mesh: dp: 2 (over core), ctx: 8 (over z, x), mp: 2 (over y).
Axes of the slice: x: 2, y: 2, z: 4, core: 2. Of those that a mesh axis runs over, the one named last changes fastest.
Arguments:
- inputs: float32 [2, 1024, 896], P('dp', 'ctx'), may hold values from -6 to 6
- positions: int32 [2, 1024], P('dp'), may hold values from 0 to 1023, as said below
- attn_gain: bfloat16 [1, 896], P(None, ('dp', 'ctx')), may hold values from 0.5 to 1.5
- qkv_weight: bfloat16 [1, 896, 1152], P(None, ('dp', 'ctx'), 'mp'), may hold values from -0.1875 to 0.1875
- qkv_bias: bfloat16 [1, 2, 576], P(None, 'mp', ('dp', 'ctx')), may hold values from -5 to 5
- out_weight: bfloat16 [1, 896, 896], P(None, 'mp', ('dp', 'ctx')), may hold values from -0.75 to 0.75
- ffn_gain: bfloat16 [1, 896], P(None, ('dp', 'ctx')), may hold values from 0.5 to 1.5
- gate_up_weight: bfloat16 [1, 896, 2, 4864], P(None, ('dp', 'ctx'), None, 'mp'), may hold values from -0.1875 to 0.1875
- down_weight: bfloat16 [1, 4864, 896], P(None, 'mp', ('dp', 'ctx')), may hold values from -0.078125 to 0.078125
- cotangent: float32 [2, 1024, 896], P('dp', 'ctx'), may hold values from -6 to 6
Outputs:
- output: float32 [2, 1024, 896], P('dp', 'ctx')
- input_grad: float32 [2, 1024, 896], P('dp', 'ctx')
- attn_gain_grad: float32 [1, 896], P(None, ('dp', 'ctx'))
- qkv_weight_grad: float32 [1, 896, 1152], P(None, ('dp', 'ctx'), 'mp')
- qkv_bias_grad: float32 [1, 2, 576], P(None, 'mp', ('dp', 'ctx'))
- out_weight_grad: float32 [1, 896, 896], P(None, 'mp', ('dp', 'ctx'))
- ffn_gain_grad: float32 [1, 896], P(None, ('dp', 'ctx'))
- gate_up_grad: float32 [1, 896, 2, 4864], P(None, ('dp', 'ctx'), None, 'mp')
- down_grad: float32 [1, 4864, 896], P(None, 'mp', ('dp', 'ctx'))
Inputs may be any that keep to these rules, and one draw needn't show every extreme that they name: In each sequence every position 0 to 1023 occurs once; the tokens come in blocks of 64 consecutive positions starting at multiples of 64, and the two blocks of one index of ctx are blocks c and 15 - c of the sequence for some c that depends on the index, in either order.
All inputs are finite; a program needn't handle non-finite values.
Results may differ from a plain program's by a relative error of at most 0.02.
The roundings to bfloat16 on the way count: a program that leaves them out, or rounds other values in their place, can miss the bound.
Values may be sent and summed in bfloat16 or wider, within the bound.
No kernel may reach another device: no remote copies, remote signals or barrier semaphores. Data moves between devices by JAX's collectives and lax.ppermute only.
A program may use at most 128 MiB of HBM per device.

v0:
```python
import jax
import jax.numpy as jnp
from jax import lax
from jax.sharding import PartitionSpec as P


HEAD_DIM = 64
GROUP = 7
LANES = 128

epsilon = 1e-06
base_theta = 1000000.0


f32 = jnp.float32
bf16 = jnp.bfloat16


def rope_tables(block_locations, head_dim):
    half_dim = head_dim // 2
    inv_freq = base_theta ** (-(jnp.arange(half_dim, dtype=f32) * 2.0) / head_dim)
    angles = block_locations.astype(f32)[:, None] * inv_freq[None, :]
    angles = jnp.concatenate([angles, angles], axis=1)
    return (jnp.cos(angles), jnp.sin(angles))


def rotate(values, cosine_lookup, sine_lookup):
    half_dim = values.shape[-1] // 2
    view_shape = (values.shape[0],) + (1,) * (values.ndim - 2) + (values.shape[-1],)
    turned = jnp.concatenate([-values[..., half_dim:], values[..., :half_dim]], axis=-1)
    return values * cosine_lookup.reshape(view_shape) + turned * sine_lookup.reshape(view_shape)


def rms_forward(hidden, gain_vec):
    scale_rows = lax.rsqrt(jnp.mean(hidden * hidden, axis=-1, keepdims=True) + epsilon)
    normed = hidden * scale_rows
    return (normed, scale_rows, (normed * gain_vec.astype(f32)).astype(bf16))


def rms_backward(grad_out, normed, scale_rows, gain_vec):
    gain_grad = jnp.sum(grad_out * normed, axis=0)
    grad_normed = grad_out * gain_vec.astype(f32)
    grad_in = scale_rows * (
        grad_normed - normed * jnp.mean(grad_normed * normed, axis=-1, keepdims=True)
    )
    return (grad_in, gain_grad)


def after(value, *others):
    return lax.optimization_barrier((value,) + others)[0]


def dot_nt(a, b):
    return lax.dot_general(a, b, (((1,), (1,)), ((), ())), preferred_element_type=f32)


def dot_tn(a, b):
    return lax.dot_general(a, b, (((0,), (0,)), ((), ())), preferred_element_type=f32)


def dot_nn(a, b):
    return jnp.dot(a, b, preferred_element_type=f32)


def make_local(n_dp, n_ctx, n_mp):
    n_lo = 2
    n_hi = n_ctx // n_lo
    assert n_dp == 2 and n_mp == 2 and n_hi * n_lo == n_ctx
    pair = [(0, 1), (1, 0)]
    lo_pair = [(i, i ^ 1) for i in range(n_ctx)]

    def swap_dp(v):
        return lax.ppermute(v, "dp", pair)

    def swap_mp(v):
        return lax.ppermute(v, "mp", pair)

    def swap_lo(v):
        return lax.ppermute(v, "ctx", lo_pair)

    def swap_hi(v, mask):
        perm = [(h * n_lo + e, (h ^ mask) * n_lo + e) for h in range(n_hi) for e in range(n_lo)]
        return lax.ppermute(v, "ctx", perm)

    def exchange(v, axes):
        return lax.all_to_all(v, axes, 0, 0, tiled=True)

    def in_order(flag, own, other, axis=0):
        first = flag == 0
        return jnp.stack([jnp.where(first, own, other), jnp.where(first, other, own)], axis=axis)

    def flipped(flag, pairs):
        return jnp.where(flag == 0, pairs, pairs[:, ::-1])

    def pick(flag, two):
        first = flag == 0
        return jnp.where(first, two[0], two[1]), jnp.where(first, two[1], two[0])

    def by_mask(got, hi):
        got = jnp.stack(got)
        return jnp.stack(
            [
                lax.dynamic_index_in_dim(got, jnp.bitwise_xor(hi, j), 0, keepdims=False)
                for j in range(n_hi)
            ]
        )

    def relay_masks():
        masks, step = [], n_hi // 2
        while step:
            masks.append(step)
            step //= 2
        return masks

    def scatter_hi(parts, hi):
        total = lax.dynamic_index_in_dim(parts, hi, 0, keepdims=False).astype(f32)
        for k in range(1, n_hi):
            part = lax.dynamic_index_in_dim(parts, jnp.bitwise_xor(hi, k), 0, keepdims=False)
            total = total + swap_hi(part, k).astype(f32)
        return total

    def gather_rows(block, c, hi, lo, start=None):
        got = [block] + [swap_hi(block, k) for k in range(1, n_hi)]
        if start is not None:
            got = [after(g, start) for g in got]
        mine = by_mask(got, hi)
        both = in_order(lo, mine, swap_lo(mine), axis=1)
        return in_order(c, both, swap_dp(both))

    def scatter_rows(parts, c, hi, lo):
        keep, send = pick(c, parts)
        keep = keep + swap_dp(send.astype(bf16)).astype(f32)
        keep, send = pick(lo, (keep[:, 0], keep[:, 1]))
        keep = keep + swap_lo(send.astype(bf16)).astype(f32)
        return scatter_hi(keep.astype(bf16), hi)

    def gather_tokens(block):
        both = jnp.concatenate([block, swap_lo(block)], axis=0)
        return jnp.concatenate([both, swap_dp(both)], axis=0)

    def scatter_tokens(parts):
        half = parts.shape[0] // 2
        keep = parts[:half] + swap_dp(parts[half:].astype(bf16)).astype(f32)
        half = half // 2
        keep = keep[:half] + swap_lo(keep[half:].astype(bf16)).astype(f32)
        return sum_mp(keep)

    def sum_mp(part):
        part = part.astype(bf16)
        return part.astype(f32) + swap_mp(part).astype(f32)

    def local(
        inputs,
        positions,
        attn_gain,
        qkv_weight,
        qkv_bias,
        out_weight,
        ffn_gain,
        gate_up_weight,
        down_weight,
        cotangent,
    ):
        c = lax.axis_index("dp")
        ctx = lax.axis_index("ctx")
        hi, lo = ctx // n_lo, ctx % n_lo
        tokens = inputs.shape[1]
        model_width = inputs.shape[2]
        head_dim = HEAD_DIM
        group_size = GROUP
        score_scale = head_dim ** (-0.5)
        rows = qkv_weight.shape[1]
        units = down_weight.shape[1]
        splits = n_dp * n_lo
        piece = -(-units // (splits * LANES)) * LANES
        n_shards = n_dp * n_ctx

        seq_pos = positions[0]
        my_pos = lax.dynamic_slice_in_dim(seq_pos, ctx * tokens, tokens)
        hidden = inputs[0]

        w_q = qkv_weight[0]
        width_q = w_q.shape[1]
        gain_cols = -(-rows // LANES) * LANES
        bias_cols = qkv_bias.shape[2]
        extra = jnp.concatenate(
            [
                jnp.pad(attn_gain[0], (0, gain_cols - rows)),
                jnp.pad(ffn_gain[0], (0, gain_cols - rows)),
                jnp.pad(qkv_bias[0, 0], (0, width_q - 2 * gain_cols - bias_cols)),
            ]
        )[None]
        extra = jnp.pad(extra, ((0, 7), (0, 0)))
        block_q = jnp.concatenate([w_q, extra], axis=0)
        got_q = gather_rows(block_q, c, hi, lo).reshape(n_shards, rows + 8, width_q)
        w_qkv = got_q[:, :rows].reshape(model_width, width_q)
        side = got_q[:, rows]
        gain_attn = side[:, :rows].reshape(model_width)
        gain_ffn = side[:, gain_cols : gain_cols + rows].reshape(model_width)
        b_qkv = side[:, 2 * gain_cols : 2 * gain_cols + bias_cols].reshape(width_q)

        gate_up_weight, down_weight, cotangent, my_pos, hidden, all_pos = (
            lax.optimization_barrier(
                (gate_up_weight, down_weight, cotangent, my_pos, hidden, seq_pos, block_q)
            )[:6]
        )
        shards = [gate_up_weight[0, :, 0], gate_up_weight[0, :, 1], down_weight[0].T]
        shards = [jnp.pad(s, ((0, 0), (0, splits * piece - units))) for s in shards]
        groups = [
            jnp.concatenate([s[:, q * piece : (q + 1) * piece] for s in shards], axis=1)
            for q in range(splits)
        ]
        halves = [jnp.stack(groups[e * n_dp : (e + 1) * n_dp]) for e in range(n_lo)]
        keep, send = pick(lo, halves)
        cosine_lookup, sine_lookup = rope_tables(my_pos, head_dim)
        key_pos = flipped(lo, all_pos.reshape(n_hi, n_lo, tokens))
        step = n_hi // 2
        while step:
            key_pos = flipped(hi // step % 2, key_pos.reshape(-1, 2, step * n_lo * tokens))
            step //= 2
        key_pos = key_pos.reshape(n_hi, n_lo, tokens).swapaxes(0, 1).reshape(-1)
        row_pos = jnp.tile(my_pos, group_size)
        both = in_order(lo, keep, swap_lo(send))
        block_o = after(out_weight[0].T, block_q)
        grad_out = cotangent[0]
        grad_half = gather_tokens(after(grad_out.astype(bf16), both))
        keep, send = pick(c, (both[:, 0], both[:, 1]))
        plane = in_order(c, keep, swap_dp(send))

        normed_a, scale_a, attn_in = rms_forward(hidden, gain_attn)
        qkv_proj = dot_nn(attn_in, w_qkv) + b_qkv.astype(f32)
        qkv_proj = qkv_proj.reshape(tokens, group_size + 2, head_dim)
        query_heads = rotate(qkv_proj[:, :group_size], cosine_lookup, sine_lookup).astype(bf16)
        key_head = rotate(
            qkv_proj[:, group_size : group_size + 1], cosine_lookup, sine_lookup
        )[:, 0].astype(bf16)
        value_head = qkv_proj[:, group_size + 1].astype(bf16)
        query_rows = jnp.transpose(query_heads, (1, 0, 2)).reshape(group_size * tokens, head_dim)
        pair_kv = jnp.concatenate([key_head, value_head], axis=1)
        w_ot = gather_rows(block_o, c, hi, lo, pair_kv).reshape(model_width, -1)
        relayed = {0: after(plane, pair_kv)}
        for mask in relay_masks():
            for k in list(relayed):
                relayed[k ^ mask] = swap_hi(relayed[k], mask)
        w_ffn = by_mask([relayed[k] for k in range(n_hi)], hi)
        w_ffn = jnp.transpose(w_ffn, (1, 0, 2, 3, 4)).reshape(model_width, 3 * piece)
        w_gu, w_dt = w_ffn[:, : 2 * piece], w_ffn[:, 2 * piece :]
        pair_kv = jnp.concatenate([pair_kv] + [swap_hi(pair_kv, k) for k in range(1, n_hi)], axis=0)
        pair_kv = jnp.concatenate([pair_kv, swap_lo(pair_kv)], axis=0)
        key_all, value_all = pair_kv[:, :head_dim], pair_kv[:, head_dim:]
        allowed = key_pos[None, :] <= row_pos[:, None]
        scores = dot_nt(query_rows, key_all) * score_scale
        scores = jnp.where(allowed, scores, -1e30)
        row_max = jnp.max(scores, axis=1)
        weights_now = jnp.where(allowed, jnp.exp(scores - row_max[:, None]), 0.0)
        row_total = jnp.sum(weights_now, axis=1)
        row_accum = jnp.dot(
            weights_now,
            value_all.astype(f32),
            precision=lax.Precision.HIGHEST,
            preferred_element_type=f32,
        )
        log_total = row_max + jnp.log(row_total)
        attn_rows = (row_accum / row_total[:, None]).astype(bf16)
        attn_flat = jnp.transpose(
            attn_rows.reshape(group_size, tokens, head_dim), (1, 0, 2)
        ).reshape(tokens, group_size * head_dim)
        hidden_mid = hidden + sum_mp(dot_nt(attn_flat, w_ot))

        normed_f, scale_f, ffn_in = rms_forward(hidden_mid, gain_ffn)
        ffn_all = gather_tokens(ffn_in)
        gate_up_pre = dot_nn(ffn_all, w_gu)
        gate_pre, up_pre = gate_up_pre[:, :piece], gate_up_pre[:, piece:]
        grad_mixed = dot_nn(grad_half, w_dt)
        sigmoid_gate = jax.nn.sigmoid(gate_pre)
        silu_gate = gate_pre * sigmoid_gate
        mixed_units = (silu_gate * up_pre).astype(bf16)
        grad_up = grad_mixed * silu_gate
        grad_gate = grad_mixed * up_pre * (sigmoid_gate + silu_gate * (1.0 - sigmoid_gate))
        grad_pre = jnp.concatenate([grad_gate, grad_up], axis=1).astype(bf16)
        ffn_in_grad = scatter_tokens(dot_nt(grad_pre, w_gu))
        hidden_next = hidden_mid + scatter_tokens(dot_nt(mixed_units, w_dt))
        w_grad = jnp.concatenate(
            [dot_tn(ffn_all, grad_pre), dot_tn(grad_half, mixed_units)], axis=1
        ).astype(bf16)
        w_grad = w_grad.reshape(n_dp, n_hi, n_lo, rows, 3 * piece)
        w_grad = jnp.transpose(w_grad, (1, 0, 2, 3, 4))
        parts = [
            lax.dynamic_index_in_dim(w_grad, jnp.bitwise_xor(hi, k), 0, keepdims=False)
            for k in range(n_hi)
        ]
        sums = {k: [part] for k, part in enumerate(parts)}
        for mask in reversed(relay_masks()):
            for k in sorted(sums, reverse=True):
                if k & mask:
                    terms = sums.pop(k)
                    if len(terms) > 1:
                        terms = [sum(m.astype(f32) for m in terms).astype(bf16)]
                    sums[k ^ mask].append(swap_hi(terms[0], mask))

        back_ffn, gain_ffn_part = rms_backward(ffn_in_grad, normed_f, scale_f, gain_ffn)
        grad_mid = grad_out + back_ffn
        grad_mid_half = grad_mid.astype(bf16)
        grad_attn = dot_nn(grad_mid_half, w_ot).astype(bf16)
        out_part = dot_tn(grad_mid_half, attn_flat)
        grad_rows = jnp.transpose(
            grad_attn.reshape(tokens, group_size, head_dim), (1, 0, 2)
        ).reshape(group_size * tokens, head_dim)
        delta_rows = jnp.sum(grad_rows.astype(f32) * attn_rows.astype(f32), axis=1)
        probs = jnp.where(allowed, jnp.exp(scores - log_total[:, None]), 0.0)
        value_grad_all = dot_tn(probs.astype(bf16), grad_rows)
        grad_probs = dot_nt(grad_rows, value_all)
        grad_scores = (probs * (grad_probs - delta_rows[:, None])).astype(bf16)
        query_grad = dot_nn(grad_scores, key_all) * score_scale
        key_grad_all = dot_tn(grad_scores, query_rows) * score_scale
        kv_grad = jnp.concatenate([key_grad_all, value_grad_all], axis=1)
        kv_grad = kv_grad.reshape(n_lo, n_hi, tokens, 2 * head_dim)
        kv_grad = kv_grad[0] + swap_lo(kv_grad[1].astype(bf16)).astype(f32)
        kv_grad = kv_grad[0] + sum(
            swap_hi(kv_grad[k].astype(bf16), k).astype(f32) for k in range(1, n_hi)
        )
        key_grad, value_grad = kv_grad[:, :head_dim], kv_grad[:, head_dim:]
        query_grad = jnp.transpose(query_grad.reshape(group_size, tokens, head_dim), (1, 0, 2))
        query_grad = rotate(query_grad, cosine_lookup, -sine_lookup)
        key_grad = rotate(key_grad[:, None], cosine_lookup, -sine_lookup)
        grad_qkv = jnp.concatenate([query_grad, key_grad, value_grad[:, None]], axis=1).reshape(
            tokens, (group_size + 2) * head_dim
        )
        bias_part = jnp.sum(grad_qkv, axis=0)
        grad_qkv_half = grad_qkv.astype(bf16)
        attn_in_grad = sum_mp(dot_nt(grad_qkv_half, w_qkv))
        back_attn, gain_attn_part = rms_backward(attn_in_grad, normed_a, scale_a, gain_attn)
        input_grad = grad_mid + back_attn
        qkv_part = dot_tn(attn_in, grad_qkv_half)

        row_parts = jnp.concatenate([qkv_part, out_part], axis=1)
        row_sums = scatter_rows(row_parts.reshape(n_dp, n_hi, n_lo, rows, -1), c, hi, lo)
        qkv_sum, out_grad = row_sums[:, :width_q], row_sums[:, width_q:]
        side = jnp.stack(
            [
                jnp.pad(v.reshape(n_shards, -1), ((0, 0), (0, gain_cols - v.shape[0] // n_shards)))
                for v in (gain_attn_part, gain_ffn_part, bias_part)
            ],
            axis=1,
        )
        side = jnp.pad(side, ((0, 0), (0, 5), (0, 0)))
        side = jnp.sum(exchange(side, ("dp", "ctx")), axis=0)

        w_grad = sum(after(m, grad_qkv_half).astype(f32) for m in sums[0]).astype(bf16)
        keep, send = pick(c, w_grad)
        by_c = in_order(c, keep, swap_dp(send))
        keep, send = pick(lo, (by_c[:, 0], by_c[:, 1]))
        by_q = in_order(lo, keep, swap_lo(send)).reshape(splits, rows, 3 * piece).astype(f32)
        gate_grad, up_grad, down_grad = [
            jnp.concatenate(
                [by_q[q, :, e * piece : (e + 1) * piece] for q in range(splits)], axis=1
            )[:, :units]
            for e in range(3)
        ]
        return (
            hidden_next[None],
            input_grad[None],
            side[:1, :rows],
            qkv_sum[None],
            side[2:3, :bias_cols][None],
            out_grad.T[None],
            side[1:2, :rows],
            jnp.stack([gate_grad, up_grad], axis=1)[None],
            down_grad.T[None],
        )

    return local


def solution(mesh):
    both = ("dp", "ctx")
    body = make_local(mesh.shape["dp"], mesh.shape["ctx"], mesh.shape["mp"])

    return jax.shard_map(
        body,
        mesh=mesh,
        in_specs=(
            P("dp", "ctx", None),
            P("dp", None),
            P(None, both),
            P(None, both, "mp"),
            P(None, "mp", both),
            P(None, "mp", both),
            P(None, both),
            P(None, both, None, "mp"),
            P(None, "mp", both),
            P("dp", "ctx", None),
        ),
        out_specs=(
            P("dp", "ctx", None),
            P("dp", "ctx", None),
            P(None, both),
            P(None, both, "mp"),
            P(None, "mp", both),
            P(None, "mp", both),
            P(None, both),
            P(None, both, None, "mp"),
            P(None, "mp", both),
        ),
        check_vma=False,
    )
```

profile of v0, /device:TPU:0, one launch (start us, length us, event | category | flops | bytes accessed | tf_op | source)
XLA Modules:
  0.0 255.8 jit_solution(18083634429753642642)
XLA Ops:
  2.3 5.1 %collective-permute-start.2 = (bf16[64,576]{1,0:T(8,128)(2,1)S(1)}, bf16[64,576]{1,0:T(8,128)(2,1)S(1)}, u32[]{:S(2)}, u32[]{:S(2)}) collective-permute-start(bf16[64,576]{1,0:T(8,128)(2,1)S(1)} %get-tuple-element.178), channel_id=1, source_target_pairs={{0,12},{2,14},{4,8},{6,10},{8,4},{10,6},{12,0},{14,2},{1,13},{3,15... | collective-permute-start | bytes 221192 | tf_op jit(solution)/shard_map/ppermute | solution.py:83
  11.2 1.7 collective-permute-start.17
  12.9 3.6 %collective-permute-start.11 = (bf16[56,448]{1,0:T(8,128)(2,1)}, bf16[56,448]{1,0:T(8,128)(2,1)}, u32[]{:S(2)}, u32[]{:S(2)}) collective-permute-start(bf16[56,448]{1,0:T(8,128)(2,1)} %bitcast.30), channel_id=1, source_target_pairs={{0,12},{2,14},{4,8},{6,10},{8,4},{10,6},{12,0},{14,2},{1,13},{3,15... | collective-permute-start | bytes 150536 | tf_op jit(solution)/shard_map/ppermute | solution.py:83
  17.8 1.6 constant_dynamic-update-slice_fusion.7
  23.0 6.4 %collective-permute-done.3 = bf16[4,64,576]{2,1,0:T(8,128)(2,1)} collective-permute-done((bf16[4,64,576]{2,1,0:T(8,128)(2,1)}, bf16[4,64,576]{2,1,0:T(8,128)(2,1)}, u32[]{:S(2)}, u32[]{:S(2)}) %collective-permute-start.3) | collective-permute-done | bytes 294944 | tf_op jit(solution)/shard_map/ppermute | solution.py:79
  37.9 2.6 %collective-permute-start.6 = (bf16[128,128]{0,1:T(8,128)(2,1)S(1)}, bf16[128,128]{0,1:T(8,128)(2,1)S(1)}, u32[]{:S(2)}, u32[]{:S(2)}) collective-permute-start(bf16[128,128]{0,1:T(8,128)(2,1)S(1)} %get-tuple-element.183), channel_id=1, source_target_pairs={{0,8},{2,10},{4,12},{6,14},{8,0},{10,2},{12,4},{14,6},{1,9},{3,11}... | collective-permute-start | bytes 98312 | tf_op jit(solution)/shard_map/ppermute | solution.py:83
  44.0 2.7 %collective-permute-done.7 = bf16[128,128]{0,1:T(8,128)(2,1)S(1)} collective-permute-done((bf16[128,128]{0,1:T(8,128)(2,1)S(1)}, bf16[128,128]{0,1:T(8,128)(2,1)S(1)}, u32[]{:S(2)}, u32[]{:S(2)}) %collective-permute-start.7) | collective-permute-done | bytes 32800 | tf_op jit(solution)/shard_map/ppermute | solution.py:83
  47.3 5.6 %collective-permute-done.8 = bf16[512,128]{0,1:T(8,128)(2,1)S(1)} collective-permute-done((bf16[512,128]{0,1:T(8,128)(2,1)S(1)}, bf16[512,128]{0,1:T(8,128)(2,1)S(1)}, u32[]{:S(2)}, u32[]{:S(2)}) %collective-permute-start.8) | collective-permute-done | bytes 131104 | tf_op jit(solution)/shard_map/ppermute | solution.py:79
  56.1 2.7 %fusion.17 = bf16[896,64]{0,1:T(8,128)(2,1)S(1)} fusion(f32[896,1024]{1,0:T(8,128)S(1)} %get-tuple-element.195, f32[896]{0:T(1024)S(1)} %get-tuple-element.194, s32[1024]{0:T(1024)S(1)} %bitcast.370, s32[896]{0:T(1024)S(1)} %broadcast_bitcast_fusion, bf16[1024,128]{0,1:T(8,128)(2,1)S(1)} %constant_dynamic-update-slice_fusion, f32[896]{0:T(1024)S(1)} %fusion), kind=kOutput, calls=%fused_computation.58 | convolution fusion | flops 707510272 | bytes 3932160 | tf_op jit(solution)/shard_map/dot_general | solution.py:257
  60.1 1.6 collective-permute-start.14
  61.7 1.9 pad_maximum_fusion.24
  63.5 1.6 constant_dynamic-update-slice_fusion.6
  65.2 14.7 %collective-permute-start.19 = (bf16[2,2,56,1920]{3,2,1,0:T(8,128)(2,1)}, bf16[2,2,56,1920]{3,2,1,0:T(8,128)(2,1)}, u32[]{:S(2)}, u32[]{:S(2)}) collective-permute-start(bf16[2,2,56,1920]{3,2,1,0:T(8,128)(2,1)} %pad_maximum_fusion.8), channel_id=1, source_target_pairs={{0,4},{2,6},{4,0},{6,2},{8,12},{10,14},{12,8},{14,10},{1,5},{3,7},... | collective-permute-start | bytes 2580488 | tf_op jit(solution)/shard_map/ppermute | solution.py:83
  83.9 1.8 constant_dynamic-update-slice_fusion.5
  86.4 3.5 %collective-permute-done.15 = bf16[128,896]{1,0:T(8,128)(2,1)S(1)} collective-permute-done((bf16[128,896]{1,0:T(8,128)(2,1)S(1)}, bf16[128,896]{1,0:T(8,128)(2,1)S(1)}, u32[]{:S(2)}, u32[]{:S(2)}) %collective-permute-start.15) | collective-permute-done | bytes 229408 | tf_op jit(solution)/shard_map/ppermute | solution.py:79
  90.0 10.3 %collective-permute-done.19 = bf16[2,2,56,1920]{3,2,1,0:T(8,128)(2,1)} collective-permute-done((bf16[2,2,56,1920]{3,2,1,0:T(8,128)(2,1)}, bf16[2,2,56,1920]{3,2,1,0:T(8,128)(2,1)}, u32[]{:S(2)}, u32[]{:S(2)}) %collective-permute-start.19) | collective-permute-done | bytes 860192 | tf_op jit(solution)/shard_map/ppermute | solution.py:83
  100.3 18.3 %collective-permute-done.21 = bf16[2,2,56,1920]{3,2,1,0:T(8,128)(2,1)S(1)} collective-permute-done((bf16[2,2,56,1920]{3,2,1,0:T(8,128)(2,1)}, bf16[2,2,56,1920]{3,2,1,0:T(8,128)(2,1)S(1)}, u32[]{:S(2)}, u32[]{:S(2)}) %collective-permute-start.21) | collective-permute-done | bytes 860192 | tf_op jit(solution)/shard_map/ppermute | solution.py:83
  118.6 1.9 pad_maximum_fusion
  121.5 1.5 fusion.5
  123.1 2.4 multiply_convert_fusion.2
  126.4 2.1 convolution_convert_fusion.1
  128.5 1.6 fusion.3
  136.7 1.6 collective-permute-start.23
  138.2 6.2 %collective-permute-done.28 = bf16[128,896]{1,0:T(8,128)(2,1)S(1)} collective-permute-done((bf16[128,896]{1,0:T(8,128)(2,1)S(1)}, bf16[128,896]{1,0:T(8,128)(2,1)S(1)}, u32[]{:S(2)}, u32[]{:S(2)}) %collective-permute-start.28) | collective-permute-done | bytes 229408 | tf_op jit(solution)/shard_map/ppermute | solution.py:79
  144.5 1.6 collective-permute-start.29
  146.1 1.9 collective-permute-done.23
  148.0 1.6 collective-permute-start.24
  149.6 6.1 %collective-permute-done.41 = bf16[2,2,56,1920]{3,2,1,0:T(8,128)(2,1)S(1)} collective-permute-done((bf16[2,2,56,1920]{3,2,1,0:T(8,128)(2,1)S(1)}, bf16[2,2,56,1920]{3,2,1,0:T(8,128)(2,1)S(1)}, u32[]{:S(2)}, u32[]{:S(2)}) %collective-permute-start.41) | collective-permute-done | bytes 860192 | tf_op jit(solution)/shard_map/ppermute | solution.py:83
  157.0 3.5 %collective-permute-start.42 = (bf16[2,2,56,1920]{3,2,1,0:T(8,128)(2,1)}, bf16[2,2,56,1920]{3,2,1,0:T(8,128)(2,1)}, u32[]{:S(2)}, u32[]{:S(2)}) collective-permute-start(bf16[2,2,56,1920]{3,2,1,0:T(8,128)(2,1)} %fusion.14), channel_id=1, source_target_pairs={{0,8},{2,10},{4,12},{6,14},{8,0},{10,2},{12,4},{14,6},{1,9},{3,11}... | collective-permute-start | bytes 2580488 | tf_op jit(solution)/shard_map/ppermute | solution.py:83
  169.5 1.8 copy.188
  171.3 1.8 copy.191
  173.1 1.7 copy.189
  174.8 1.7 copy.190
  177.0 1.6 copy.242
  179.8 2.0 collective-permute-done.30
  184.6 2.7 %collective-permute-start.31 = (bf16[128,128]{0,1:T(8,128)(2,1)S(1)}, bf16[128,128]{0,1:T(8,128)(2,1)S(1)}, u32[]{:S(2)}, u32[]{:S(2)}) collective-permute-start(bf16[128,128]{0,1:T(8,128)(2,1)S(1)} %get-tuple-element.174), channel_id=1, source_target_pairs={{0,4},{2,6},{4,0},{6,2},{8,12},{10,14},{12,8},{14,10},{1,5},{3,7},... | collective-permute-start | bytes 98312 | tf_op jit(solution)/shard_map/ppermute | solution.py:83
  187.3 8.8 %collective-permute-done.33 = bf16[128,128]{0,1:T(8,128)(2,1)S(1)} collective-permute-done((bf16[128,128]{0,1:T(8,128)(2,1)S(1)}, bf16[128,128]{0,1:T(8,128)(2,1)S(1)}, u32[]{:S(2)}, u32[]{:S(2)}) %collective-permute-start.33) | collective-permute-done | bytes 32800 | tf_op jit(solution)/shard_map/ppermute | solution.py:83
  196.1 3.4 %collective-permute-done.32 = bf16[128,128]{0,1:T(8,128)(2,1)S(1)} collective-permute-done((bf16[128,128]{0,1:T(8,128)(2,1)S(1)}, bf16[128,128]{0,1:T(8,128)(2,1)S(1)}, u32[]{:S(2)}, u32[]{:S(2)}) %collective-permute-start.32) | collective-permute-done | bytes 32800 | tf_op jit(solution)/shard_map/ppermute | solution.py:83
  204.9 1.8 broadcast_select_fusion
  209.1 3.7 %all-to-all-start = ((f32[16,8,128]{2,1,0:T(8,128)}), f32[16,8,128]{2,1,0:T(8,128)S(1)}, u32[]{:S(2)}, u32[]{:S(2)}) async-start(f32[16,8,128]{2,1,0:T(8,128)} %pad.50.clone), calls=%async_computation | async-start | bytes 131072 | tf_op jit(solution)/shard_map/all_to_all | solution.py:86
  212.8 1.9 add_bitcast_fusion
  214.7 4.9 %all-to-all-done = f32[16,8,128]{2,1,0:T(8,128)S(1)} async-done(((f32[16,8,128]{2,1,0:T(8,128)}), f32[16,8,128]{2,1,0:T(8,128)S(1)}, u32[]{:S(2)}, u32[]{:S(2)}) %all-to-all-start) | async-done | bytes 65568 | tf_op jit(solution)/shard_map/all_to_all | solution.py:86
  220.6 1.9 add_convert_fusion
  225.0 12.1 %collective-permute-done.36 = bf16[4,56,1024]{2,1,0:T(8,128)(2,1)S(1)} collective-permute-done((bf16[4,56,1024]{2,1,0:T(8,128)(2,1)S(1)}, bf16[4,56,1024]{2,1,0:T(8,128)(2,1)S(1)}, u32[]{:S(2)}, u32[]{:S(2)}) %collective-permute-start.36) | collective-permute-done | bytes 458784 | tf_op jit(solution)/shard_map/ppermute | solution.py:79
  239.6 2.3 collective-permute-start.37
  242.6 2.7 %collective-permute-done.39 = bf16[56,1024]{1,0:T(8,128)(2,1)S(1)} collective-permute-done((bf16[56,1024]{1,0:T(8,128)(2,1)S(1)}, bf16[56,1024]{1,0:T(8,128)(2,1)S(1)}, u32[]{:S(2)}, u32[]{:S(2)}) %collective-permute-start.39) | collective-permute-done | bytes 114720 | tf_op jit(solution)/shard_map/ppermute | solution.py:83
  245.4 4.4 %collective-permute-done.38 = bf16[56,1024]{1,0:T(8,128)(2,1)S(1)} collective-permute-done((bf16[56,1024]{1,0:T(8,128)(2,1)S(1)}, bf16[56,1024]{1,0:T(8,128)(2,1)S(1)}, u32[]{:S(2)}, u32[]{:S(2)}) %collective-permute-start.38) | collective-permute-done | bytes 114720 | tf_op jit(solution)/shard_map/ppermute | solution.py:83
  253.4 1.5 copy.204
  (284 shorter events, 73.6 us)
Async XLA Ops:
  2.3 17.2 %collective-permute-start.2 = (bf16[64,576]{1,0:T(8,128)(2,1)S(1)}, bf16[64,576]{1,0:T(8,128)(2,1)S(1)}, u32[]{:S(2)}, u32[]{:S(2)}) collective-permute-start(bf16[64,576]{1,0:T(8,128)(2,1)S(1)} %get-tuple-element.178), channel_id=1, source_target_pairs={{0,12},{2,14},{4,8},{6,10},{8,4},{10,6},{12,0},{14,2},{1,13},{3,15... | collective-permute-start | bytes 221192 | tf_op jit(solution)/shard_map/ppermute | solution.py:83
  7.4 12.1 %collective-permute-start.1 = (bf16[64,576]{1,0:T(8,128)(2,1)S(1)}, bf16[64,576]{1,0:T(8,128)(2,1)S(1)}, u32[]{:S(2)}, u32[]{:S(2)}) collective-permute-start(bf16[64,576]{1,0:T(8,128)(2,1)S(1)} %get-tuple-element.178), channel_id=1, source_target_pairs={{0,8},{2,10},{4,12},{6,14},{8,0},{10,2},{12,4},{14,6},{1,9},{3,11}... | collective-permute-start | bytes 221192 | tf_op jit(solution)/shard_map/ppermute | solution.py:83
  7.4 12.9 %collective-permute-start = (bf16[64,576]{1,0:T(8,128)(2,1)S(1)}, bf16[64,576]{1,0:T(8,128)(2,1)S(1)}, u32[]{:S(2)}, u32[]{:S(2)}) collective-permute-start(bf16[64,576]{1,0:T(8,128)(2,1)S(1)} %get-tuple-element.178), channel_id=1, source_target_pairs={{0,4},{2,6},{4,0},{6,2},{8,12},{10,14},{12,8},{14,10},{1,5},{3,7},... | collective-permute-start | bytes 221192 | tf_op jit(solution)/shard_map/ppermute | solution.py:83
  11.2 11.4 %collective-permute-start.17 = (bf16[2,56,1920]{2,1,0:T(8,128)(2,1)S(1)}, bf16[2,56,1920]{2,1,0:T(8,128)(2,1)S(1)}, u32[]{:S(2)}, u32[]{:S(2)}) collective-permute-start(bf16[2,56,1920]{2,1,0:T(8,128)(2,1)S(1)} %broadcast_select_fusion.3), channel_id=1, source_target_pairs={{0,2},{2,0},{4,6},{6,4},{8,10},{10,8},{12,14},{14,12},{1,3},{3,1},... | collective-permute-start | bytes 1290248 | tf_op jit(solution)/shard_map/ppermute | solution.py:79
  12.9 25.0 %collective-permute-start.11 = (bf16[56,448]{1,0:T(8,128)(2,1)}, bf16[56,448]{1,0:T(8,128)(2,1)}, u32[]{:S(2)}, u32[]{:S(2)}) collective-permute-start(bf16[56,448]{1,0:T(8,128)(2,1)} %bitcast.30), channel_id=1, source_target_pairs={{0,12},{2,14},{4,8},{6,10},{8,4},{10,6},{12,0},{14,2},{1,13},{3,15... | collective-permute-start | bytes 150536 | tf_op jit(solution)/shard_map/ppermute | solution.py:83
  16.5 38.4 %copy-start.28 = (s32[896]{0:T(1024)}, s32[896]{0:T(1024)S(1)}, u32[]{:S(2)}) copy-start(s32[896]{0:T(1024)S(1)} %broadcast_bitcast_fusion) | copy-start | bytes 10756
  19.5 21.0 %collective-permute-start.10 = (bf16[56,448]{1,0:T(8,128)(2,1)}, bf16[56,448]{1,0:T(8,128)(2,1)}, u32[]{:S(2)}, u32[]{:S(2)}) collective-permute-start(bf16[56,448]{1,0:T(8,128)(2,1)} %bitcast.30), channel_id=1, source_target_pairs={{0,8},{2,10},{4,12},{6,14},{8,0},{10,2},{12,4},{14,6},{1,9},{3,11}... | collective-permute-start | bytes 150536 | tf_op jit(solution)/shard_map/ppermute | solution.py:83
  19.5 21.4 %collective-permute-start.9 = (bf16[56,448]{1,0:T(8,128)(2,1)}, bf16[56,448]{1,0:T(8,128)(2,1)}, u32[]{:S(2)}, u32[]{:S(2)}) collective-permute-start(bf16[56,448]{1,0:T(8,128)(2,1)} %bitcast.30), channel_id=1, source_target_pairs={{0,4},{2,6},{4,0},{6,2},{8,12},{10,14},{12,8},{14,10},{1,5},{3,7},... | collective-permute-start | bytes 150536 | tf_op jit(solution)/shard_map/ppermute | solution.py:83
  21.2 8.2 %collective-permute-start.3 = (bf16[4,64,576]{2,1,0:T(8,128)(2,1)}, bf16[4,64,576]{2,1,0:T(8,128)(2,1)}, u32[]{:S(2)}, u32[]{:S(2)}) collective-permute-start(bf16[4,64,576]{2,1,0:T(8,128)(2,1)} %pad_maximum_fusion.31), channel_id=1, source_target_pairs={{0,2},{2,0},{4,6},{6,4},{8,10},{10,8},{12,14},{14,12},{1,3},{3,1},... | collective-permute-start | bytes 884744 | tf_op jit(solution)/shard_map/ppermute | solution.py:79
  22.8 9.3 %collective-permute-start.18 = (bf16[2,56,1920]{2,1,0:T(8,128)(2,1)S(1)}, bf16[2,56,1920]{2,1,0:T(8,128)(2,1)S(1)}, u32[]{:S(2)}, u32[]{:S(2)}) collective-permute-start(bf16[2,56,1920]{2,1,0:T(8,128)(2,1)S(1)} %select_bitcast_fusion.6), channel_id=1, source_target_pairs={{0,16},{16,0},{1,17},{17,1},{2,18},{18,2},{3,19},{19,3},{4,20},{20... | collective-permute-start | bytes 1290248 | tf_op jit(solution)/shard_map/ppermute | solution.py:73
  23.0 31.8 %copy-start.30 = (s32[2,4,128]{2,1,0:T(4,128)}, s32[2,4,128]{2,1,0:T(4,128)S(1)}, u32[]{:S(2)}) copy-start(s32[2,4,128]{2,1,0:T(4,128)S(1)} %copy.175) | copy-start | bytes 12292
  29.4 32.2 %collective-permute-start.25 = (bf16[128,896]{1,0:T(8,128)(2,1)}, bf16[128,896]{1,0:T(8,128)(2,1)}, u32[]{:S(2)}, u32[]{:S(2)}) collective-permute-start(bf16[128,896]{1,0:T(8,128)(2,1)} %bitcast_convert_fusion.1), channel_id=1, source_target_pairs={{0,2},{2,0},{4,6},{6,4},{8,10},{10,8},{12,14},{14,12},{1,3},{3,1},... | collective-permute-start | bytes 688136 | tf_op jit(solution)/shard_map/ppermute | solution.py:79
  32.1 2.2 collective-permute-start.4
  36.4 7.0 %collective-permute-start.5 = (bf16[128,128]{0,1:T(8,128)(2,1)S(1)}, bf16[128,128]{0,1:T(8,128)(2,1)S(1)}, u32[]{:S(2)}, u32[]{:S(2)}) collective-permute-start(bf16[128,128]{0,1:T(8,128)(2,1)S(1)} %get-tuple-element.183), channel_id=1, source_target_pairs={{0,4},{2,6},{4,0},{6,2},{8,12},{10,14},{12,8},{14,10},{1,5},{3,7},... | collective-permute-start | bytes 98312 | tf_op jit(solution)/shard_map/ppermute | solution.py:83
  37.9 6.1 %collective-permute-start.6 = (bf16[128,128]{0,1:T(8,128)(2,1)S(1)}, bf16[128,128]{0,1:T(8,128)(2,1)S(1)}, u32[]{:S(2)}, u32[]{:S(2)}) collective-permute-start(bf16[128,128]{0,1:T(8,128)(2,1)S(1)} %get-tuple-element.183), channel_id=1, source_target_pairs={{0,8},{2,10},{4,12},{6,14},{8,0},{10,2},{12,4},{14,6},{1,9},{3,11}... | collective-permute-start | bytes 98312 | tf_op jit(solution)/shard_map/ppermute | solution.py:83
  40.5 6.1 %collective-permute-start.7 = (bf16[128,128]{0,1:T(8,128)(2,1)S(1)}, bf16[128,128]{0,1:T(8,128)(2,1)S(1)}, u32[]{:S(2)}, u32[]{:S(2)}) collective-permute-start(bf16[128,128]{0,1:T(8,128)(2,1)S(1)} %get-tuple-element.183), channel_id=1, source_target_pairs={{0,12},{2,14},{4,8},{6,10},{8,4},{10,6},{12,0},{14,2},{1,13},{3,15... | collective-permute-start | bytes 98312 | tf_op jit(solution)/shard_map/ppermute | solution.py:83
  40.9 41.0 %collective-permute-start.20 = (bf16[2,2,56,1920]{3,2,1,0:T(8,128)(2,1)}, bf16[2,2,56,1920]{3,2,1,0:T(8,128)(2,1)}, u32[]{:S(2)}, u32[]{:S(2)}) collective-permute-start(bf16[2,2,56,1920]{3,2,1,0:T(8,128)(2,1)} %pad_maximum_fusion.8), channel_id=1, source_target_pairs={{0,8},{2,10},{4,12},{6,14},{8,0},{10,2},{12,4},{14,6},{1,9},{3,11}... | collective-permute-start | bytes 2580488 | tf_op jit(solution)/shard_map/ppermute | solution.py:83
  43.4 10.3 %collective-permute-start.12 = (bf16[4,56,448]{2,1,0:T(8,128)(2,1)S(1)}, bf16[4,56,448]{2,1,0:T(8,128)(2,1)S(1)}, u32[]{:S(2)}, u32[]{:S(2)}) collective-permute-start(bf16[4,56,448]{2,1,0:T(8,128)(2,1)S(1)} %pad_maximum_fusion.35), channel_id=1, source_target_pairs={{0,2},{2,0},{4,6},{6,4},{8,10},{10,8},{12,14},{14,12},{1,3},{3,1},... | collective-permute-start | bytes 602120 | tf_op jit(solution)/shard_map/ppermute | solution.py:79
  46.6 6.2 %collective-permute-start.8 = (bf16[512,128]{0,1:T(8,128)(2,1)S(1)}, bf16[512,128]{0,1:T(8,128)(2,1)S(1)}, u32[]{:S(2)}, u32[]{:S(2)}) collective-permute-start(bf16[512,128]{0,1:T(8,128)(2,1)S(1)} %pad_maximum_fusion.36), channel_id=1, source_target_pairs={{0,2},{2,0},{4,6},{6,4},{8,10},{10,8},{12,14},{14,12},{1,3},{3,1},... | collective-permute-start | bytes 393224 | tf_op jit(solution)/shard_map/ppermute | solution.py:79
  53.8 5.2 %collective-permute-start.13 = (bf16[4,2,56,448]{3,2,0,1:T(8,128)(2,1)S(1)}, bf16[4,2,56,448]{3,2,0,1:T(8,128)(2,1)S(1)}, u32[]{:S(2)}, u32[]{:S(2)}) collective-permute-start(bf16[4,2,56,448]{3,2,0,1:T(8,128)(2,1)S(1)} %pad_maximum_fusion.22), channel_id=1, source_target_pairs={{0,16},{16,0},{1,17},{17,1},{2,18},{18,2},{3,19},{19,3},{4,20},{20... | collective-permute-start | bytes 1204232 | tf_op jit(solution)/shard_map/ppermute | solution.py:73
  60.1 20.5 %collective-permute-start.14 = (bf16[128,896]{1,0:T(8,128)(2,1)S(1)}, bf16[128,896]{1,0:T(8,128)(2,1)S(1)}, u32[]{:S(2)}, u32[]{:S(2)}) collective-permute-start(bf16[128,896]{1,0:T(8,128)(2,1)S(1)} %convolution_convert_fusion.3), channel_id=1, source_target_pairs={{0,1},{1,0},{2,3},{3,2},{4,5},{5,4},{6,7},{7,6},{8,9},{9,8},{10,11... | collective-permute-start | bytes 688136 | tf_op jit(solution)/shard_map/ppermute | solution.py:76
  63.5 20.4 %collective-permute-start.26 = (bf16[256,896]{1,0:T(8,128)(2,1)}, bf16[256,896]{1,0:T(8,128)(2,1)}, u32[]{:S(2)}, u32[]{:S(2)}) collective-permute-start(bf16[256,896]{1,0:T(8,128)(2,1)} %pad_maximum_fusion.24), channel_id=1, source_target_pairs={{0,16},{16,0},{1,17},{17,1},{2,18},{18,2},{3,19},{19,3},{4,20},{20... | collective-permute-start | bytes 1376264 | tf_op jit(solution)/shard_map/ppermute | solution.py:73
  65.2 35.1 %collective-permute-start.19 = (bf16[2,2,56,1920]{3,2,1,0:T(8,128)(2,1)}, bf16[2,2,56,1920]{3,2,1,0:T(8,128)(2,1)}, u32[]{:S(2)}, u32[]{:S(2)}) collective-permute-start(bf16[2,2,56,1920]{3,2,1,0:T(8,128)(2,1)} %pad_maximum_fusion.8), channel_id=1, source_target_pairs={{0,4},{2,6},{4,0},{6,2},{8,12},{10,14},{12,8},{14,10},{1,5},{3,7},... | collective-permute-start | bytes 2580488 | tf_op jit(solution)/shard_map/ppermute | solution.py:83
  81.8 36.7 %collective-permute-start.21 = (bf16[2,2,56,1920]{3,2,1,0:T(8,128)(2,1)}, bf16[2,2,56,1920]{3,2,1,0:T(8,128)(2,1)S(1)}, u32[]{:S(2)}, u32[]{:S(2)}) collective-permute-start(bf16[2,2,56,1920]{3,2,1,0:T(8,128)(2,1)} %collective-permute-done.20), channel_id=1, source_target_pairs={{0,4},{2,6},{4,0},{6,2},{8,12},{10,14},{12,8},{14,10},{1,5},{3,7},... | collective-permute-start | bytes 2580488 | tf_op jit(solution)/shard_map/ppermute | solution.py:83
  83.3 6.6 %collective-permute-start.15 = (bf16[128,896]{1,0:T(8,128)(2,1)S(1)}, bf16[128,896]{1,0:T(8,128)(2,1)S(1)}, u32[]{:S(2)}, u32[]{:S(2)}) collective-permute-start(bf16[128,896]{1,0:T(8,128)(2,1)S(1)} %multiply_convert_fusion.4), channel_id=1, source_target_pairs={{0,2},{2,0},{4,6},{6,4},{8,10},{10,8},{12,14},{14,12},{1,3},{3,1},... | collective-permute-start | bytes 688136 | tf_op jit(solution)/shard_map/ppermute | solution.py:79
  89.9 31.6 %collective-permute-start.16 = (bf16[256,896]{1,0:T(8,128)(2,1)S(1)}, bf16[256,896]{1,0:T(8,128)(2,1)S(1)}, u32[]{:S(2)}, u32[]{:S(2)}) collective-permute-start(bf16[256,896]{1,0:T(8,128)(2,1)S(1)} %pad_maximum_fusion.23), channel_id=1, source_target_pairs={{0,16},{16,0},{1,17},{17,1},{2,18},{18,2},{3,19},{19,3},{4,20},{20... | collective-permute-start | bytes 1376264 | tf_op jit(solution)/shard_map/ppermute | solution.py:73
  130.2 5.6 %collective-permute-start.27 = (bf16[256,896]{1,0:T(8,128)(2,1)S(1)}, bf16[256,896]{1,0:T(8,128)(2,1)S(1)}, u32[]{:S(2)}, u32[]{:S(2)}) collective-permute-start(bf16[256,896]{1,0:T(8,128)(2,1)S(1)} %slice.627), channel_id=1, source_target_pairs={{0,16},{16,0},{1,17},{17,1},{2,18},{18,2},{3,19},{19,3},{4,20},{20... | collective-permute-start | bytes 1376264 | tf_op jit(solution)/shard_map/ppermute | solution.py:73
  130.4 6.1 %collective-permute-start.22 = (bf16[256,896]{1,0:T(8,128)(2,1)S(1)}, bf16[256,896]{1,0:T(8,128)(2,1)S(1)}, u32[]{:S(2)}, u32[]{:S(2)}) collective-permute-start(bf16[256,896]{1,0:T(8,128)(2,1)S(1)} %slice.628), channel_id=1, source_target_pairs={{0,16},{16,0},{1,17},{17,1},{2,18},{18,2},{3,19},{19,3},{4,20},{20... | collective-permute-start | bytes 1376264 | tf_op jit(solution)/shard_map/ppermute | solution.py:73
  133.7 22.0 %collective-permute-start.41 = (bf16[2,2,56,1920]{3,2,1,0:T(8,128)(2,1)S(1)}, bf16[2,2,56,1920]{3,2,1,0:T(8,128)(2,1)S(1)}, u32[]{:S(2)}, u32[]{:S(2)}) collective-permute-start(bf16[2,2,56,1920]{3,2,1,0:T(8,128)(2,1)S(1)} %get-tuple-element.107), channel_id=1, source_target_pairs={{0,4},{2,6},{4,0},{6,2},{8,12},{10,14},{12,8},{14,10},{1,5},{3,7},... | collective-permute-start | bytes 2580488 | tf_op jit(solution)/shard_map/ppermute | solution.py:83
  135.2 69.6 %collective-permute-start.40 = (bf16[2,2,56,1920]{3,2,1,0:T(8,128)(2,1)}, bf16[2,2,56,1920]{3,2,1,0:T(8,128)(2,1)}, u32[]{:S(2)}, u32[]{:S(2)}) collective-permute-start(bf16[2,2,56,1920]{3,2,1,0:T(8,128)(2,1)} %get-tuple-element.106), channel_id=1, source_target_pairs={{0,4},{2,6},{4,0},{6,2},{8,12},{10,14},{12,8},{14,10},{1,5},{3,7},... | collective-permute-start | bytes 2580488 | tf_op jit(solution)/shard_map/ppermute | solution.py:83
  135.9 8.5 %collective-permute-start.28 = (bf16[128,896]{1,0:T(8,128)(2,1)S(1)}, bf16[128,896]{1,0:T(8,128)(2,1)S(1)}, u32[]{:S(2)}, u32[]{:S(2)}) collective-permute-start(bf16[128,896]{1,0:T(8,128)(2,1)S(1)} %slice.629), channel_id=1, source_target_pairs={{0,2},{2,0},{4,6},{6,4},{8,10},{10,8},{12,14},{14,12},{1,3},{3,1},... | collective-permute-start | bytes 688136 | tf_op jit(solution)/shard_map/ppermute | solution.py:79
  136.7 11.3 %collective-permute-start.23 = (bf16[128,896]{1,0:T(8,128)(2,1)S(1)}, bf16[128,896]{1,0:T(8,128)(2,1)S(1)}, u32[]{:S(2)}, u32[]{:S(2)}) collective-permute-start(bf16[128,896]{1,0:T(8,128)(2,1)S(1)} %slice.630), channel_id=1, source_target_pairs={{0,2},{2,0},{4,6},{6,4},{8,10},{10,8},{12,14},{14,12},{1,3},{3,1},... | collective-permute-start | bytes 688136 | tf_op jit(solution)/shard_map/ppermute | solution.py:79
  144.5 16.0 %collective-permute-start.29 = (bf16[128,896]{1,0:T(8,128)(2,1)S(1)}, bf16[128,896]{1,0:T(8,128)(2,1)S(1)}, u32[]{:S(2)}, u32[]{:S(2)}) collective-permute-start(bf16[128,896]{1,0:T(8,128)(2,1)S(1)} %fusion.37), channel_id=1, source_target_pairs={{0,1},{1,0},{2,3},{3,2},{4,5},{5,4},{6,7},{7,6},{8,9},{9,8},{10,11... | collective-permute-start | bytes 688136 | tf_op jit(solution)/shard_map/ppermute | solution.py:76
  148.0 13.2 %collective-permute-start.24 = (bf16[128,896]{1,0:T(8,128)(2,1)S(1)}, bf16[128,896]{1,0:T(8,128)(2,1)S(1)}, u32[]{:S(2)}, u32[]{:S(2)}) collective-permute-start(bf16[128,896]{1,0:T(8,128)(2,1)S(1)} %fusion.38), channel_id=1, source_target_pairs={{0,1},{1,0},{2,3},{3,2},{4,5},{5,4},{6,7},{7,6},{8,9},{9,8},{10,11... | collective-permute-start | bytes 688136 | tf_op jit(solution)/shard_map/ppermute | solution.py:76
  157.0 63.7 %collective-permute-start.42 = (bf16[2,2,56,1920]{3,2,1,0:T(8,128)(2,1)}, bf16[2,2,56,1920]{3,2,1,0:T(8,128)(2,1)}, u32[]{:S(2)}, u32[]{:S(2)}) collective-permute-start(bf16[2,2,56,1920]{3,2,1,0:T(8,128)(2,1)} %fusion.14), channel_id=1, source_target_pairs={{0,8},{2,10},{4,12},{6,14},{8,0},{10,2},{12,4},{14,6},{1,9},{3,11}... | collective-permute-start | bytes 2580488 | tf_op jit(solution)/shard_map/ppermute | solution.py:83
  176.5 5.3 %collective-permute-start.30 = (bf16[4,128,128]{1,2,0:T(8,128)(2,1)}, bf16[4,128,128]{1,2,0:T(8,128)(2,1)}, u32[]{:S(2)}, u32[]{:S(2)}) collective-permute-start(bf16[4,128,128]{1,2,0:T(8,128)(2,1)} %copy.190), channel_id=1, source_target_pairs={{0,2},{2,0},{4,6},{6,4},{8,10},{10,8},{12,14},{14,12},{1,3},{3,1},... | collective-permute-start | bytes 393224 | tf_op jit(solution)/shard_map/ppermute | solution.py:79
  182.8 13.3 %collective-permute-start.33 = (bf16[128,128]{0,1:T(8,128)(2,1)S(1)}, bf16[128,128]{0,1:T(8,128)(2,1)S(1)}, u32[]{:S(2)}, u32[]{:S(2)}) collective-permute-start(bf16[128,128]{0,1:T(8,128)(2,1)S(1)} %get-tuple-element.175), channel_id=1, source_target_pairs={{0,12},{2,14},{4,8},{6,10},{8,4},{10,6},{12,0},{14,2},{1,13},{3,15... | collective-permute-start | bytes 98312 | tf_op jit(solution)/shard_map/ppermute | solution.py:83
  183.2 16.3 %collective-permute-start.32 = (bf16[128,128]{0,1:T(8,128)(2,1)S(1)}, bf16[128,128]{0,1:T(8,128)(2,1)S(1)}, u32[]{:S(2)}, u32[]{:S(2)}) collective-permute-start(bf16[128,128]{0,1:T(8,128)(2,1)S(1)} %get-tuple-element.176), channel_id=1, source_target_pairs={{0,8},{2,10},{4,12},{6,14},{8,0},{10,2},{12,4},{14,6},{1,9},{3,11}... | collective-permute-start | bytes 98312 | tf_op jit(solution)/shard_map/ppermute | solution.py:83
  184.6 14.9 %collective-permute-start.31 = (bf16[128,128]{0,1:T(8,128)(2,1)S(1)}, bf16[128,128]{0,1:T(8,128)(2,1)S(1)}, u32[]{:S(2)}, u32[]{:S(2)}) collective-permute-start(bf16[128,128]{0,1:T(8,128)(2,1)S(1)} %get-tuple-element.174), channel_id=1, source_target_pairs={{0,4},{2,6},{4,0},{6,2},{8,12},{10,14},{12,8},{14,10},{1,5},{3,7},... | collective-permute-start | bytes 98312 | tf_op jit(solution)/shard_map/ppermute | solution.py:83
  200.9 6.2 %collective-permute-start.34 = (bf16[128,896]{1,0:T(8,128)(2,1)}, bf16[128,896]{1,0:T(8,128)(2,1)S(1)}, u32[]{:S(2)}, u32[]{:S(2)}) collective-permute-start(bf16[128,896]{1,0:T(8,128)(2,1)} %convolution_convert_fusion.2), channel_id=1, source_target_pairs={{0,1},{1,0},{2,3},{3,2},{4,5},{5,4},{6,7},{7,6},{8,9},{9,8},{10,11... | collective-permute-start | bytes 688136 | tf_op jit(solution)/shard_map/ppermute | solution.py:76
  204.8 17.8 %collective-permute-start.35 = (bf16[4,2,56,1024]{3,2,1,0:T(8,128)(2,1)}, bf16[4,2,56,1024]{3,2,1,0:T(8,128)(2,1)}, u32[]{:S(2)}, u32[]{:S(2)}) collective-permute-start(bf16[4,2,56,1024]{3,2,1,0:T(8,128)(2,1)} %bitcast.88), channel_id=1, source_target_pairs={{0,16},{16,0},{1,17},{17,1},{2,18},{18,2},{3,19},{19,3},{4,20},{20... | collective-permute-start | bytes 2752520 | tf_op jit(solution)/shard_map/ppermute | solution.py:73
  209.1 10.5 %all-to-all-start = ((f32[16,8,128]{2,1,0:T(8,128)}), f32[16,8,128]{2,1,0:T(8,128)S(1)}, u32[]{:S(2)}, u32[]{:S(2)}) async-start(f32[16,8,128]{2,1,0:T(8,128)} %pad.50.clone), calls=%async_computation | async-start | bytes 131072 | tf_op jit(solution)/shard_map/all_to_all | solution.py:86
  222.6 2.4 collective-permute-start.43
  224.2 13.0 %collective-permute-start.36 = (bf16[4,56,1024]{2,1,0:T(8,128)(2,1)S(1)}, bf16[4,56,1024]{2,1,0:T(8,128)(2,1)S(1)}, u32[]{:S(2)}, u32[]{:S(2)}) collective-permute-start(bf16[4,56,1024]{2,1,0:T(8,128)(2,1)S(1)} %fusion.36), channel_id=1, source_target_pairs={{0,2},{2,0},{4,6},{6,4},{8,10},{10,8},{12,14},{14,12},{1,3},{3,1},... | collective-permute-start | bytes 1376264 | tf_op jit(solution)/shard_map/ppermute | solution.py:79
  237.5 7.9 %collective-permute-start.39 = (bf16[56,1024]{1,0:T(8,128)(2,1)S(1)}, bf16[56,1024]{1,0:T(8,128)(2,1)S(1)}, u32[]{:S(2)}, u32[]{:S(2)}) collective-permute-start(bf16[56,1024]{1,0:T(8,128)(2,1)S(1)} %get-tuple-element.142), channel_id=1, source_target_pairs={{0,12},{2,14},{4,8},{6,10},{8,4},{10,6},{12,0},{14,2},{1,13},{3,15... | collective-permute-start | bytes 344072 | tf_op jit(solution)/shard_map/ppermute | solution.py:83
  238.4 11.3 %collective-permute-start.38 = (bf16[56,1024]{1,0:T(8,128)(2,1)S(1)}, bf16[56,1024]{1,0:T(8,128)(2,1)S(1)}, u32[]{:S(2)}, u32[]{:S(2)}) collective-permute-start(bf16[56,1024]{1,0:T(8,128)(2,1)S(1)} %get-tuple-element.143), channel_id=1, source_target_pairs={{0,8},{2,10},{4,12},{6,14},{8,0},{10,2},{12,4},{14,6},{1,9},{3,11}... | collective-permute-start | bytes 344072 | tf_op jit(solution)/shard_map/ppermute | solution.py:83
  239.6 10.1 %collective-permute-start.37 = (bf16[56,1024]{1,0:T(8,128)(2,1)S(1)}, bf16[56,1024]{1,0:T(8,128)(2,1)S(1)}, u32[]{:S(2)}, u32[]{:S(2)}) collective-permute-start(bf16[56,1024]{1,0:T(8,128)(2,1)S(1)} %get-tuple-element.141), channel_id=1, source_target_pairs={{0,4},{2,6},{4,0},{6,2},{8,12},{10,14},{12,8},{14,10},{1,5},{3,7},... | collective-permute-start | bytes 344072 | tf_op jit(solution)/shard_map/ppermute | solution.py:83
  242.0 10.7 %collective-permute-start.44 = (bf16[2,56,1920]{2,1,0:T(8,128)(2,1)S(1)}, bf16[2,56,1920]{2,1,0:T(8,128)(2,1)S(1)}, u32[]{:S(2)}, u32[]{:S(2)}) collective-permute-start(bf16[2,56,1920]{2,1,0:T(8,128)(2,1)S(1)} %select_bitcast_fusion.4), channel_id=1, source_target_pairs={{0,2},{2,0},{4,6},{6,4},{8,10},{10,8},{12,14},{14,12},{1,3},{3,1},... | collective-permute-start | bytes 1290248 | tf_op jit(solution)/shard_map/ppermute | solution.py:79
  (33 other events, 301.2 us)
where the time goes:
time: 257 us; the launch traced here: 256 us
  waiting for transfers between devices  104 us (40%)
  starting transfers between devices  65.5 us (25%)
  other arithmetic  36.1 us (14%)
  local copies, waits for them, and re-layouts  26.3 us (10%)
  matrix products  21.9 us (9%)
    ppermute x21, waiting for transfers between devices, swap_hi(): return lax.ppermute(v, 'ctx', perm)  57.8 us
    ppermute x21, starting transfers between devices, swap_hi(): return lax.ppermute(v, 'ctx', perm)  45.8 us
    ppermute x11, waiting for transfers between devices, swap_lo(): return lax.ppermute(v, 'ctx', lo_pair)  40.1 us
    ppermute x11, starting transfers between devices, swap_lo(): return lax.ppermute(v, 'ctx', lo_pair)  9.42 us
    unnamed x78, local copies, waits for them, and re-layouts  7.44 us
    dot_general x6, matrix products, dot_tn(): lax.dot_general(a, b, (((0,), (0,)), ((), ())), preferred_element_type=f32)  6.69 us
    dot_general x5, matrix products, dot_nn(): return jnp.dot(a, b, preferred_element_type=f32)  6.4 us
    dot_general x6, matrix products, dot_nt(): lax.dot_general(a, b, (((1,), (1,)), ((), ())), preferred_element_type=f32)  6.08 us
  transfers between devices with their start and end apart: 46, of which 21 were waited for; matrix products, arithmetic and copies ran while one was open for 27% of the time, Pallas kernels for 0%

commit v1 on v0

--- a/solution.py
+++ b/solution.py
@@ -50,6 +50,12 @@
     return lax.optimization_barrier((value,) + others)[0]
 
 
+def summed(terms):
+    if len(terms) == 1:
+        return terms[0]
+    return sum(m.astype(f32) for m in terms).astype(bf16)
+
+
 def dot_nt(a, b):
     return lax.dot_general(a, b, (((1,), (1,)), ((), ())), preferred_element_type=f32)
 
@@ -116,7 +122,8 @@
         total = lax.dynamic_index_in_dim(parts, hi, 0, keepdims=False).astype(f32)
         for k in range(1, n_hi):
             part = lax.dynamic_index_in_dim(parts, jnp.bitwise_xor(hi, k), 0, keepdims=False)
-            total = total + swap_hi(part, k).astype(f32)
+            part = swap_hi(part, k)
+            total = total + part.astype(f32)
         return total
 
     def gather_rows(block, c, hi, lo, start=None):
@@ -127,12 +134,11 @@
         both = in_order(lo, mine, swap_lo(mine), axis=1)
         return in_order(c, both, swap_dp(both))
 
-    def scatter_rows(parts, c, hi, lo):
+    def scatter_near(parts, c, lo):
         keep, send = pick(c, parts)
         keep = keep + swap_dp(send.astype(bf16)).astype(f32)
         keep, send = pick(lo, (keep[:, 0], keep[:, 1]))
-        keep = keep + swap_lo(send.astype(bf16)).astype(f32)
-        return scatter_hi(keep.astype(bf16), hi)
+        return (keep + swap_lo(send.astype(bf16)).astype(f32)).astype(bf16)
 
     def gather_tokens(block):
         both = jnp.concatenate([block, swap_lo(block)], axis=0)
@@ -238,13 +244,17 @@
         query_rows = jnp.transpose(query_heads, (1, 0, 2)).reshape(group_size * tokens, head_dim)
         pair_kv = jnp.concatenate([key_head, value_head], axis=1)
         w_ot = gather_rows(block_o, c, hi, lo, pair_kv).reshape(model_width, -1)
-        relayed = {0: after(plane, pair_kv)}
-        for mask in relay_masks():
-            for k in list(relayed):
-                relayed[k ^ mask] = swap_hi(relayed[k], mask)
-        w_ffn = by_mask([relayed[k] for k in range(n_hi)], hi)
-        w_ffn = jnp.transpose(w_ffn, (1, 0, 2, 3, 4)).reshape(model_width, 3 * piece)
-        w_gu, w_dt = w_ffn[:, : 2 * piece], w_ffn[:, 2 * piece :]
+        plane = after(plane, pair_kv)
+        cut = 2 * piece
+        relays = {}
+        for part, block in (("gu", plane[..., :cut]), ("d", plane[..., cut:])):
+            got = {0: block}
+            for mask in relay_masks():
+                for k in list(got):
+                    got[k ^ mask] = swap_hi(got[k], mask)
+            got = by_mask([got[k] for k in range(n_hi)], hi)
+            relays[part] = jnp.transpose(got, (1, 0, 2, 3, 4)).reshape(model_width, -1)
+        w_gu, w_dt = relays["gu"], relays["d"]
         pair_kv = jnp.concatenate([pair_kv] + [swap_hi(pair_kv, k) for k in range(1, n_hi)], axis=0)
         pair_kv = jnp.concatenate([pair_kv, swap_lo(pair_kv)], axis=0)
         key_all, value_all = pair_kv[:, :head_dim], pair_kv[:, head_dim:]
@@ -280,29 +290,32 @@
         grad_pre = jnp.concatenate([grad_gate, grad_up], axis=1).astype(bf16)
         ffn_in_grad = scatter_tokens(dot_nt(grad_pre, w_gu))
         hidden_next = hidden_mid + scatter_tokens(dot_nt(mixed_units, w_dt))
-        w_grad = jnp.concatenate(
-            [dot_tn(ffn_all, grad_pre), dot_tn(grad_half, mixed_units)], axis=1
-        ).astype(bf16)
-        w_grad = w_grad.reshape(n_dp, n_hi, n_lo, rows, 3 * piece)
-        w_grad = jnp.transpose(w_grad, (1, 0, 2, 3, 4))
-        parts = [
-            lax.dynamic_index_in_dim(w_grad, jnp.bitwise_xor(hi, k), 0, keepdims=False)
-            for k in range(n_hi)
-        ]
-        sums = {k: [part] for k, part in enumerate(parts)}
-        for mask in reversed(relay_masks()):
-            for k in sorted(sums, reverse=True):
-                if k & mask:
-                    terms = sums.pop(k)
-                    if len(terms) > 1:
-                        terms = [sum(m.astype(f32) for m in terms).astype(bf16)]
-                    sums[k ^ mask].append(swap_hi(terms[0], mask))
+        far = n_hi // 2
+        own_sum, far_sum = {}, {}
+        for part, full in (
+            ("gu", dot_tn(ffn_all, grad_pre)),
+            ("d", dot_tn(grad_half, mixed_units)),
+        ):
+            full = full.astype(bf16).reshape(n_dp, n_hi, n_lo, rows, -1)
+            full = jnp.transpose(full, (1, 0, 2, 3, 4))
+            sums = {
+                k: [lax.dynamic_index_in_dim(full, jnp.bitwise_xor(hi, k), 0, keepdims=False)]
+                for k in range(n_hi)
+            }
+            for mask in reversed(relay_masks()[1:]):
+                for k in sorted(sums, reverse=True):
+                    if k & mask:
+                        arrived = swap_hi(summed(sums.pop(k)), mask)
+                        sums[k ^ mask].append(arrived)
+            own_sum[part], far_sum[part] = sums[0], sums[far]
+        far_sum["gu"] = swap_hi(summed(far_sum["gu"]), far)
 
         back_ffn, gain_ffn_part = rms_backward(ffn_in_grad, normed_f, scale_f, gain_ffn)
         grad_mid = grad_out + back_ffn
         grad_mid_half = grad_mid.astype(bf16)
         grad_attn = dot_nn(grad_mid_half, w_ot).astype(bf16)
         out_part = dot_tn(grad_mid_half, attn_flat)
+        out_near = scatter_near(out_part.reshape(n_dp, n_hi, n_lo, rows, -1), c, lo)
         grad_rows = jnp.transpose(
             grad_attn.reshape(tokens, group_size, head_dim), (1, 0, 2)
         ).reshape(group_size * tokens, head_dim)
@@ -314,6 +327,8 @@
         query_grad = dot_nn(grad_scores, key_all) * score_scale
         key_grad_all = dot_tn(grad_scores, query_rows) * score_scale
         kv_grad = jnp.concatenate([key_grad_all, value_grad_all], axis=1)
+        far_sum["d"] = [after(m, kv_grad) for m in far_sum["d"]]
+        far_sum["d"] = swap_hi(summed(far_sum["d"]), far)
         kv_grad = kv_grad.reshape(n_lo, n_hi, tokens, 2 * head_dim)
         kv_grad = kv_grad[0] + swap_lo(kv_grad[1].astype(bf16)).astype(f32)
         kv_grad = kv_grad[0] + sum(
@@ -333,8 +348,8 @@
         input_grad = grad_mid + back_attn
         qkv_part = dot_tn(attn_in, grad_qkv_half)
 
-        row_parts = jnp.concatenate([qkv_part, out_part], axis=1)
-        row_sums = scatter_rows(row_parts.reshape(n_dp, n_hi, n_lo, rows, -1), c, hi, lo)
+        qkv_near = scatter_near(qkv_part.reshape(n_dp, n_hi, n_lo, rows, -1), c, lo)
+        row_sums = scatter_hi(jnp.concatenate([qkv_near, out_near], axis=-1), hi)
         qkv_sum, out_grad = row_sums[:, :width_q], row_sums[:, width_q:]
         side = jnp.stack(
             [
@@ -343,13 +358,18 @@
             ],
             axis=1,
         )
-        side = jnp.pad(side, ((0, 0), (0, 5), (0, 0)))
-        side = jnp.sum(exchange(side, ("dp", "ctx")), axis=0)
-
-        w_grad = sum(after(m, grad_qkv_half).astype(f32) for m in sums[0]).astype(bf16)
+        w_grad = jnp.concatenate(
+            [
+                sum(after(m, qkv_near).astype(f32) for m in own_sum[part] + [far_sum[part]])
+                for part in ("gu", "d")
+            ],
+            axis=-1,
+        ).astype(bf16)
         keep, send = pick(c, w_grad)
         by_c = in_order(c, keep, swap_dp(send))
         keep, send = pick(lo, (by_c[:, 0], by_c[:, 1]))
+        side = jnp.pad(after(side, send), ((0, 0), (0, 5), (0, 0)))
+        side = jnp.sum(exchange(side, ("dp", "ctx")), axis=0)
         by_q = in_order(lo, keep, swap_lo(send)).reshape(splits, rows, 3 * piece).astype(f32)
         gate_grad, up_grad, down_grad = [
             jnp.concatenate(

time: 257 us -> 269 us (1.047)
  waiting for transfers between devices: 104 us -> 117 us
  matrix products: 21.9 us -> 17.4 us
    ppermute x11 -> x12, waiting for transfers between devices: 40.1 us -> 48.5 us  [swap_lo(): return lax.ppermute(v, 'ctx', lo_pair)]
    ppermute x21 -> x27, starting transfers between devices: 45.8 us -> 38.1 us  [swap_hi(): return lax.ppermute(v, 'ctx', perm)]
    ppermute x4, waiting for transfers between devices: 0.44 us -> 8.07 us  [swap_mp(): return lax.ppermute(v, 'mp', pair)]
    ppermute x11 -> x12, starting transfers between devices: 9.42 us -> 15.8 us  [swap_lo(): return lax.ppermute(v, 'ctx', lo_pair)]
    unnamed x78 -> x96, local copies, waits for them, and re-layouts: 7.44 us -> 3.98 us
    another operation x2 -> x4, other arithmetic: 1.69 us -> 4.88 us
    ppermute x21 -> x27, waiting for transfers between devices: 57.8 us -> 55.2 us  [swap_hi(): return lax.ppermute(v, 'ctx', perm)]
  transfers between devices with their start and end apart: 46 -> 54, of which waited for: 21 -> 23; matrix products, arithmetic and copies ran while one was open for 27% -> 26% of each run, Pallas kernels for 0% -> 0%
where the time goes in v1:
time: 269 us; the launch traced here: 268 us
  waiting for transfers between devices  117 us (43%)
  starting transfers between devices  66.5 us (25%)
  other arithmetic  38.7 us (14%)
  local copies, waits for them, and re-layouts  26.4 us (10%)
  matrix products  17.4 us (6%)
    ppermute x27, waiting for transfers between devices, swap_hi(): return lax.ppermute(v, 'ctx', perm)  55.2 us
    ppermute x12, waiting for transfers between devices, swap_lo(): return lax.ppermute(v, 'ctx', lo_pair)  48.5 us
    ppermute x27, starting transfers between devices, swap_hi(): return lax.ppermute(v, 'ctx', perm)  38.1 us
    ppermute x12, starting transfers between devices, swap_lo(): return lax.ppermute(v, 'ctx', lo_pair)  15.8 us
    ppermute x4, waiting for transfers between devices, swap_mp(): return lax.ppermute(v, 'mp', pair)  8.07 us
    ppermute x4, starting transfers between devices, swap_mp(): return lax.ppermute(v, 'mp', pair)  6.33 us
    dot_general x6, matrix products, dot_nt(): lax.dot_general(a, b, (((1,), (1,)), ((), ())), preferred_element_type=f32)  5.39 us
  transfers between devices with their start and end apart: 54, of which 23 were waited for; matrix products, arithmetic and copies ran while one was open for 26% of the time, Pallas kernels for 0%

profile of v1, /device:TPU:0, one launch (start us, length us, event | category | flops | bytes accessed | tf_op | source)
XLA Modules:
  0.0 267.9 jit_solution(10311861333743657432)
XLA Ops:
  2.3 5.1 %collective-permute-start.11 = (bf16[56,448]{1,0:T(8,128)(2,1)}, bf16[56,448]{1,0:T(8,128)(2,1)S(1)}, u32[]{:S(2)}, u32[]{:S(2)}) collective-permute-start(bf16[56,448]{1,0:T(8,128)(2,1)} %bitcast.391), channel_id=1, source_target_pairs={{0,12},{2,14},{4,8},{6,10},{8,4},{10,6},{12,0},{14,2},{1,13},{3,15... | collective-permute-start | bytes 150536 | tf_op jit(solution)/shard_map/ppermute | solution.py:89
  7.5 1.9 collective-permute-start.2
  21.9 6.3 %collective-permute-done.28 = bf16[128,896]{1,0:T(8,128)(2,1)S(1)} collective-permute-done((bf16[128,896]{1,0:T(8,128)(2,1)S(1)}, bf16[128,896]{1,0:T(8,128)(2,1)S(1)}, u32[]{:S(2)}, u32[]{:S(2)}) %collective-permute-start.28) | collective-permute-done | bytes 229408 | tf_op jit(solution)/shard_map/ppermute | solution.py:85
  29.8 7.6 %collective-permute-done.17 = bf16[2,56,1920]{2,1,0:T(8,128)(2,1)S(1)} collective-permute-done((bf16[2,56,1920]{2,1,0:T(8,128)(2,1)S(1)}, bf16[2,56,1920]{2,1,0:T(8,128)(2,1)S(1)}, u32[]{:S(2)}, u32[]{:S(2)}) %collective-permute-start.17) | collective-permute-done | bytes 430112 | tf_op jit(solution)/shard_map/ppermute | solution.py:85
  37.6 5.5 %collective-permute-done.3 = bf16[4,64,576]{2,1,0:T(8,128)(2,1)S(1)} collective-permute-done((bf16[4,64,576]{2,1,0:T(8,128)(2,1)S(1)}, bf16[4,64,576]{2,1,0:T(8,128)(2,1)S(1)}, u32[]{:S(2)}, u32[]{:S(2)}) %collective-permute-start.3) | collective-permute-done | bytes 294944 | tf_op jit(solution)/shard_map/ppermute | solution.py:85
  48.8 2.5 collective-permute-start.7
  53.3 2.0 collective-permute-start.5
  55.4 2.9 %collective-permute-start.23 = (bf16[2,2,56,640]{3,2,1,0:T(8,128)(2,1)}, bf16[2,2,56,640]{3,2,1,0:T(8,128)(2,1)}, u32[]{:S(2)}, u32[]{:S(2)}) collective-permute-start(bf16[2,2,56,640]{3,2,1,0:T(8,128)(2,1)} %get-tuple-element.158), channel_id=1, source_target_pairs={{0,8},{2,10},{4,12},{6,14},{8,0},{10,2},{12,4},{14,6},{1,9},{3,11}... | collective-permute-start | bytes 860168 | tf_op jit(solution)/shard_map/ppermute | solution.py:89
  59.6 1.8 collective-permute-start.20
  62.2 1.6 collective-permute-start.8
  65.3 1.9 collective-permute-done.8
  69.6 3.7 %collective-permute-done.12 = bf16[4,56,448]{2,1,0:T(8,128)(2,1)S(1)} collective-permute-done((bf16[4,56,448]{2,1,0:T(8,128)(2,1)S(1)}, bf16[4,56,448]{2,1,0:T(8,128)(2,1)S(1)}, u32[]{:S(2)}, u32[]{:S(2)}) %collective-permute-start.12) | collective-permute-done | bytes 200736 | tf_op jit(solution)/shard_map/ppermute | solution.py:85
  74.4 2.7 %fusion.12 = bf16[896,64]{0,1:T(8,128)(2,1)S(1)} fusion(f32[896,1024]{1,0:T(8,128)S(1)} %get-tuple-element.219, f32[896]{0:T(1024)S(1)} %get-tuple-element.218, s32[1024]{0:T(1024)S(1)} %bitcast.402, s32[896]{0:T(1024)S(1)} %copy-done.38, bf16[1024,128]{0,1:T(8,128)(2,1)S(1)} %copy-done.27, f32[896]{0:T(1024)S(1)} %fusion), kind=kOutput, calls=%fused_computation.45 | convolution fusion | flops 707510272 | bytes 3932160 | tf_op jit(solution)/shard_map/dot_general | solution.py:267
  79.6 1.6 collective-permute-start.14
  81.2 13.1 %collective-permute-done.20 = bf16[2,2,56,1280]{3,2,1,0:T(8,128)(2,1)} collective-permute-done((bf16[2,2,56,1280]{3,2,1,0:T(8,128)(2,1)}, bf16[2,2,56,1280]{3,2,1,0:T(8,128)(2,1)}, u32[]{:S(2)}, u32[]{:S(2)}) %collective-permute-start.20) | collective-permute-done | bytes 573472 | tf_op jit(solution)/shard_map/ppermute | solution.py:89
  94.3 3.4 %collective-permute-start.21 = (bf16[2,2,56,1280]{3,2,1,0:T(8,128)(2,1)}, bf16[2,2,56,1280]{3,2,1,0:T(8,128)(2,1)S(1)}, u32[]{:S(2)}, u32[]{:S(2)}) collective-permute-start(bf16[2,2,56,1280]{3,2,1,0:T(8,128)(2,1)} %collective-permute-done.20), channel_id=1, source_target_pairs={{0,4},{2,6},{4,0},{6,2},{8,12},{10,14},{12,8},{14,10},{1,5},{3,7},... | collective-permute-start | bytes 1720328 | tf_op jit(solution)/shard_map/ppermute | solution.py:89
  97.7 3.8 %collective-permute-done.24 = bf16[2,2,56,640]{3,2,1,0:T(8,128)(2,1)S(1)} collective-permute-done((bf16[2,2,56,640]{3,2,1,0:T(8,128)(2,1)}, bf16[2,2,56,640]{3,2,1,0:T(8,128)(2,1)S(1)}, u32[]{:S(2)}, u32[]{:S(2)}) %collective-permute-start.24) | collective-permute-done | bytes 286752 | tf_op jit(solution)/shard_map/ppermute | solution.py:89
  105.0 4.1 %collective-permute-done.15 = bf16[128,896]{1,0:T(8,128)(2,1)S(1)} collective-permute-done((bf16[128,896]{1,0:T(8,128)(2,1)S(1)}, bf16[128,896]{1,0:T(8,128)(2,1)S(1)}, u32[]{:S(2)}, u32[]{:S(2)}) %collective-permute-start.15) | collective-permute-done | bytes 229408 | tf_op jit(solution)/shard_map/ppermute | solution.py:85
  109.2 3.5 %collective-permute-done.21 = bf16[2,2,56,1280]{3,2,1,0:T(8,128)(2,1)S(1)} collective-permute-done((bf16[2,2,56,1280]{3,2,1,0:T(8,128)(2,1)}, bf16[2,2,56,1280]{3,2,1,0:T(8,128)(2,1)S(1)}, u32[]{:S(2)}, u32[]{:S(2)}) %collective-permute-start.21) | collective-permute-done | bytes 573472 | tf_op jit(solution)/shard_map/ppermute | solution.py:89
  114.8 1.7 fusion.35
  131.5 8.9 %collective-permute-done.41 = bf16[2,2,56,1280]{3,2,1,0:T(8,128)(2,1)S(1)} collective-permute-done((bf16[2,2,56,1280]{3,2,1,0:T(8,128)(2,1)S(1)}, bf16[2,2,56,1280]{3,2,1,0:T(8,128)(2,1)S(1)}, u32[]{:S(2)}, u32[]{:S(2)}) %collective-permute-start.41) | collective-permute-done | bytes 573472 | tf_op jit(solution)/shard_map/ppermute | solution.py:89
  142.9 1.6 collective-permute-start.32
  144.5 2.0 collective-permute-done.26
  146.5 1.6 collective-permute-start.27
  148.1 3.2 %collective-permute-done.32 = bf16[128,896]{1,0:T(8,128)(2,1)S(1)} collective-permute-done((bf16[128,896]{1,0:T(8,128)(2,1)S(1)}, bf16[128,896]{1,0:T(8,128)(2,1)S(1)}, u32[]{:S(2)}, u32[]{:S(2)}) %collective-permute-start.32) | collective-permute-done | bytes 229408 | tf_op jit(solution)/shard_map/ppermute | solution.py:82
  151.5 2.3 collective-permute-done.27
  161.9 1.7 copy.211
  163.5 1.7 copy.212
  166.4 1.8 copy.210
  168.2 1.8 copy.213
  171.3 1.8 add_convert_fusion.2
  173.1 1.7 fusion.103
  176.4 2.4 collective-permute-start.36
  181.2 2.8 %collective-permute-start.42 = (bf16[2,2,56,1280]{3,2,1,0:T(8,128)(2,1)}, bf16[2,2,56,1280]{3,2,1,0:T(8,128)(2,1)}, u32[]{:S(2)}, u32[]{:S(2)}) collective-permute-start(bf16[2,2,56,1280]{3,2,1,0:T(8,128)(2,1)} %fusion.10), channel_id=1, source_target_pairs={{0,8},{2,10},{4,12},{6,14},{8,0},{10,2},{12,4},{14,6},{1,9},{3,11}... | collective-permute-start | bytes 1720328 | tf_op jit(solution)/shard_map/ppermute | solution.py:89
  184.0 12.6 %collective-permute-done.35 = bf16[128,128]{0,1:T(8,128)(2,1)} collective-permute-done((bf16[128,128]{0,1:T(8,128)(2,1)}, bf16[128,128]{0,1:T(8,128)(2,1)}, u32[]{:S(2)}, u32[]{:S(2)}) %collective-permute-start.35) | collective-permute-done | bytes 32800 | tf_op jit(solution)/shard_map/ppermute | solution.py:89
  199.0 1.6 collective-permute-start.37
  202.6 2.5 collective-permute-done.37
  206.5 1.9 add_bitcast_fusion
  212.0 6.2 %collective-permute-done.48 = bf16[4,56,448]{2,1,0:T(8,128)(2,1)S(1)} collective-permute-done((bf16[4,56,448]{2,1,0:T(8,128)(2,1)S(1)}, bf16[4,56,448]{2,1,0:T(8,128)(2,1)S(1)}, u32[]{:S(2)}, u32[]{:S(2)}) %collective-permute-start.48) | collective-permute-done | bytes 200736 | tf_op jit(solution)/shard_map/ppermute | solution.py:85
  218.4 5.5 %collective-permute-done.39 = bf16[4,56,576]{2,1,0:T(8,128)(2,1)S(1)} collective-permute-done((bf16[4,56,576]{2,1,0:T(8,128)(2,1)S(1)}, bf16[4,56,576]{2,1,0:T(8,128)(2,1)S(1)}, u32[]{:S(2)}, u32[]{:S(2)}) %collective-permute-start.39) | collective-permute-done | bytes 258080 | tf_op jit(solution)/shard_map/ppermute | solution.py:85
  224.0 8.3 %collective-permute-done.45 = bf16[2,2,56,640]{3,2,1,0:T(8,128)(2,1)S(1)} collective-permute-done((bf16[2,2,56,640]{3,2,1,0:T(8,128)(2,1)S(1)}, bf16[2,2,56,640]{3,2,1,0:T(8,128)(2,1)S(1)}, u32[]{:S(2)}, u32[]{:S(2)}) %collective-permute-start.45) | collective-permute-done | bytes 286752 | tf_op jit(solution)/shard_map/ppermute | solution.py:89
  232.5 2.7 collective-permute-start.50
  235.2 1.7 collective-permute-start.51
  239.6 4.8 %collective-permute-done.50 = bf16[56,1024]{1,0:T(8,128)(2,1)S(1)} collective-permute-done((bf16[56,1024]{1,0:T(8,128)(2,1)S(1)}, bf16[56,1024]{1,0:T(8,128)(2,1)S(1)}, u32[]{:S(2)}, u32[]{:S(2)}) %collective-permute-start.50) | collective-permute-done | bytes 114720 | tf_op jit(solution)/shard_map/ppermute | solution.py:89
  246.2 5.0 %all-to-all-start = ((f32[16,8,128]{2,1,0:T(8,128)}), f32[16,8,128]{2,1,0:T(8,128)S(1)}, u32[]{:S(2)}, u32[]{:S(2)}) async-start(f32[16,8,128]{2,1,0:T(8,128)} %pad.50.clone), calls=%async_computation | async-start | bytes 131072 | tf_op jit(solution)/shard_map/all_to_all | solution.py:92
  251.9 1.9 collective-permute-start.52
  253.9 4.1 %all-to-all-done = f32[16,8,128]{2,1,0:T(8,128)S(1)} async-done(((f32[16,8,128]{2,1,0:T(8,128)}), f32[16,8,128]{2,1,0:T(8,128)S(1)}, u32[]{:S(2)}, u32[]{:S(2)}) %all-to-all-start) | async-done | bytes 65568 | tf_op jit(solution)/shard_map/all_to_all | solution.py:92
  259.0 5.7 %collective-permute-done.52 = bf16[2,56,1920]{2,1,0:T(8,128)(2,1)S(1)} collective-permute-done((bf16[2,56,1920]{2,1,0:T(8,128)(2,1)S(1)}, bf16[2,56,1920]{2,1,0:T(8,128)(2,1)S(1)}, u32[]{:S(2)}, u32[]{:S(2)}) %collective-permute-start.52) | collective-permute-done | bytes 430112 | tf_op jit(solution)/shard_map/ppermute | solution.py:85
  (335 shorter events, 89.4 us)
Async XLA Ops:
  2.3 52.9 %collective-permute-start.11 = (bf16[56,448]{1,0:T(8,128)(2,1)}, bf16[56,448]{1,0:T(8,128)(2,1)S(1)}, u32[]{:S(2)}, u32[]{:S(2)}) collective-permute-start(bf16[56,448]{1,0:T(8,128)(2,1)} %bitcast.391), channel_id=1, source_target_pairs={{0,12},{2,14},{4,8},{6,10},{8,4},{10,6},{12,0},{14,2},{1,13},{3,15... | collective-permute-start | bytes 150536 | tf_op jit(solution)/shard_map/ppermute | solution.py:89
  7.5 47.9 %collective-permute-start.10 = (bf16[56,448]{1,0:T(8,128)(2,1)}, bf16[56,448]{1,0:T(8,128)(2,1)S(1)}, u32[]{:S(2)}, u32[]{:S(2)}) collective-permute-start(bf16[56,448]{1,0:T(8,128)(2,1)} %bitcast.392), channel_id=1, source_target_pairs={{0,8},{2,10},{4,12},{6,14},{8,0},{10,2},{12,4},{14,6},{1,9},{3,11}... | collective-permute-start | bytes 150536 | tf_op jit(solution)/shard_map/ppermute | solution.py:89
  7.5 11.4 %collective-permute-start.2 = (bf16[64,576]{1,0:T(8,128)(2,1)S(1)}, bf16[64,576]{1,0:T(8,128)(2,1)S(1)}, u32[]{:S(2)}, u32[]{:S(2)}) collective-permute-start(bf16[64,576]{1,0:T(8,128)(2,1)S(1)} %get-tuple-element.202), channel_id=1, source_target_pairs={{0,12},{2,14},{4,8},{6,10},{8,4},{10,6},{12,0},{14,2},{1,13},{3,15... | collective-permute-start | bytes 221192 | tf_op jit(solution)/shard_map/ppermute | solution.py:89
  9.4 10.3 %collective-permute-start.1 = (bf16[64,576]{1,0:T(8,128)(2,1)S(1)}, bf16[64,576]{1,0:T(8,128)(2,1)S(1)}, u32[]{:S(2)}, u32[]{:S(2)}) collective-permute-start(bf16[64,576]{1,0:T(8,128)(2,1)S(1)} %get-tuple-element.202), channel_id=1, source_target_pairs={{0,8},{2,10},{4,12},{6,14},{8,0},{10,2},{12,4},{14,6},{1,9},{3,11}... | collective-permute-start | bytes 221192 | tf_op jit(solution)/shard_map/ppermute | solution.py:89
  10.4 10.8 %collective-permute-start = (bf16[64,576]{1,0:T(8,128)(2,1)S(1)}, bf16[64,576]{1,0:T(8,128)(2,1)S(1)}, u32[]{:S(2)}, u32[]{:S(2)}) collective-permute-start(bf16[64,576]{1,0:T(8,128)(2,1)S(1)} %get-tuple-element.202), channel_id=1, source_target_pairs={{0,4},{2,6},{4,0},{6,2},{8,12},{10,14},{12,8},{14,10},{1,5},{3,7},... | collective-permute-start | bytes 221192 | tf_op jit(solution)/shard_map/ppermute | solution.py:89
  18.9 34.3 %collective-permute-start.9 = (bf16[56,448]{1,0:T(8,128)(2,1)S(1)}, bf16[56,448]{1,0:T(8,128)(2,1)S(1)}, u32[]{:S(2)}, u32[]{:S(2)}) collective-permute-start(bf16[56,448]{1,0:T(8,128)(2,1)S(1)} %bitcast.393), channel_id=1, source_target_pairs={{0,4},{2,6},{4,0},{6,2},{8,12},{10,14},{12,8},{14,10},{1,5},{3,7},... | collective-permute-start | bytes 150536 | tf_op jit(solution)/shard_map/ppermute | solution.py:89
  19.7 8.5 %collective-permute-start.28 = (bf16[128,896]{1,0:T(8,128)(2,1)S(1)}, bf16[128,896]{1,0:T(8,128)(2,1)S(1)}, u32[]{:S(2)}, u32[]{:S(2)}) collective-permute-start(bf16[128,896]{1,0:T(8,128)(2,1)S(1)} %bitcast_convert_fusion.1), channel_id=1, source_target_pairs={{0,2},{2,0},{4,6},{6,4},{8,10},{10,8},{12,14},{14,12},{1,3},{3,1},... | collective-permute-start | bytes 688136 | tf_op jit(solution)/shard_map/ppermute | solution.py:85
  21.2 16.2 %collective-permute-start.17 = (bf16[2,56,1920]{2,1,0:T(8,128)(2,1)S(1)}, bf16[2,56,1920]{2,1,0:T(8,128)(2,1)S(1)}, u32[]{:S(2)}, u32[]{:S(2)}) collective-permute-start(bf16[2,56,1920]{2,1,0:T(8,128)(2,1)S(1)} %broadcast_select_fusion.2), channel_id=1, source_target_pairs={{0,2},{2,0},{4,6},{6,4},{8,10},{10,8},{12,14},{14,12},{1,3},{3,1},... | collective-permute-start | bytes 1290248 | tf_op jit(solution)/shard_map/ppermute | solution.py:85
  28.2 15.0 %collective-permute-start.3 = (bf16[4,64,576]{2,1,0:T(8,128)(2,1)S(1)}, bf16[4,64,576]{2,1,0:T(8,128)(2,1)S(1)}, u32[]{:S(2)}, u32[]{:S(2)}) collective-permute-start(bf16[4,64,576]{2,1,0:T(8,128)(2,1)S(1)} %pad_maximum_fusion.33), channel_id=1, source_target_pairs={{0,2},{2,0},{4,6},{6,4},{8,10},{10,8},{12,14},{14,12},{1,3},{3,1},... | collective-permute-start | bytes 884744 | tf_op jit(solution)/shard_map/ppermute | solution.py:85
  37.4 6.0 %collective-permute-start.29 = (bf16[256,896]{1,0:T(8,128)(2,1)S(1)}, bf16[256,896]{1,0:T(8,128)(2,1)S(1)}, u32[]{:S(2)}, u32[]{:S(2)}) collective-permute-start(bf16[256,896]{1,0:T(8,128)(2,1)S(1)} %pad_maximum_fusion.25), channel_id=1, source_target_pairs={{0,16},{16,0},{1,17},{17,1},{2,18},{18,2},{3,19},{19,3},{4,20},{20... | collective-permute-start | bytes 1376264 | tf_op jit(solution)/shard_map/ppermute | solution.py:79
  48.8 10.5 %collective-permute-start.7 = (bf16[128,128]{0,1:T(8,128)(2,1)}, bf16[128,128]{0,1:T(8,128)(2,1)}, u32[]{:S(2)}, u32[]{:S(2)}) collective-permute-start(bf16[128,128]{0,1:T(8,128)(2,1)} %get-tuple-element.207), channel_id=1, source_target_pairs={{0,12},{2,14},{4,8},{6,10},{8,4},{10,6},{12,0},{14,2},{1,13},{3,15... | collective-permute-start | bytes 98312 | tf_op jit(solution)/shard_map/ppermute | solution.py:89
  51.3 8.2 %collective-permute-start.6 = (bf16[128,128]{0,1:T(8,128)(2,1)}, bf16[128,128]{0,1:T(8,128)(2,1)}, u32[]{:S(2)}, u32[]{:S(2)}) collective-permute-start(bf16[128,128]{0,1:T(8,128)(2,1)} %get-tuple-element.207), channel_id=1, source_target_pairs={{0,8},{2,10},{4,12},{6,14},{8,0},{10,2},{12,4},{14,6},{1,9},{3,11}... | collective-permute-start | bytes 98312 | tf_op jit(solution)/shard_map/ppermute | solution.py:89
  53.3 8.1 %collective-permute-start.5 = (bf16[128,128]{0,1:T(8,128)(2,1)}, bf16[128,128]{0,1:T(8,128)(2,1)S(1)}, u32[]{:S(2)}, u32[]{:S(2)}) collective-permute-start(bf16[128,128]{0,1:T(8,128)(2,1)} %get-tuple-element.207), channel_id=1, source_target_pairs={{0,4},{2,6},{4,0},{6,2},{8,12},{10,14},{12,8},{14,10},{1,5},{3,7},... | collective-permute-start | bytes 98312 | tf_op jit(solution)/shard_map/ppermute | solution.py:89
  55.2 42.5 %collective-permute-start.22 = (bf16[2,2,56,640]{3,2,1,0:T(8,128)(2,1)}, bf16[2,2,56,640]{3,2,1,0:T(8,128)(2,1)}, u32[]{:S(2)}, u32[]{:S(2)}) collective-permute-start(bf16[2,2,56,640]{3,2,1,0:T(8,128)(2,1)} %get-tuple-element.158), channel_id=1, source_target_pairs={{0,4},{2,6},{4,0},{6,2},{8,12},{10,14},{12,8},{14,10},{1,5},{3,7},... | collective-permute-start | bytes 860168 | tf_op jit(solution)/shard_map/ppermute | solution.py:89
  55.4 22.0 %collective-permute-start.23 = (bf16[2,2,56,640]{3,2,1,0:T(8,128)(2,1)}, bf16[2,2,56,640]{3,2,1,0:T(8,128)(2,1)}, u32[]{:S(2)}, u32[]{:S(2)}) collective-permute-start(bf16[2,2,56,640]{3,2,1,0:T(8,128)(2,1)} %get-tuple-element.158), channel_id=1, source_target_pairs={{0,8},{2,10},{4,12},{6,14},{8,0},{10,2},{12,4},{14,6},{1,9},{3,11}... | collective-permute-start | bytes 860168 | tf_op jit(solution)/shard_map/ppermute | solution.py:89
  59.4 49.8 %collective-permute-start.19 = (bf16[2,2,56,1280]{3,2,1,0:T(8,128)(2,1)}, bf16[2,2,56,1280]{3,2,1,0:T(8,128)(2,1)}, u32[]{:S(2)}, u32[]{:S(2)}) collective-permute-start(bf16[2,2,56,1280]{3,2,1,0:T(8,128)(2,1)} %get-tuple-element.160), channel_id=1, source_target_pairs={{0,4},{2,6},{4,0},{6,2},{8,12},{10,14},{12,8},{14,10},{1,5},{3,7},... | collective-permute-start | bytes 1720328 | tf_op jit(solution)/shard_map/ppermute | solution.py:89
  59.6 34.7 %collective-permute-start.20 = (bf16[2,2,56,1280]{3,2,1,0:T(8,128)(2,1)}, bf16[2,2,56,1280]{3,2,1,0:T(8,128)(2,1)}, u32[]{:S(2)}, u32[]{:S(2)}) collective-permute-start(bf16[2,2,56,1280]{3,2,1,0:T(8,128)(2,1)} %get-tuple-element.160), channel_id=1, source_target_pairs={{0,8},{2,10},{4,12},{6,14},{8,0},{10,2},{12,4},{14,6},{1,9},{3,11}... | collective-permute-start | bytes 1720328 | tf_op jit(solution)/shard_map/ppermute | solution.py:89
  67.2 6.0 %collective-permute-start.12 = (bf16[4,56,448]{2,1,0:T(8,128)(2,1)S(1)}, bf16[4,56,448]{2,1,0:T(8,128)(2,1)S(1)}, u32[]{:S(2)}, u32[]{:S(2)}) collective-permute-start(bf16[4,56,448]{2,1,0:T(8,128)(2,1)S(1)} %pad_maximum_fusion.36), channel_id=1, source_target_pairs={{0,2},{2,0},{4,6},{6,4},{8,10},{10,8},{12,14},{14,12},{1,3},{3,1},... | collective-permute-start | bytes 602120 | tf_op jit(solution)/shard_map/ppermute | solution.py:85
  77.4 24.1 %collective-permute-start.24 = (bf16[2,2,56,640]{3,2,1,0:T(8,128)(2,1)}, bf16[2,2,56,640]{3,2,1,0:T(8,128)(2,1)S(1)}, u32[]{:S(2)}, u32[]{:S(2)}) collective-permute-start(bf16[2,2,56,640]{3,2,1,0:T(8,128)(2,1)} %collective-permute-done.23), channel_id=1, source_target_pairs={{0,4},{2,6},{4,0},{6,2},{8,12},{10,14},{12,8},{14,10},{1,5},{3,7},... | collective-permute-start | bytes 860168 | tf_op jit(solution)/shard_map/ppermute | solution.py:89
  79.6 23.1 %collective-permute-start.14 = (bf16[128,896]{1,0:T(8,128)(2,1)S(1)}, bf16[128,896]{1,0:T(8,128)(2,1)S(1)}, u32[]{:S(2)}, u32[]{:S(2)}) collective-permute-start(bf16[128,896]{1,0:T(8,128)(2,1)S(1)} %convolution_convert_fusion.3), channel_id=1, source_target_pairs={{0,1},{1,0},{2,3},{3,2},{4,5},{5,4},{6,7},{7,6},{8,9},{9,8},{10,11... | collective-permute-start | bytes 688136 | tf_op jit(solution)/shard_map/ppermute | solution.py:82
  94.3 18.5 %collective-permute-start.21 = (bf16[2,2,56,1280]{3,2,1,0:T(8,128)(2,1)}, bf16[2,2,56,1280]{3,2,1,0:T(8,128)(2,1)S(1)}, u32[]{:S(2)}, u32[]{:S(2)}) collective-permute-start(bf16[2,2,56,1280]{3,2,1,0:T(8,128)(2,1)} %collective-permute-done.20), channel_id=1, source_target_pairs={{0,4},{2,6},{4,0},{6,2},{8,12},{10,14},{12,8},{14,10},{1,5},{3,7},... | collective-permute-start | bytes 1720328 | tf_op jit(solution)/shard_map/ppermute | solution.py:89
  103.0 6.1 %collective-permute-start.15 = (bf16[128,896]{1,0:T(8,128)(2,1)S(1)}, bf16[128,896]{1,0:T(8,128)(2,1)S(1)}, u32[]{:S(2)}, u32[]{:S(2)}) collective-permute-start(bf16[128,896]{1,0:T(8,128)(2,1)S(1)} %multiply_convert_fusion.4), channel_id=1, source_target_pairs={{0,2},{2,0},{4,6},{6,4},{8,10},{10,8},{12,14},{14,12},{1,3},{3,1},... | collective-permute-start | bytes 688136 | tf_op jit(solution)/shard_map/ppermute | solution.py:85
  120.4 8.2 %collective-permute-start.30 = (bf16[256,896]{1,0:T(8,128)(2,1)S(1)}, bf16[256,896]{1,0:T(8,128)(2,1)S(1)}, u32[]{:S(2)}, u32[]{:S(2)}) collective-permute-start(bf16[256,896]{1,0:T(8,128)(2,1)S(1)} %slice.661), channel_id=1, source_target_pairs={{0,16},{16,0},{1,17},{17,1},{2,18},{18,2},{3,19},{19,3},{4,20},{20... | collective-permute-start | bytes 1376264 | tf_op jit(solution)/shard_map/ppermute | solution.py:79
  120.5 9.3 %collective-permute-start.25 = (bf16[256,896]{1,0:T(8,128)(2,1)S(1)}, bf16[256,896]{1,0:T(8,128)(2,1)S(1)}, u32[]{:S(2)}, u32[]{:S(2)}) collective-permute-start(bf16[256,896]{1,0:T(8,128)(2,1)S(1)} %slice.662), channel_id=1, source_target_pairs={{0,16},{16,0},{1,17},{17,1},{2,18},{18,2},{3,19},{19,3},{4,20},{20... | collective-permute-start | bytes 1376264 | tf_op jit(solution)/shard_map/ppermute | solution.py:79
  124.5 15.9 %collective-permute-start.41 = (bf16[2,2,56,1280]{3,2,1,0:T(8,128)(2,1)S(1)}, bf16[2,2,56,1280]{3,2,1,0:T(8,128)(2,1)S(1)}, u32[]{:S(2)}, u32[]{:S(2)}) collective-permute-start(bf16[2,2,56,1280]{3,2,1,0:T(8,128)(2,1)S(1)} %get-tuple-element.119), channel_id=1, source_target_pairs={{0,4},{2,6},{4,0},{6,2},{8,12},{10,14},{12,8},{14,10},{1,5},{3,7},... | collective-permute-start | bytes 1720328 | tf_op jit(solution)/shard_map/ppermute | solution.py:89
  126.6 44.7 %collective-permute-start.44 = (bf16[2,2,56,640]{3,2,1,0:T(8,128)(2,1)}, bf16[2,2,56,640]{3,2,1,0:T(8,128)(2,1)}, u32[]{:S(2)}, u32[]{:S(2)}) collective-permute-start(bf16[2,2,56,640]{3,2,1,0:T(8,128)(2,1)} %get-tuple-element.148), channel_id=1, source_target_pairs={{0,4},{2,6},{4,0},{6,2},{8,12},{10,14},{12,8},{14,10},{1,5},{3,7},... | collective-permute-start | bytes 860168 | tf_op jit(solution)/shard_map/ppermute | solution.py:89
  127.6 104.6 %collective-permute-start.43 = (bf16[2,2,56,640]{3,2,1,0:T(8,128)(2,1)}, bf16[2,2,56,640]{3,2,1,0:T(8,128)(2,1)}, u32[]{:S(2)}, u32[]{:S(2)}) collective-permute-start(bf16[2,2,56,640]{3,2,1,0:T(8,128)(2,1)} %get-tuple-element.150), channel_id=1, source_target_pairs={{0,4},{2,6},{4,0},{6,2},{8,12},{10,14},{12,8},{14,10},{1,5},{3,7},... | collective-permute-start | bytes 860168 | tf_op jit(solution)/shard_map/ppermute | solution.py:89
  128.6 103.7 %collective-permute-start.40 = (bf16[2,2,56,1280]{3,2,1,0:T(8,128)(2,1)}, bf16[2,2,56,1280]{3,2,1,0:T(8,128)(2,1)}, u32[]{:S(2)}, u32[]{:S(2)}) collective-permute-start(bf16[2,2,56,1280]{3,2,1,0:T(8,128)(2,1)} %get-tuple-element.120), channel_id=1, source_target_pairs={{0,4},{2,6},{4,0},{6,2},{8,12},{10,14},{12,8},{14,10},{1,5},{3,7},... | collective-permute-start | bytes 1720328 | tf_op jit(solution)/shard_map/ppermute | solution.py:89
  129.8 13.0 %collective-permute-start.31 = (bf16[128,896]{1,0:T(8,128)(2,1)S(1)}, bf16[128,896]{1,0:T(8,128)(2,1)S(1)}, u32[]{:S(2)}, u32[]{:S(2)}) collective-permute-start(bf16[128,896]{1,0:T(8,128)(2,1)S(1)} %slice.663), channel_id=1, source_target_pairs={{0,2},{2,0},{4,6},{6,4},{8,10},{10,8},{12,14},{14,12},{1,3},{3,1},... | collective-permute-start | bytes 688136 | tf_op jit(solution)/shard_map/ppermute | solution.py:85
  140.4 6.0 %collective-permute-start.26 = (bf16[128,896]{1,0:T(8,128)(2,1)S(1)}, bf16[128,896]{1,0:T(8,128)(2,1)S(1)}, u32[]{:S(2)}, u32[]{:S(2)}) collective-permute-start(bf16[128,896]{1,0:T(8,128)(2,1)S(1)} %slice.664), channel_id=1, source_target_pairs={{0,2},{2,0},{4,6},{6,4},{8,10},{10,8},{12,14},{14,12},{1,3},{3,1},... | collective-permute-start | bytes 688136 | tf_op jit(solution)/shard_map/ppermute | solution.py:85
  142.9 8.4 %collective-permute-start.32 = (bf16[128,896]{1,0:T(8,128)(2,1)S(1)}, bf16[128,896]{1,0:T(8,128)(2,1)S(1)}, u32[]{:S(2)}, u32[]{:S(2)}) collective-permute-start(bf16[128,896]{1,0:T(8,128)(2,1)S(1)} %fusion.20), channel_id=1, source_target_pairs={{0,1},{1,0},{2,3},{3,2},{4,5},{5,4},{6,7},{7,6},{8,9},{9,8},{10,11... | collective-permute-start | bytes 688136 | tf_op jit(solution)/shard_map/ppermute | solution.py:82
  146.5 7.4 %collective-permute-start.27 = (bf16[128,896]{1,0:T(8,128)(2,1)S(1)}, bf16[128,896]{1,0:T(8,128)(2,1)S(1)}, u32[]{:S(2)}, u32[]{:S(2)}) collective-permute-start(bf16[128,896]{1,0:T(8,128)(2,1)S(1)} %fusion.21), channel_id=1, source_target_pairs={{0,1},{1,0},{2,3},{3,2},{4,5},{5,4},{6,7},{7,6},{8,9},{9,8},{10,11... | collective-permute-start | bytes 688136 | tf_op jit(solution)/shard_map/ppermute | solution.py:82
  165.2 7.9 %collective-permute-start.33 = (bf16[4,128,128]{1,2,0:T(8,128)(2,1)}, bf16[4,128,128]{1,2,0:T(8,128)(2,1)}, u32[]{:S(2)}, u32[]{:S(2)}) collective-permute-start(bf16[4,128,128]{1,2,0:T(8,128)(2,1)} %copy.212), channel_id=1, source_target_pairs={{0,2},{2,0},{4,6},{6,4},{8,10},{10,8},{12,14},{14,12},{1,3},{3,1},... | collective-permute-start | bytes 393224 | tf_op jit(solution)/shard_map/ppermute | solution.py:85
  175.5 5.7 %collective-permute-start.34 = (bf16[128,128]{0,1:T(8,128)(2,1)}, bf16[128,128]{0,1:T(8,128)(2,1)S(1)}, u32[]{:S(2)}, u32[]{:S(2)}) collective-permute-start(bf16[128,128]{0,1:T(8,128)(2,1)} %get-tuple-element.198), channel_id=1, source_target_pairs={{0,4},{2,6},{4,0},{6,2},{8,12},{10,14},{12,8},{14,10},{1,5},{3,7},... | collective-permute-start | bytes 98312 | tf_op jit(solution)/shard_map/ppermute | solution.py:89
  176.4 7.6 %collective-permute-start.36 = (bf16[128,128]{0,1:T(8,128)(2,1)}, bf16[128,128]{0,1:T(8,128)(2,1)}, u32[]{:S(2)}, u32[]{:S(2)}) collective-permute-start(bf16[128,128]{0,1:T(8,128)(2,1)} %get-tuple-element.199), channel_id=1, source_target_pairs={{0,12},{2,14},{4,8},{6,10},{8,4},{10,6},{12,0},{14,2},{1,13},{3,15... | collective-permute-start | bytes 98312 | tf_op jit(solution)/shard_map/ppermute | solution.py:89
  178.8 17.8 %collective-permute-start.35 = (bf16[128,128]{0,1:T(8,128)(2,1)}, bf16[128,128]{0,1:T(8,128)(2,1)}, u32[]{:S(2)}, u32[]{:S(2)}) collective-permute-start(bf16[128,128]{0,1:T(8,128)(2,1)} %get-tuple-element.200), channel_id=1, source_target_pairs={{0,8},{2,10},{4,12},{6,14},{8,0},{10,2},{12,4},{14,6},{1,9},{3,11}... | collective-permute-start | bytes 98312 | tf_op jit(solution)/shard_map/ppermute | solution.py:89
  181.2 51.1 %collective-permute-start.42 = (bf16[2,2,56,1280]{3,2,1,0:T(8,128)(2,1)}, bf16[2,2,56,1280]{3,2,1,0:T(8,128)(2,1)}, u32[]{:S(2)}, u32[]{:S(2)}) collective-permute-start(bf16[2,2,56,1280]{3,2,1,0:T(8,128)(2,1)} %fusion.10), channel_id=1, source_target_pairs={{0,8},{2,10},{4,12},{6,14},{8,0},{10,2},{12,4},{14,6},{1,9},{3,11}... | collective-permute-start | bytes 1720328 | tf_op jit(solution)/shard_map/ppermute | solution.py:89
  184.0 24.3 %collective-permute-start.47 = (bf16[4,2,56,448]{3,2,0,1:T(8,128)(2,1)}, bf16[4,2,56,448]{3,2,0,1:T(8,128)(2,1)}, u32[]{:S(2)}, u32[]{:S(2)}) collective-permute-start(bf16[4,2,56,448]{3,2,0,1:T(8,128)(2,1)} %copy.227), channel_id=1, source_target_pairs={{0,16},{16,0},{1,17},{17,1},{2,18},{18,2},{3,19},{19,3},{4,20},{20... | collective-permute-start | bytes 1204232 | tf_op jit(solution)/shard_map/ppermute | solution.py:79
  199.0 6.2 %collective-permute-start.37 = (bf16[128,896]{1,0:T(8,128)(2,1)S(1)}, bf16[128,896]{1,0:T(8,128)(2,1)}, u32[]{:S(2)}, u32[]{:S(2)}) collective-permute-start(bf16[128,896]{1,0:T(8,128)(2,1)S(1)} %convolution_convert_fusion.2), channel_id=1, source_target_pairs={{0,1},{1,0},{2,3},{3,2},{4,5},{5,4},{6,7},{7,6},{8,9},{9,8},{10,11... | collective-permute-start | bytes 688136 | tf_op jit(solution)/shard_map/ppermute | solution.py:82
  205.2 6.0 %collective-permute-start.38 = (bf16[4,2,56,576]{3,2,1,0:T(8,128)(2,1)}, bf16[4,2,56,576]{3,2,1,0:T(8,128)(2,1)S(1)}, u32[]{:S(2)}, u32[]{:S(2)}) collective-permute-start(bf16[4,2,56,576]{3,2,1,0:T(8,128)(2,1)} %bitcast.96), channel_id=1, source_target_pairs={{0,16},{16,0},{1,17},{17,1},{2,18},{18,2},{3,19},{19,3},{4,20},{20... | collective-permute-start | bytes 1548296 | tf_op jit(solution)/shard_map/ppermute | solution.py:79
  209.7 8.5 %collective-permute-start.48 = (bf16[4,56,448]{2,1,0:T(8,128)(2,1)S(1)}, bf16[4,56,448]{2,1,0:T(8,128)(2,1)S(1)}, u32[]{:S(2)}, u32[]{:S(2)}) collective-permute-start(bf16[4,56,448]{2,1,0:T(8,128)(2,1)S(1)} %fusion.40), channel_id=1, source_target_pairs={{0,2},{2,0},{4,6},{6,4},{8,10},{10,8},{12,14},{14,12},{1,3},{3,1},... | collective-permute-start | bytes 602120 | tf_op jit(solution)/shard_map/ppermute | solution.py:85
  211.4 12.5 %collective-permute-start.39 = (bf16[4,56,576]{2,1,0:T(8,128)(2,1)S(1)}, bf16[4,56,576]{2,1,0:T(8,128)(2,1)S(1)}, u32[]{:S(2)}, u32[]{:S(2)}) collective-permute-start(bf16[4,56,576]{2,1,0:T(8,128)(2,1)S(1)} %fusion.36), channel_id=1, source_target_pairs={{0,2},{2,0},{4,6},{6,4},{8,10},{10,8},{12,14},{14,12},{1,3},{3,1},... | collective-permute-start | bytes 774152 | tf_op jit(solution)/shard_map/ppermute | solution.py:85
  218.2 14.0 %collective-permute-start.45 = (bf16[2,2,56,640]{3,2,1,0:T(8,128)(2,1)S(1)}, bf16[2,2,56,640]{3,2,1,0:T(8,128)(2,1)S(1)}, u32[]{:S(2)}, u32[]{:S(2)}) collective-permute-start(bf16[2,2,56,640]{3,2,1,0:T(8,128)(2,1)S(1)} %copy-done.23), channel_id=1, source_target_pairs={{0,8},{2,10},{4,12},{6,14},{8,0},{10,2},{12,4},{14,6},{1,9},{3,11}... | collective-permute-start | bytes 860168 | tf_op jit(solution)/shard_map/ppermute | solution.py:89
  232.4 7.2 %collective-permute-start.49 = (bf16[56,1024]{1,0:T(8,128)(2,1)S(1)}, bf16[56,1024]{1,0:T(8,128)(2,1)S(1)}, u32[]{:S(2)}, u32[]{:S(2)}) collective-permute-start(bf16[56,1024]{1,0:T(8,128)(2,1)S(1)} %get-tuple-element.165), channel_id=1, source_target_pairs={{0,4},{2,6},{4,0},{6,2},{8,12},{10,14},{12,8},{14,10},{1,5},{3,7},... | collective-permute-start | bytes 344072 | tf_op jit(solution)/shard_map/ppermute | solution.py:89
  232.5 11.9 %collective-permute-start.50 = (bf16[56,1024]{1,0:T(8,128)(2,1)S(1)}, bf16[56,1024]{1,0:T(8,128)(2,1)S(1)}, u32[]{:S(2)}, u32[]{:S(2)}) collective-permute-start(bf16[56,1024]{1,0:T(8,128)(2,1)S(1)} %get-tuple-element.166), channel_id=1, source_target_pairs={{0,8},{2,10},{4,12},{6,14},{8,0},{10,2},{12,4},{14,6},{1,9},{3,11}... | collective-permute-start | bytes 344072 | tf_op jit(solution)/shard_map/ppermute | solution.py:89
  235.2 9.3 %collective-permute-start.51 = (bf16[56,1024]{1,0:T(8,128)(2,1)S(1)}, bf16[56,1024]{1,0:T(8,128)(2,1)S(1)}, u32[]{:S(2)}, u32[]{:S(2)}) collective-permute-start(bf16[56,1024]{1,0:T(8,128)(2,1)S(1)} %get-tuple-element.167), channel_id=1, source_target_pairs={{0,12},{2,14},{4,8},{6,10},{8,4},{10,6},{12,0},{14,2},{1,13},{3,15... | collective-permute-start | bytes 344072 | tf_op jit(solution)/shard_map/ppermute | solution.py:89
  246.2 11.8 %all-to-all-start = ((f32[16,8,128]{2,1,0:T(8,128)}), f32[16,8,128]{2,1,0:T(8,128)S(1)}, u32[]{:S(2)}, u32[]{:S(2)}) async-start(f32[16,8,128]{2,1,0:T(8,128)} %pad.50.clone), calls=%async_computation | async-start | bytes 131072 | tf_op jit(solution)/shard_map/all_to_all | solution.py:92
  251.9 12.8 %collective-permute-start.52 = (bf16[2,56,1920]{2,1,0:T(8,128)(2,1)S(1)}, bf16[2,56,1920]{2,1,0:T(8,128)(2,1)S(1)}, u32[]{:S(2)}, u32[]{:S(2)}) collective-permute-start(bf16[2,56,1920]{2,1,0:T(8,128)(2,1)S(1)} %select_bitcast_fusion.4), channel_id=1, source_target_pairs={{0,2},{2,0},{4,6},{6,4},{8,10},{10,8},{12,14},{14,12},{1,3},{3,1},... | collective-permute-start | bytes 1290248 | tf_op jit(solution)/shard_map/ppermute | solution.py:85
  (50 other events, 353.9 us)

commit v2 on v1

--- a/solution.py
+++ b/solution.py
@@ -135,10 +135,11 @@
         return in_order(c, both, swap_dp(both))
 
     def scatter_near(parts, c, lo):
-        keep, send = pick(c, parts)
-        keep = keep + swap_dp(send.astype(bf16)).astype(f32)
+        keep, sent = pick(c, parts.astype(bf16))
+        keep = keep.astype(f32) + swap_dp(sent).astype(f32)
         keep, send = pick(lo, (keep[:, 0], keep[:, 1]))
-        return (keep + swap_lo(send.astype(bf16)).astype(f32)).astype(bf16)
+        near = keep + swap_lo(send.astype(bf16)).astype(f32)
+        return near.astype(bf16), sent
 
     def gather_tokens(block):
         both = jnp.concatenate([block, swap_lo(block)], axis=0)
@@ -229,11 +230,11 @@
         both = in_order(lo, keep, swap_lo(send))
         block_o = after(out_weight[0].T, block_q)
         grad_out = cotangent[0]
-        grad_half = gather_tokens(after(grad_out.astype(bf16), both))
         keep, send = pick(c, (both[:, 0], both[:, 1]))
         plane = in_order(c, keep, swap_dp(send))
 
         normed_a, scale_a, attn_in = rms_forward(hidden, gain_attn)
+        attn_in = lax.optimization_barrier(attn_in)
         qkv_proj = dot_nn(attn_in, w_qkv) + b_qkv.astype(f32)
         qkv_proj = qkv_proj.reshape(tokens, group_size + 2, head_dim)
         query_heads = rotate(qkv_proj[:, :group_size], cosine_lookup, sine_lookup).astype(bf16)
@@ -243,6 +244,7 @@
         value_head = qkv_proj[:, group_size + 1].astype(bf16)
         query_rows = jnp.transpose(query_heads, (1, 0, 2)).reshape(group_size * tokens, head_dim)
         pair_kv = jnp.concatenate([key_head, value_head], axis=1)
+        grad_half = gather_tokens(after(grad_out.astype(bf16), pair_kv))
         w_ot = gather_rows(block_o, c, hi, lo, pair_kv).reshape(model_width, -1)
         plane = after(plane, pair_kv)
         cut = 2 * piece
@@ -315,7 +317,7 @@
         grad_mid_half = grad_mid.astype(bf16)
         grad_attn = dot_nn(grad_mid_half, w_ot).astype(bf16)
         out_part = dot_tn(grad_mid_half, attn_flat)
-        out_near = scatter_near(out_part.reshape(n_dp, n_hi, n_lo, rows, -1), c, lo)
+        out_near, _ = scatter_near(out_part.reshape(n_dp, n_hi, n_lo, rows, -1), c, lo)
         grad_rows = jnp.transpose(
             grad_attn.reshape(tokens, group_size, head_dim), (1, 0, 2)
         ).reshape(group_size * tokens, head_dim)
@@ -331,9 +333,8 @@
         far_sum["d"] = swap_hi(summed(far_sum["d"]), far)
         kv_grad = kv_grad.reshape(n_lo, n_hi, tokens, 2 * head_dim)
         kv_grad = kv_grad[0] + swap_lo(kv_grad[1].astype(bf16)).astype(f32)
-        kv_grad = kv_grad[0] + sum(
-            swap_hi(kv_grad[k].astype(bf16), k).astype(f32) for k in range(1, n_hi)
-        )
+        arrived = [swap_hi(kv_grad[k].astype(bf16), k) for k in range(1, n_hi)]
+        kv_grad = kv_grad[0] + sum(m.astype(f32) for m in arrived)
         key_grad, value_grad = kv_grad[:, :head_dim], kv_grad[:, head_dim:]
         query_grad = jnp.transpose(query_grad.reshape(group_size, tokens, head_dim), (1, 0, 2))
         query_grad = rotate(query_grad, cosine_lookup, -sine_lookup)
@@ -348,7 +349,7 @@
         input_grad = grad_mid + back_attn
         qkv_part = dot_tn(attn_in, grad_qkv_half)
 
-        qkv_near = scatter_near(qkv_part.reshape(n_dp, n_hi, n_lo, rows, -1), c, lo)
+        qkv_near, qkv_sent = scatter_near(qkv_part.reshape(n_dp, n_hi, n_lo, rows, -1), c, lo)
         row_sums = scatter_hi(jnp.concatenate([qkv_near, out_near], axis=-1), hi)
         qkv_sum, out_grad = row_sums[:, :width_q], row_sums[:, width_q:]
         side = jnp.stack(
@@ -358,25 +359,23 @@
             ],
             axis=1,
         )
-        w_grad = jnp.concatenate(
-            [
-                sum(after(m, qkv_near).astype(f32) for m in own_sum[part] + [far_sum[part]])
-                for part in ("gu", "d")
-            ],
-            axis=-1,
-        ).astype(bf16)
-        keep, send = pick(c, w_grad)
-        by_c = in_order(c, keep, swap_dp(send))
-        keep, send = pick(lo, (by_c[:, 0], by_c[:, 1]))
-        side = jnp.pad(after(side, send), ((0, 0), (0, 5), (0, 0)))
-        side = jnp.sum(exchange(side, ("dp", "ctx")), axis=0)
-        by_q = in_order(lo, keep, swap_lo(send)).reshape(splits, rows, 3 * piece).astype(f32)
-        gate_grad, up_grad, down_grad = [
-            jnp.concatenate(
-                [by_q[q, :, e * piece : (e + 1) * piece] for q in range(splits)], axis=1
-            )[:, :units]
-            for e in range(3)
-        ]
+        side = jnp.pad(side, ((0, 0), (0, 5), (0, 0)))
+        side = jnp.sum(after(exchange(side, ("dp", "ctx")), row_sums), axis=0)
+        by_q = {}
+        for part, tie in (("gu", qkv_sent), ("d", qkv_near)):
+            terms = own_sum[part] + [far_sum[part]]
+            w_grad = sum(after(m, tie).astype(f32) for m in terms).astype(bf16)
+            keep, send = pick(c, w_grad)
+            by_c = in_order(c, keep, swap_dp(send))
+            keep, send = pick(lo, (by_c[:, 0], by_c[:, 1]))
+            whole = in_order(lo, keep, swap_lo(send))
+            by_q[part] = whole.reshape(splits, rows, -1).astype(f32)
+
+        def units_of(part, e):
+            cols = [by_q[part][q, :, e * piece : (e + 1) * piece] for q in range(splits)]
+            return jnp.concatenate(cols, axis=1)[:, :units]
+
+        gate_grad, up_grad, down_grad = units_of("gu", 0), units_of("gu", 1), units_of("d", 0)
         return (
             hidden_next[None],
             input_grad[None],

time: 269 us -> 272 us (1.011)
  waiting for transfers between devices: 117 us -> 104 us
  starting transfers between devices: 66.5 us -> 75.6 us
    ppermute x12 -> x13, waiting for transfers between devices: 48.5 us -> 36 us  [swap_lo(): return lax.ppermute(v, 'ctx', lo_pair)]
    ppermute x27, starting transfers between devices: 38.1 us -> 49 us  [swap_hi(): return lax.ppermute(v, 'ctx', perm)]
    all_to_all x1, waiting for transfers between devices: 4.09 us -> 0.01 us  [exchange(): return lax.all_to_all(v, axes, 0, 0, tiled=True)]
    another operation x4 -> x2, other arithmetic: 4.88 us -> 1.02 us
    ppermute x27, waiting for transfers between devices: 55.2 us -> 59.1 us  [swap_hi(): return lax.ppermute(v, 'ctx', perm)]
    unnamed x96 -> x69, local copies, waits for them, and re-layouts: 3.98 us -> 7.71 us
    slice x2, local copies, waits for them, and re-layouts: 3.44 us -> 0.24 us  [local(): kv_grad = kv_grad[0] + swap_lo(kv_grad[1].astype(bf16)).astype(f32)]
    ppermute x12 -> x13, starting transfers between devices: 15.8 us -> 14.8 us  [swap_lo(): return lax.ppermute(v, 'ctx', lo_pair)]
  transfers between devices with their start and end apart: 54 -> 56, of which waited for: 23 -> 22; matrix products, arithmetic and copies ran while one was open for 26% -> 29% of each run, Pallas kernels for 0% -> 0%
where the time goes in v2:
time: 272 us; the launch traced here: 271 us
  waiting for transfers between devices  104 us (38%)
  starting transfers between devices  75.6 us (28%)
  other arithmetic  41.2 us (15%)
  local copies, waits for them, and re-layouts  28.7 us (11%)
  matrix products  19.2 us (7%)
    ppermute x27, waiting for transfers between devices, swap_hi(): return lax.ppermute(v, 'ctx', perm)  59.1 us
    ppermute x27, starting transfers between devices, swap_hi(): return lax.ppermute(v, 'ctx', perm)  49 us
    ppermute x13, waiting for transfers between devices, swap_lo(): return lax.ppermute(v, 'ctx', lo_pair)  36 us
    ppermute x13, starting transfers between devices, swap_lo(): return lax.ppermute(v, 'ctx', lo_pair)  14.8 us
    unnamed x69, local copies, waits for them, and re-layouts  7.71 us
    ppermute x4, waiting for transfers between devices, swap_mp(): return lax.ppermute(v, 'mp', pair)  7.14 us
    dot_general x6, matrix products, dot_nt(): lax.dot_general(a, b, (((1,), (1,)), ((), ())), preferred_element_type=f32)  6.28 us
    ppermute x4, starting transfers between devices, swap_mp(): return lax.ppermute(v, 'mp', pair)  6.28 us
  transfers between devices with their start and end apart: 56, of which 22 were waited for; matrix products, arithmetic and copies ran while one was open for 29% of the time, Pallas kernels for 0%

profile of v2, /device:TPU:0, one launch (start us, length us, event | category | flops | bytes accessed | tf_op | source)
XLA Modules:
  0.0 270.7 jit_solution(18056817350453666042)
XLA Ops:
  2.3 5.1 %collective-permute-start.2 = (bf16[64,576]{1,0:T(8,128)(2,1)S(1)}, bf16[64,576]{1,0:T(8,128)(2,1)S(1)}, u32[]{:S(2)}, u32[]{:S(2)}) collective-permute-start(bf16[64,576]{1,0:T(8,128)(2,1)S(1)} %get-tuple-element.153), channel_id=1, source_target_pairs={{0,12},{2,14},{4,8},{6,10},{8,4},{10,6},{12,0},{14,2},{1,13},{3,15... | collective-permute-start | bytes 221192 | tf_op jit(solution)/shard_map/ppermute | solution.py:89
  8.0 3.7 %collective-permute-start.11 = (bf16[56,448]{1,0:T(8,128)(2,1)}, bf16[56,448]{1,0:T(8,128)(2,1)}, u32[]{:S(2)}, u32[]{:S(2)}) collective-permute-start(bf16[56,448]{1,0:T(8,128)(2,1)} %bitcast.30), channel_id=1, source_target_pairs={{0,12},{2,14},{4,8},{6,10},{8,4},{10,6},{12,0},{14,2},{1,13},{3,15... | collective-permute-start | bytes 150536 | tf_op jit(solution)/shard_map/ppermute | solution.py:89
  14.9 1.6 collective-permute-start.17
  20.9 6.8 %collective-permute-done.17 = bf16[2,56,1920]{2,1,0:T(8,128)(2,1)S(1)} collective-permute-done((bf16[2,56,1920]{2,1,0:T(8,128)(2,1)S(1)}, bf16[2,56,1920]{2,1,0:T(8,128)(2,1)S(1)}, u32[]{:S(2)}, u32[]{:S(2)}) %collective-permute-start.17) | collective-permute-done | bytes 430112 | tf_op jit(solution)/shard_map/ppermute | solution.py:85
  29.4 3.3 %collective-permute-done.3 = bf16[4,64,576]{2,1,0:T(8,128)(2,1)} collective-permute-done((bf16[4,64,576]{2,1,0:T(8,128)(2,1)}, bf16[4,64,576]{2,1,0:T(8,128)(2,1)}, u32[]{:S(2)}, u32[]{:S(2)}) %collective-permute-start.3) | collective-permute-done | bytes 294944 | tf_op jit(solution)/shard_map/ppermute | solution.py:85
  34.2 1.8 collective-permute-done.4
  43.3 1.7 collective-permute-start.7
  45.1 1.8 copy.222
  46.9 1.7 collective-permute-start.5
  54.1 1.6 collective-permute-start.8
  58.3 5.1 %collective-permute-done.8 = bf16[512,128]{0,1:T(8,128)(2,1)S(1)} collective-permute-done((bf16[512,128]{0,1:T(8,128)(2,1)S(1)}, bf16[512,128]{0,1:T(8,128)(2,1)S(1)}, u32[]{:S(2)}, u32[]{:S(2)}) %collective-permute-start.8) | collective-permute-done | bytes 131104 | tf_op jit(solution)/shard_map/ppermute | solution.py:85
  65.2 1.7 fusion.108
  68.7 2.7 fusion.12
  73.2 1.6 constant_dynamic-update-slice_fusion.6
  75.8 3.4 %collective-permute-done.23 = bf16[2,2,56,640]{3,2,1,0:T(8,128)(2,1)} collective-permute-done((bf16[2,2,56,640]{3,2,1,0:T(8,128)(2,1)}, bf16[2,2,56,640]{3,2,1,0:T(8,128)(2,1)}, u32[]{:S(2)}, u32[]{:S(2)}) %collective-permute-start.23) | collective-permute-done | bytes 286752 | tf_op jit(solution)/shard_map/ppermute | solution.py:89
  79.2 12.0 %collective-permute-done.20 = bf16[2,2,56,1280]{3,2,1,0:T(8,128)(2,1)} collective-permute-done((bf16[2,2,56,1280]{3,2,1,0:T(8,128)(2,1)}, bf16[2,2,56,1280]{3,2,1,0:T(8,128)(2,1)}, u32[]{:S(2)}, u32[]{:S(2)}) %collective-permute-start.20) | collective-permute-done | bytes 573472 | tf_op jit(solution)/shard_map/ppermute | solution.py:89
  91.3 2.0 collective-permute-start.21
  95.0 1.6 collective-permute-start.14
  96.6 11.0 %collective-permute-done.24 = bf16[2,2,56,640]{3,2,1,0:T(8,128)(2,1)S(1)} collective-permute-done((bf16[2,2,56,640]{3,2,1,0:T(8,128)(2,1)}, bf16[2,2,56,640]{3,2,1,0:T(8,128)(2,1)S(1)}, u32[]{:S(2)}, u32[]{:S(2)}) %collective-permute-start.24) | collective-permute-done | bytes 286752 | tf_op jit(solution)/shard_map/ppermute | solution.py:89
  111.3 4.7 %collective-permute-done.15 = bf16[128,896]{1,0:T(8,128)(2,1)S(1)} collective-permute-done((bf16[128,896]{1,0:T(8,128)(2,1)S(1)}, bf16[128,896]{1,0:T(8,128)(2,1)S(1)}, u32[]{:S(2)}, u32[]{:S(2)}) %collective-permute-start.15) | collective-permute-done | bytes 229408 | tf_op jit(solution)/shard_map/ppermute | solution.py:85
  116.1 3.3 %collective-permute-done.21 = bf16[2,2,56,1280]{3,2,1,0:T(8,128)(2,1)S(1)} collective-permute-done((bf16[2,2,56,1280]{3,2,1,0:T(8,128)(2,1)}, bf16[2,2,56,1280]{3,2,1,0:T(8,128)(2,1)S(1)}, u32[]{:S(2)}, u32[]{:S(2)}) %collective-permute-start.21) | collective-permute-done | bytes 573472 | tf_op jit(solution)/shard_map/ppermute | solution.py:89
  121.2 1.7 fusion.27
  131.9 2.0 collective-permute-start.51
  134.0 2.0 collective-permute-start.45
  137.1 9.7 %collective-permute-done.46 = bf16[2,2,56,1280]{3,2,1,0:T(8,128)(2,1)S(1)} collective-permute-done((bf16[2,2,56,1280]{3,2,1,0:T(8,128)(2,1)S(1)}, bf16[2,2,56,1280]{3,2,1,0:T(8,128)(2,1)S(1)}, u32[]{:S(2)}, u32[]{:S(2)}) %collective-permute-start.46) | collective-permute-done | bytes 573472 | tf_op jit(solution)/shard_map/ppermute | solution.py:89
  148.6 1.6 collective-permute-start.32
  150.2 2.7 collective-permute-done.26
  152.9 1.6 collective-permute-start.27
  154.5 1.8 collective-permute-done.32
  156.5 3.1 %collective-permute-done.27 = bf16[128,896]{1,0:T(8,128)(2,1)S(1)} collective-permute-done((bf16[128,896]{1,0:T(8,128)(2,1)S(1)}, bf16[128,896]{1,0:T(8,128)(2,1)S(1)}, u32[]{:S(2)}, u32[]{:S(2)}) %collective-permute-start.27) | collective-permute-done | bytes 229408 | tf_op jit(solution)/shard_map/ppermute | solution.py:82
  169.2 1.7 add_convert_fusion.2
  172.2 1.6 collective-permute-start.36
  173.8 1.8 collective-permute-start.35
  178.1 16.5 %collective-permute-start.52 = (bf16[2,2,56,640]{3,2,1,0:T(8,128)(2,1)}, bf16[2,2,56,640]{3,2,1,0:T(8,128)(2,1)}, u32[]{:S(2)}, u32[]{:S(2)}) collective-permute-start(bf16[2,2,56,640]{3,2,1,0:T(8,128)(2,1)} %add_convert_fusion.2), channel_id=1, source_target_pairs={{0,8},{2,10},{4,12},{6,14},{8,0},{10,2},{12,4},{14,6},{1,9},{3,11}... | collective-permute-start | bytes 860168 | tf_op jit(solution)/shard_map/ppermute | solution.py:89
  198.2 11.9 %collective-permute-done.47 = bf16[2,2,56,1280]{3,2,1,0:T(8,128)(2,1)} collective-permute-done((bf16[2,2,56,1280]{3,2,1,0:T(8,128)(2,1)}, bf16[2,2,56,1280]{3,2,1,0:T(8,128)(2,1)}, u32[]{:S(2)}, u32[]{:S(2)}) %collective-permute-start.47) | collective-permute-done | bytes 573472 | tf_op jit(solution)/shard_map/ppermute | solution.py:89
  213.8 2.3 collective-permute-done.37
  220.3 4.1 %all-to-all-start = ((f32[16,8,128]{2,1,0:T(8,128)}), f32[16,8,128]{2,1,0:T(8,128)}, u32[]{:S(2)}, u32[]{:S(2)}) async-start(f32[16,8,128]{2,1,0:T(8,128)} %pad.50.clone), calls=%async_computation | async-start | bytes 131072 | tf_op jit(solution)/shard_map/all_to_all | solution.py:92
  225.1 2.0 add_bitcast_fusion
  228.3 1.8 collective-permute-start.41
  231.5 5.3 %collective-permute-done.41 = bf16[4,56,448]{2,1,0:T(8,128)(2,1)S(1)} collective-permute-done((bf16[4,56,448]{2,1,0:T(8,128)(2,1)S(1)}, bf16[4,56,448]{2,1,0:T(8,128)(2,1)S(1)}, u32[]{:S(2)}, u32[]{:S(2)}) %collective-permute-start.41) | collective-permute-done | bytes 200736 | tf_op jit(solution)/shard_map/ppermute | solution.py:85
  238.3 1.8 collective-permute-start.39
  240.1 2.9 %collective-permute-done.49 = bf16[2,56,1280]{2,1,0:T(8,128)(2,1)S(1)} collective-permute-done((bf16[2,56,1280]{2,1,0:T(8,128)(2,1)S(1)}, bf16[2,56,1280]{2,1,0:T(8,128)(2,1)S(1)}, u32[]{:S(2)}, u32[]{:S(2)}) %collective-permute-start.49) | collective-permute-done | bytes 286752 | tf_op jit(solution)/shard_map/ppermute | solution.py:85
  244.3 2.0 maximum_bitcast_fusion.1
  246.3 2.2 collective-permute-done.39
  248.8 1.6 collective-permute-start.42
  250.4 2.4 collective-permute-start.43
  254.9 6.6 %collective-permute-done.43 = bf16[56,1024]{1,0:T(8,128)(2,1)S(1)} collective-permute-done((bf16[56,1024]{1,0:T(8,128)(2,1)S(1)}, bf16[56,1024]{1,0:T(8,128)(2,1)S(1)}, u32[]{:S(2)}, u32[]{:S(2)}) %collective-permute-start.43) | collective-permute-done | bytes 114720 | tf_op jit(solution)/shard_map/ppermute | solution.py:89
  266.6 3.1 %collective-permute-done.54 = bf16[2,56,640]{2,1,0:T(8,128)(2,1)S(1)} collective-permute-done((bf16[2,56,640]{2,1,0:T(8,128)(2,1)S(1)}, bf16[2,56,640]{2,1,0:T(8,128)(2,1)S(1)}, u32[]{:S(2)}, u32[]{:S(2)}) %collective-permute-start.54) | collective-permute-done | bytes 143392 | tf_op jit(solution)/shard_map/ppermute | solution.py:85
  (319 shorter events, 92.9 us)
Async XLA Ops:
  2.3 16.6 %collective-permute-start.2 = (bf16[64,576]{1,0:T(8,128)(2,1)S(1)}, bf16[64,576]{1,0:T(8,128)(2,1)S(1)}, u32[]{:S(2)}, u32[]{:S(2)}) collective-permute-start(bf16[64,576]{1,0:T(8,128)(2,1)S(1)} %get-tuple-element.153), channel_id=1, source_target_pairs={{0,12},{2,14},{4,8},{6,10},{8,4},{10,6},{12,0},{14,2},{1,13},{3,15... | collective-permute-start | bytes 221192 | tf_op jit(solution)/shard_map/ppermute | solution.py:89
  7.4 11.5 %collective-permute-start.1 = (bf16[64,576]{1,0:T(8,128)(2,1)S(1)}, bf16[64,576]{1,0:T(8,128)(2,1)S(1)}, u32[]{:S(2)}, u32[]{:S(2)}) collective-permute-start(bf16[64,576]{1,0:T(8,128)(2,1)S(1)} %get-tuple-element.153), channel_id=1, source_target_pairs={{0,8},{2,10},{4,12},{6,14},{8,0},{10,2},{12,4},{14,6},{1,9},{3,11}... | collective-permute-start | bytes 221192 | tf_op jit(solution)/shard_map/ppermute | solution.py:89
  7.4 12.2 %collective-permute-start = (bf16[64,576]{1,0:T(8,128)(2,1)S(1)}, bf16[64,576]{1,0:T(8,128)(2,1)S(1)}, u32[]{:S(2)}, u32[]{:S(2)}) collective-permute-start(bf16[64,576]{1,0:T(8,128)(2,1)S(1)} %get-tuple-element.153), channel_id=1, source_target_pairs={{0,4},{2,6},{4,0},{6,2},{8,12},{10,14},{12,8},{14,10},{1,5},{3,7},... | collective-permute-start | bytes 221192 | tf_op jit(solution)/shard_map/ppermute | solution.py:89
  8.0 42.1 %collective-permute-start.11 = (bf16[56,448]{1,0:T(8,128)(2,1)}, bf16[56,448]{1,0:T(8,128)(2,1)}, u32[]{:S(2)}, u32[]{:S(2)}) collective-permute-start(bf16[56,448]{1,0:T(8,128)(2,1)} %bitcast.30), channel_id=1, source_target_pairs={{0,12},{2,14},{4,8},{6,10},{8,4},{10,6},{12,0},{14,2},{1,13},{3,15... | collective-permute-start | bytes 150536 | tf_op jit(solution)/shard_map/ppermute | solution.py:89
  14.9 12.8 %collective-permute-start.17 = (bf16[2,56,1920]{2,1,0:T(8,128)(2,1)S(1)}, bf16[2,56,1920]{2,1,0:T(8,128)(2,1)S(1)}, u32[]{:S(2)}, u32[]{:S(2)}) collective-permute-start(bf16[2,56,1920]{2,1,0:T(8,128)(2,1)S(1)} %broadcast_select_fusion), channel_id=1, source_target_pairs={{0,2},{2,0},{4,6},{6,4},{8,10},{10,8},{12,14},{14,12},{1,3},{3,1},... | collective-permute-start | bytes 1290248 | tf_op jit(solution)/shard_map/ppermute | solution.py:85
  18.8 28.0 %collective-permute-start.10 = (bf16[56,448]{1,0:T(8,128)(2,1)}, bf16[56,448]{1,0:T(8,128)(2,1)}, u32[]{:S(2)}, u32[]{:S(2)}) collective-permute-start(bf16[56,448]{1,0:T(8,128)(2,1)} %bitcast.30), channel_id=1, source_target_pairs={{0,8},{2,10},{4,12},{6,14},{8,0},{10,2},{12,4},{14,6},{1,9},{3,11}... | collective-permute-start | bytes 150536 | tf_op jit(solution)/shard_map/ppermute | solution.py:89
  18.8 29.8 %collective-permute-start.9 = (bf16[56,448]{1,0:T(8,128)(2,1)}, bf16[56,448]{1,0:T(8,128)(2,1)}, u32[]{:S(2)}, u32[]{:S(2)}) collective-permute-start(bf16[56,448]{1,0:T(8,128)(2,1)} %bitcast.30), channel_id=1, source_target_pairs={{0,4},{2,6},{4,0},{6,2},{8,12},{10,14},{12,8},{14,10},{1,5},{3,7},... | collective-permute-start | bytes 150536 | tf_op jit(solution)/shard_map/ppermute | solution.py:89
  20.5 12.1 %collective-permute-start.3 = (bf16[4,64,576]{2,1,0:T(8,128)(2,1)}, bf16[4,64,576]{2,1,0:T(8,128)(2,1)}, u32[]{:S(2)}, u32[]{:S(2)}) collective-permute-start(bf16[4,64,576]{2,1,0:T(8,128)(2,1)} %pad_maximum_fusion.31), channel_id=1, source_target_pairs={{0,2},{2,0},{4,6},{6,4},{8,10},{10,8},{12,14},{14,12},{1,3},{3,1},... | collective-permute-start | bytes 884744 | tf_op jit(solution)/shard_map/ppermute | solution.py:85
  40.8 12.1 %collective-permute-start.6 = (bf16[128,128]{0,1:T(8,128)(2,1)}, bf16[128,128]{0,1:T(8,128)(2,1)}, u32[]{:S(2)}, u32[]{:S(2)}) collective-permute-start(bf16[128,128]{0,1:T(8,128)(2,1)} %get-tuple-element.158), channel_id=1, source_target_pairs={{0,8},{2,10},{4,12},{6,14},{8,0},{10,2},{12,4},{14,6},{1,9},{3,11}... | collective-permute-start | bytes 98312 | tf_op jit(solution)/shard_map/ppermute | solution.py:89
  43.3 8.3 %collective-permute-start.7 = (bf16[128,128]{0,1:T(8,128)(2,1)}, bf16[128,128]{0,1:T(8,128)(2,1)S(1)}, u32[]{:S(2)}, u32[]{:S(2)}) collective-permute-start(bf16[128,128]{0,1:T(8,128)(2,1)} %get-tuple-element.158), channel_id=1, source_target_pairs={{0,12},{2,14},{4,8},{6,10},{8,4},{10,6},{12,0},{14,2},{1,13},{3,15... | collective-permute-start | bytes 98312 | tf_op jit(solution)/shard_map/ppermute | solution.py:89
  46.9 6.5 %collective-permute-start.5 = (bf16[128,128]{0,1:T(8,128)(2,1)}, bf16[128,128]{0,1:T(8,128)(2,1)S(1)}, u32[]{:S(2)}, u32[]{:S(2)}) collective-permute-start(bf16[128,128]{0,1:T(8,128)(2,1)} %get-tuple-element.158), channel_id=1, source_target_pairs={{0,4},{2,6},{4,0},{6,2},{8,12},{10,14},{12,8},{14,10},{1,5},{3,7},... | collective-permute-start | bytes 98312 | tf_op jit(solution)/shard_map/ppermute | solution.py:89
  48.6 23.9 %collective-permute-start.28 = (bf16[128,896]{1,0:T(8,128)(2,1)}, bf16[128,896]{1,0:T(8,128)(2,1)}, u32[]{:S(2)}, u32[]{:S(2)}) collective-permute-start(bf16[128,896]{1,0:T(8,128)(2,1)} %bitcast_convert_fusion.1), channel_id=1, source_target_pairs={{0,2},{2,0},{4,6},{6,4},{8,10},{10,8},{12,14},{14,12},{1,3},{3,1},... | collective-permute-start | bytes 688136 | tf_op jit(solution)/shard_map/ppermute | solution.py:85
  51.1 43.9 %collective-permute-start.22 = (bf16[2,2,56,640]{3,2,1,0:T(8,128)(2,1)}, bf16[2,2,56,640]{3,2,1,0:T(8,128)(2,1)}, u32[]{:S(2)}, u32[]{:S(2)}) collective-permute-start(bf16[2,2,56,640]{3,2,1,0:T(8,128)(2,1)} %get-tuple-element.102), channel_id=1, source_target_pairs={{0,4},{2,6},{4,0},{6,2},{8,12},{10,14},{12,8},{14,10},{1,5},{3,7},... | collective-permute-start | bytes 860168 | tf_op jit(solution)/shard_map/ppermute | solution.py:89
  51.6 27.7 %collective-permute-start.23 = (bf16[2,2,56,640]{3,2,1,0:T(8,128)(2,1)}, bf16[2,2,56,640]{3,2,1,0:T(8,128)(2,1)}, u32[]{:S(2)}, u32[]{:S(2)}) collective-permute-start(bf16[2,2,56,640]{3,2,1,0:T(8,128)(2,1)} %get-tuple-element.102), channel_id=1, source_target_pairs={{0,8},{2,10},{4,12},{6,14},{8,0},{10,2},{12,4},{14,6},{1,9},{3,11}... | collective-permute-start | bytes 860168 | tf_op jit(solution)/shard_map/ppermute | solution.py:89
  52.8 18.6 %collective-permute-start.12 = (bf16[4,56,448]{2,1,0:T(8,128)(2,1)S(1)}, bf16[4,56,448]{2,1,0:T(8,128)(2,1)S(1)}, u32[]{:S(2)}, u32[]{:S(2)}) collective-permute-start(bf16[4,56,448]{2,1,0:T(8,128)(2,1)S(1)} %pad_maximum_fusion.36), channel_id=1, source_target_pairs={{0,2},{2,0},{4,6},{6,4},{8,10},{10,8},{12,14},{14,12},{1,3},{3,1},... | collective-permute-start | bytes 602120 | tf_op jit(solution)/shard_map/ppermute | solution.py:85
  54.1 9.2 %collective-permute-start.8 = (bf16[512,128]{0,1:T(8,128)(2,1)S(1)}, bf16[512,128]{0,1:T(8,128)(2,1)S(1)}, u32[]{:S(2)}, u32[]{:S(2)}) collective-permute-start(bf16[512,128]{0,1:T(8,128)(2,1)S(1)} %pad_maximum_fusion.38), channel_id=1, source_target_pairs={{0,2},{2,0},{4,6},{6,4},{8,10},{10,8},{12,14},{14,12},{1,3},{3,1},... | collective-permute-start | bytes 393224 | tf_op jit(solution)/shard_map/ppermute | solution.py:85
  63.4 27.9 %collective-permute-start.20 = (bf16[2,2,56,1280]{3,2,1,0:T(8,128)(2,1)}, bf16[2,2,56,1280]{3,2,1,0:T(8,128)(2,1)}, u32[]{:S(2)}, u32[]{:S(2)}) collective-permute-start(bf16[2,2,56,1280]{3,2,1,0:T(8,128)(2,1)} %get-tuple-element.104), channel_id=1, source_target_pairs={{0,8},{2,10},{4,12},{6,14},{8,0},{10,2},{12,4},{14,6},{1,9},{3,11}... | collective-permute-start | bytes 1720328 | tf_op jit(solution)/shard_map/ppermute | solution.py:89
  72.3 18.9 %collective-permute-start.13 = (bf16[4,2,56,448]{3,2,0,1:T(8,128)(2,1)}, bf16[4,2,56,448]{3,2,0,1:T(8,128)(2,1)}, u32[]{:S(2)}, u32[]{:S(2)}) collective-permute-start(bf16[4,2,56,448]{3,2,0,1:T(8,128)(2,1)} %pad_maximum_fusion.22), channel_id=1, source_target_pairs={{0,16},{16,0},{1,17},{17,1},{2,18},{18,2},{3,19},{19,3},{4,20},{20... | collective-permute-start | bytes 1204232 | tf_op jit(solution)/shard_map/ppermute | solution.py:79
  72.5 43.6 %collective-permute-start.19 = (bf16[2,2,56,1280]{3,2,1,0:T(8,128)(2,1)}, bf16[2,2,56,1280]{3,2,1,0:T(8,128)(2,1)S(1)}, u32[]{:S(2)}, u32[]{:S(2)}) collective-permute-start(bf16[2,2,56,1280]{3,2,1,0:T(8,128)(2,1)} %get-tuple-element.104), channel_id=1, source_target_pairs={{0,4},{2,6},{4,0},{6,2},{8,12},{10,14},{12,8},{14,10},{1,5},{3,7},... | collective-permute-start | bytes 1720328 | tf_op jit(solution)/shard_map/ppermute | solution.py:89
  79.2 31.1 %collective-permute-start.29 = (bf16[256,896]{1,0:T(8,128)(2,1)S(1)}, bf16[256,896]{1,0:T(8,128)(2,1)S(1)}, u32[]{:S(2)}, u32[]{:S(2)}) collective-permute-start(bf16[256,896]{1,0:T(8,128)(2,1)S(1)} %pad_maximum_fusion.24), channel_id=1, source_target_pairs={{0,16},{16,0},{1,17},{17,1},{2,18},{18,2},{3,19},{19,3},{4,20},{20... | collective-permute-start | bytes 1376264 | tf_op jit(solution)/shard_map/ppermute | solution.py:79
  91.2 16.3 %collective-permute-start.24 = (bf16[2,2,56,640]{3,2,1,0:T(8,128)(2,1)}, bf16[2,2,56,640]{3,2,1,0:T(8,128)(2,1)S(1)}, u32[]{:S(2)}, u32[]{:S(2)}) collective-permute-start(bf16[2,2,56,640]{3,2,1,0:T(8,128)(2,1)} %collective-permute-done.23), channel_id=1, source_target_pairs={{0,4},{2,6},{4,0},{6,2},{8,12},{10,14},{12,8},{14,10},{1,5},{3,7},... | collective-permute-start | bytes 860168 | tf_op jit(solution)/shard_map/ppermute | solution.py:89
  91.3 28.2 %collective-permute-start.21 = (bf16[2,2,56,1280]{3,2,1,0:T(8,128)(2,1)}, bf16[2,2,56,1280]{3,2,1,0:T(8,128)(2,1)S(1)}, u32[]{:S(2)}, u32[]{:S(2)}) collective-permute-start(bf16[2,2,56,1280]{3,2,1,0:T(8,128)(2,1)} %collective-permute-done.20), channel_id=1, source_target_pairs={{0,4},{2,6},{4,0},{6,2},{8,12},{10,14},{12,8},{14,10},{1,5},{3,7},... | collective-permute-start | bytes 1720328 | tf_op jit(solution)/shard_map/ppermute | solution.py:89
  95.0 13.9 %collective-permute-start.14 = (bf16[128,896]{1,0:T(8,128)(2,1)S(1)}, bf16[128,896]{1,0:T(8,128)(2,1)S(1)}, u32[]{:S(2)}, u32[]{:S(2)}) collective-permute-start(bf16[128,896]{1,0:T(8,128)(2,1)S(1)} %convolution_convert_fusion.5), channel_id=1, source_target_pairs={{0,1},{1,0},{2,3},{3,2},{4,5},{5,4},{6,7},{7,6},{8,9},{9,8},{10,11... | collective-permute-start | bytes 688136 | tf_op jit(solution)/shard_map/ppermute | solution.py:82
  109.2 6.8 %collective-permute-start.15 = (bf16[128,896]{1,0:T(8,128)(2,1)S(1)}, bf16[128,896]{1,0:T(8,128)(2,1)S(1)}, u32[]{:S(2)}, u32[]{:S(2)}) collective-permute-start(bf16[128,896]{1,0:T(8,128)(2,1)S(1)} %multiply_convert_fusion.4), channel_id=1, source_target_pairs={{0,2},{2,0},{4,6},{6,4},{8,10},{10,8},{12,14},{14,12},{1,3},{3,1},... | collective-permute-start | bytes 688136 | tf_op jit(solution)/shard_map/ppermute | solution.py:85
  126.8 7.1 %collective-permute-start.30 = (bf16[256,896]{1,0:T(8,128)(2,1)S(1)}, bf16[256,896]{1,0:T(8,128)(2,1)S(1)}, u32[]{:S(2)}, u32[]{:S(2)}) collective-permute-start(bf16[256,896]{1,0:T(8,128)(2,1)S(1)} %slice.683), channel_id=1, source_target_pairs={{0,16},{16,0},{1,17},{17,1},{2,18},{18,2},{3,19},{19,3},{4,20},{20... | collective-permute-start | bytes 1376264 | tf_op jit(solution)/shard_map/ppermute | solution.py:79
  126.9 9.2 %collective-permute-start.25 = (bf16[256,896]{1,0:T(8,128)(2,1)S(1)}, bf16[256,896]{1,0:T(8,128)(2,1)S(1)}, u32[]{:S(2)}, u32[]{:S(2)}) collective-permute-start(bf16[256,896]{1,0:T(8,128)(2,1)S(1)} %slice.684), channel_id=1, source_target_pairs={{0,16},{16,0},{1,17},{17,1},{2,18},{18,2},{3,19},{19,3},{4,20},{20... | collective-permute-start | bytes 1376264 | tf_op jit(solution)/shard_map/ppermute | solution.py:79
  130.9 15.9 %collective-permute-start.46 = (bf16[2,2,56,1280]{3,2,1,0:T(8,128)(2,1)S(1)}, bf16[2,2,56,1280]{3,2,1,0:T(8,128)(2,1)S(1)}, u32[]{:S(2)}, u32[]{:S(2)}) collective-permute-start(bf16[2,2,56,1280]{3,2,1,0:T(8,128)(2,1)S(1)} %get-tuple-element.67), channel_id=1, source_target_pairs={{0,4},{2,6},{4,0},{6,2},{8,12},{10,14},{12,8},{14,10},{1,5},{3,7},... | collective-permute-start | bytes 1720328 | tf_op jit(solution)/shard_map/ppermute | solution.py:89
  131.9 36.0 %collective-permute-start.51 = (bf16[2,2,56,640]{3,2,1,0:T(8,128)(2,1)}, bf16[2,2,56,640]{3,2,1,0:T(8,128)(2,1)}, u32[]{:S(2)}, u32[]{:S(2)}) collective-permute-start(bf16[2,2,56,640]{3,2,1,0:T(8,128)(2,1)} %get-tuple-element.80), channel_id=1, source_target_pairs={{0,4},{2,6},{4,0},{6,2},{8,12},{10,14},{12,8},{14,10},{1,5},{3,7},... | collective-permute-start | bytes 860168 | tf_op jit(solution)/shard_map/ppermute | solution.py:89
  133.9 114.7 %collective-permute-start.50 = (bf16[2,2,56,640]{3,2,1,0:T(8,128)(2,1)}, bf16[2,2,56,640]{3,2,1,0:T(8,128)(2,1)}, u32[]{:S(2)}, u32[]{:S(2)}) collective-permute-start(bf16[2,2,56,640]{3,2,1,0:T(8,128)(2,1)} %get-tuple-element.82), channel_id=1, source_target_pairs={{0,4},{2,6},{4,0},{6,2},{8,12},{10,14},{12,8},{14,10},{1,5},{3,7},... | collective-permute-start | bytes 860168 | tf_op jit(solution)/shard_map/ppermute | solution.py:89
  134.0 62.6 %collective-permute-start.45 = (bf16[2,2,56,1280]{3,2,1,0:T(8,128)(2,1)}, bf16[2,2,56,1280]{3,2,1,0:T(8,128)(2,1)}, u32[]{:S(2)}, u32[]{:S(2)}) collective-permute-start(bf16[2,2,56,1280]{3,2,1,0:T(8,128)(2,1)} %get-tuple-element.68), channel_id=1, source_target_pairs={{0,4},{2,6},{4,0},{6,2},{8,12},{10,14},{12,8},{14,10},{1,5},{3,7},... | collective-permute-start | bytes 1720328 | tf_op jit(solution)/shard_map/ppermute | solution.py:89
  136.1 12.5 %collective-permute-start.31 = (bf16[128,896]{1,0:T(8,128)(2,1)S(1)}, bf16[128,896]{1,0:T(8,128)(2,1)S(1)}, u32[]{:S(2)}, u32[]{:S(2)}) collective-permute-start(bf16[128,896]{1,0:T(8,128)(2,1)S(1)} %slice.685), channel_id=1, source_target_pairs={{0,2},{2,0},{4,6},{6,4},{8,10},{10,8},{12,14},{14,12},{1,3},{3,1},... | collective-permute-start | bytes 688136 | tf_op jit(solution)/shard_map/ppermute | solution.py:85
  148.6 7.6 %collective-permute-start.32 = (bf16[128,896]{1,0:T(8,128)(2,1)S(1)}, bf16[128,896]{1,0:T(8,128)(2,1)S(1)}, u32[]{:S(2)}, u32[]{:S(2)}) collective-permute-start(bf16[128,896]{1,0:T(8,128)(2,1)S(1)} %fusion.19), channel_id=1, source_target_pairs={{0,1},{1,0},{2,3},{3,2},{4,5},{5,4},{6,7},{7,6},{8,9},{9,8},{10,11... | collective-permute-start | bytes 688136 | tf_op jit(solution)/shard_map/ppermute | solution.py:82
  152.9 6.7 %collective-permute-start.27 = (bf16[128,896]{1,0:T(8,128)(2,1)S(1)}, bf16[128,896]{1,0:T(8,128)(2,1)S(1)}, u32[]{:S(2)}, u32[]{:S(2)}) collective-permute-start(bf16[128,896]{1,0:T(8,128)(2,1)S(1)} %fusion.20), channel_id=1, source_target_pairs={{0,1},{1,0},{2,3},{3,2},{4,5},{5,4},{6,7},{7,6},{8,9},{9,8},{10,11... | collective-permute-start | bytes 688136 | tf_op jit(solution)/shard_map/ppermute | solution.py:82
  173.8 20.8 %collective-permute-start.35 = (bf16[128,128]{0,1:T(8,128)(2,1)S(1)}, bf16[128,128]{0,1:T(8,128)(2,1)S(1)}, u32[]{:S(2)}, u32[]{:S(2)}) collective-permute-start(bf16[128,128]{0,1:T(8,128)(2,1)S(1)} %get-tuple-element.151), channel_id=1, source_target_pairs={{0,8},{2,10},{4,12},{6,14},{8,0},{10,2},{12,4},{14,6},{1,9},{3,11}... | collective-permute-start | bytes 98312 | tf_op jit(solution)/shard_map/ppermute | solution.py:89
  176.2 33.9 %collective-permute-start.47 = (bf16[2,2,56,1280]{3,2,1,0:T(8,128)(2,1)}, bf16[2,2,56,1280]{3,2,1,0:T(8,128)(2,1)}, u32[]{:S(2)}, u32[]{:S(2)}) collective-permute-start(bf16[2,2,56,1280]{3,2,1,0:T(8,128)(2,1)} %fusion.10), channel_id=1, source_target_pairs={{0,8},{2,10},{4,12},{6,14},{8,0},{10,2},{12,4},{14,6},{1,9},{3,11}... | collective-permute-start | bytes 1720328 | tf_op jit(solution)/shard_map/ppermute | solution.py:89
  178.1 70.5 %collective-permute-start.52 = (bf16[2,2,56,640]{3,2,1,0:T(8,128)(2,1)}, bf16[2,2,56,640]{3,2,1,0:T(8,128)(2,1)}, u32[]{:S(2)}, u32[]{:S(2)}) collective-permute-start(bf16[2,2,56,640]{3,2,1,0:T(8,128)(2,1)} %add_convert_fusion.2), channel_id=1, source_target_pairs={{0,8},{2,10},{4,12},{6,14},{8,0},{10,2},{12,4},{14,6},{1,9},{3,11}... | collective-permute-start | bytes 860168 | tf_op jit(solution)/shard_map/ppermute | solution.py:89
  194.6 32.4 %collective-permute-start.40 = (bf16[4,2,56,448]{3,2,0,1:T(8,128)(2,1)}, bf16[4,2,56,448]{3,2,0,1:T(8,128)(2,1)}, u32[]{:S(2)}, u32[]{:S(2)}) collective-permute-start(bf16[4,2,56,448]{3,2,0,1:T(8,128)(2,1)} %select_bitcast_fusion.3), channel_id=1, source_target_pairs={{0,16},{16,0},{1,17},{17,1},{2,18},{18,2},{3,19},{19,3},{4,20},{20... | collective-permute-start | bytes 1204232 | tf_op jit(solution)/shard_map/ppermute | solution.py:79
  196.5 40.4 %collective-permute-start.38 = (bf16[4,2,56,576]{3,2,1,0:T(8,128)(2,1)}, bf16[4,2,56,576]{3,2,1,0:T(8,128)(2,1)}, u32[]{:S(2)}, u32[]{:S(2)}) collective-permute-start(bf16[4,2,56,576]{3,2,1,0:T(8,128)(2,1)} %select_bitcast_fusion.2), channel_id=1, source_target_pairs={{0,16},{16,0},{1,17},{17,1},{2,18},{18,2},{3,19},{19,3},{4,20},{20... | collective-permute-start | bytes 1548296 | tf_op jit(solution)/shard_map/ppermute | solution.py:79
  210.0 6.0 %collective-permute-start.37 = (bf16[128,896]{1,0:T(8,128)(2,1)S(1)}, bf16[128,896]{1,0:T(8,128)(2,1)S(1)}, u32[]{:S(2)}, u32[]{:S(2)}) collective-permute-start(bf16[128,896]{1,0:T(8,128)(2,1)S(1)} %convolution_convert_fusion.4), channel_id=1, source_target_pairs={{0,1},{1,0},{2,3},{3,2},{4,5},{5,4},{6,7},{7,6},{8,9},{9,8},{10,11... | collective-permute-start | bytes 688136 | tf_op jit(solution)/shard_map/ppermute | solution.py:82
  216.1 14.0 %collective-permute-start.48 = (bf16[2,56,1280]{2,1,0:T(8,128)(2,1)}, bf16[2,56,1280]{2,1,0:T(8,128)(2,1)}, u32[]{:S(2)}, u32[]{:S(2)}) collective-permute-start(bf16[2,56,1280]{2,1,0:T(8,128)(2,1)} %select_bitcast_fusion.13), channel_id=1, source_target_pairs={{0,16},{16,0},{1,17},{17,1},{2,18},{18,2},{3,19},{19,3},{4,20},{20... | collective-permute-start | bytes 860168 | tf_op jit(solution)/shard_map/ppermute | solution.py:79
  220.3 42.8 %all-to-all-start = ((f32[16,8,128]{2,1,0:T(8,128)}), f32[16,8,128]{2,1,0:T(8,128)}, u32[]{:S(2)}, u32[]{:S(2)}) async-start(f32[16,8,128]{2,1,0:T(8,128)} %pad.50.clone), calls=%async_computation | async-start | bytes 131072 | tf_op jit(solution)/shard_map/all_to_all | solution.py:92
  228.3 8.5 %collective-permute-start.41 = (bf16[4,56,448]{2,1,0:T(8,128)(2,1)S(1)}, bf16[4,56,448]{2,1,0:T(8,128)(2,1)S(1)}, u32[]{:S(2)}, u32[]{:S(2)}) collective-permute-start(bf16[4,56,448]{2,1,0:T(8,128)(2,1)S(1)} %fusion.37), channel_id=1, source_target_pairs={{0,2},{2,0},{4,6},{6,4},{8,10},{10,8},{12,14},{14,12},{1,3},{3,1},... | collective-permute-start | bytes 602120 | tf_op jit(solution)/shard_map/ppermute | solution.py:85
  231.2 11.8 %collective-permute-start.49 = (bf16[2,56,1280]{2,1,0:T(8,128)(2,1)S(1)}, bf16[2,56,1280]{2,1,0:T(8,128)(2,1)S(1)}, u32[]{:S(2)}, u32[]{:S(2)}) collective-permute-start(bf16[2,56,1280]{2,1,0:T(8,128)(2,1)S(1)} %fusion.28), channel_id=1, source_target_pairs={{0,2},{2,0},{4,6},{6,4},{8,10},{10,8},{12,14},{14,12},{1,3},{3,1},... | collective-permute-start | bytes 860168 | tf_op jit(solution)/shard_map/ppermute | solution.py:85
  238.3 10.3 %collective-permute-start.39 = (bf16[4,56,576]{2,1,0:T(8,128)(2,1)S(1)}, bf16[4,56,576]{2,1,0:T(8,128)(2,1)S(1)}, u32[]{:S(2)}, u32[]{:S(2)}) collective-permute-start(bf16[4,56,576]{2,1,0:T(8,128)(2,1)S(1)} %fusion.29), channel_id=1, source_target_pairs={{0,2},{2,0},{4,6},{6,4},{8,10},{10,8},{12,14},{14,12},{1,3},{3,1},... | collective-permute-start | bytes 774152 | tf_op jit(solution)/shard_map/ppermute | solution.py:85
  248.8 6.1 %collective-permute-start.42 = (bf16[56,1024]{1,0:T(8,128)(2,1)S(1)}, bf16[56,1024]{1,0:T(8,128)(2,1)S(1)}, u32[]{:S(2)}, u32[]{:S(2)}) collective-permute-start(bf16[56,1024]{1,0:T(8,128)(2,1)S(1)} %get-tuple-element.113), channel_id=1, source_target_pairs={{0,4},{2,6},{4,0},{6,2},{8,12},{10,14},{12,8},{14,10},{1,5},{3,7},... | collective-permute-start | bytes 344072 | tf_op jit(solution)/shard_map/ppermute | solution.py:89
  250.4 11.1 %collective-permute-start.43 = (bf16[56,1024]{1,0:T(8,128)(2,1)S(1)}, bf16[56,1024]{1,0:T(8,128)(2,1)S(1)}, u32[]{:S(2)}, u32[]{:S(2)}) collective-permute-start(bf16[56,1024]{1,0:T(8,128)(2,1)S(1)} %get-tuple-element.114), channel_id=1, source_target_pairs={{0,8},{2,10},{4,12},{6,14},{8,0},{10,2},{12,4},{14,6},{1,9},{3,11}... | collective-permute-start | bytes 344072 | tf_op jit(solution)/shard_map/ppermute | solution.py:89
  252.8 8.7 %collective-permute-start.44 = (bf16[56,1024]{1,0:T(8,128)(2,1)S(1)}, bf16[56,1024]{1,0:T(8,128)(2,1)S(1)}, u32[]{:S(2)}, u32[]{:S(2)}) collective-permute-start(bf16[56,1024]{1,0:T(8,128)(2,1)S(1)} %get-tuple-element.115), channel_id=1, source_target_pairs={{0,12},{2,14},{4,8},{6,10},{8,4},{10,6},{12,0},{14,2},{1,13},{3,15... | collective-permute-start | bytes 344072 | tf_op jit(solution)/shard_map/ppermute | solution.py:89
  254.5 10.0 %collective-permute-start.53 = (bf16[2,56,640]{2,1,0:T(8,128)(2,1)S(1)}, bf16[2,56,640]{2,1,0:T(8,128)(2,1)S(1)}, u32[]{:S(2)}, u32[]{:S(2)}) collective-permute-start(bf16[2,56,640]{2,1,0:T(8,128)(2,1)S(1)} %select_bitcast_fusion.17), channel_id=1, source_target_pairs={{0,16},{16,0},{1,17},{17,1},{2,18},{18,2},{3,19},{19,3},{4,20},{20... | collective-permute-start | bytes 430088 | tf_op jit(solution)/shard_map/ppermute | solution.py:79
  (39 other events, 296.8 us)

commit v3 on v2

--- a/solution.py
+++ b/solution.py
@@ -138,7 +138,8 @@
         keep, sent = pick(c, parts.astype(bf16))
         keep = keep.astype(f32) + swap_dp(sent).astype(f32)
         keep, send = pick(lo, (keep[:, 0], keep[:, 1]))
-        near = keep + swap_lo(send.astype(bf16)).astype(f32)
+        sent = send.astype(bf16)
+        near = keep + swap_lo(sent).astype(f32)
         return near.astype(bf16), sent
 
     def gather_tokens(block):
@@ -150,7 +151,8 @@
         keep = parts[:half] + swap_dp(parts[half:].astype(bf16)).astype(f32)
         half = half // 2
         keep = keep[:half] + swap_lo(keep[half:].astype(bf16)).astype(f32)
-        return sum_mp(keep)
+        sent = keep.astype(bf16)
+        return sum_mp(sent), sent
 
     def sum_mp(part):
         part = part.astype(bf16)
@@ -246,7 +248,6 @@
         pair_kv = jnp.concatenate([key_head, value_head], axis=1)
         grad_half = gather_tokens(after(grad_out.astype(bf16), pair_kv))
         w_ot = gather_rows(block_o, c, hi, lo, pair_kv).reshape(model_width, -1)
-        plane = after(plane, pair_kv)
         cut = 2 * piece
         relays = {}
         for part, block in (("gu", plane[..., :cut]), ("d", plane[..., cut:])):
@@ -254,9 +255,12 @@
             for mask in relay_masks():
                 for k in list(got):
                     got[k ^ mask] = swap_hi(got[k], mask)
-            got = by_mask([got[k] for k in range(n_hi)], hi)
-            relays[part] = jnp.transpose(got, (1, 0, 2, 3, 4)).reshape(model_width, -1)
-        w_gu, w_dt = relays["gu"], relays["d"]
+            relays[part] = [got[k] for k in range(n_hi)]
+
+        def assembled(got):
+            return jnp.transpose(by_mask(got, hi), (1, 0, 2, 3, 4)).reshape(model_width, -1)
+
+        w_gu = assembled(relays["gu"])
         pair_kv = jnp.concatenate([pair_kv] + [swap_hi(pair_kv, k) for k in range(1, n_hi)], axis=0)
         pair_kv = jnp.concatenate([pair_kv, swap_lo(pair_kv)], axis=0)
         key_all, value_all = pair_kv[:, :head_dim], pair_kv[:, head_dim:]
@@ -282,6 +286,7 @@
         normed_f, scale_f, ffn_in = rms_forward(hidden_mid, gain_ffn)
         ffn_all = gather_tokens(ffn_in)
         gate_up_pre = dot_nn(ffn_all, w_gu)
+        w_dt = assembled([after(v, gate_up_pre) for v in relays["d"]])
         gate_pre, up_pre = gate_up_pre[:, :piece], gate_up_pre[:, piece:]
         grad_mixed = dot_nn(grad_half, w_dt)
         sigmoid_gate = jax.nn.sigmoid(gate_pre)
@@ -290,14 +295,15 @@
         grad_up = grad_mixed * silu_gate
         grad_gate = grad_mixed * up_pre * (sigmoid_gate + silu_gate * (1.0 - sigmoid_gate))
         grad_pre = jnp.concatenate([grad_gate, grad_up], axis=1).astype(bf16)
-        ffn_in_grad = scatter_tokens(dot_nt(grad_pre, w_gu))
-        hidden_next = hidden_mid + scatter_tokens(dot_nt(mixed_units, w_dt))
+        ffn_in_grad, db_sent = scatter_tokens(dot_nt(grad_pre, w_gu))
         far = n_hi // 2
         own_sum, far_sum = {}, {}
-        for part, full in (
-            ("gu", dot_tn(ffn_all, grad_pre)),
-            ("d", dot_tn(grad_half, mixed_units)),
-        ):
+        for part in ("gu", "d"):
+            if part == "gu":
+                full = dot_tn(ffn_all, grad_pre)
+            else:
+                mixed_units = after(mixed_units, own_sum["gu"][0])
+                full = dot_tn(grad_half, mixed_units)
             full = full.astype(bf16).reshape(n_dp, n_hi, n_lo, rows, -1)
             full = jnp.transpose(full, (1, 0, 2, 3, 4))
             sums = {
@@ -310,6 +316,9 @@
                         arrived = swap_hi(summed(sums.pop(k)), mask)
                         sums[k ^ mask].append(arrived)
             own_sum[part], far_sum[part] = sums[0], sums[far]
+        ffn_part = dot_nt(after(mixed_units, db_sent), w_dt)
+        hidden_next = hidden_mid + scatter_tokens(ffn_part)[0]
+        far_sum["gu"] = [after(m, db_sent) for m in far_sum["gu"]]
         far_sum["gu"] = swap_hi(summed(far_sum["gu"]), far)
 
         back_ffn, gain_ffn_part = rms_backward(ffn_in_grad, normed_f, scale_f, gain_ffn)
@@ -323,12 +332,13 @@
         ).reshape(group_size * tokens, head_dim)
         delta_rows = jnp.sum(grad_rows.astype(f32) * attn_rows.astype(f32), axis=1)
         probs = jnp.where(allowed, jnp.exp(scores - log_total[:, None]), 0.0)
-        value_grad_all = dot_tn(probs.astype(bf16), grad_rows)
         grad_probs = dot_nt(grad_rows, value_all)
         grad_scores = (probs * (grad_probs - delta_rows[:, None])).astype(bf16)
         query_grad = dot_nn(grad_scores, key_all) * score_scale
-        key_grad_all = dot_tn(grad_scores, query_rows) * score_scale
-        kv_grad = jnp.concatenate([key_grad_all, value_grad_all], axis=1)
+        scaled = (query_rows.astype(f32) * score_scale).astype(bf16)
+        kv_grad = dot_tn(grad_scores, jnp.pad(scaled, ((0, 0), (0, head_dim)))) + dot_tn(
+            probs.astype(bf16), jnp.pad(grad_rows, ((0, 0), (head_dim, 0)))
+        )
         far_sum["d"] = [after(m, kv_grad) for m in far_sum["d"]]
         far_sum["d"] = swap_hi(summed(far_sum["d"]), far)
         kv_grad = kv_grad.reshape(n_lo, n_hi, tokens, 2 * head_dim)
@@ -355,14 +365,14 @@
         side = jnp.stack(
             [
                 jnp.pad(v.reshape(n_shards, -1), ((0, 0), (0, gain_cols - v.shape[0] // n_shards)))
-                for v in (gain_attn_part, gain_ffn_part, bias_part)
+                for v in (after(v, qkv_sent) for v in (gain_attn_part, gain_ffn_part, bias_part))
             ],
             axis=1,
         )
         side = jnp.pad(side, ((0, 0), (0, 5), (0, 0)))
         side = jnp.sum(after(exchange(side, ("dp", "ctx")), row_sums), axis=0)
         by_q = {}
-        for part, tie in (("gu", qkv_sent), ("d", qkv_near)):
+        for part, tie in (("gu", qkv_near), ("d", qkv_near)):
             terms = own_sum[part] + [far_sum[part]]
             w_grad = sum(after(m, tie).astype(f32) for m in terms).astype(bf16)
             keep, send = pick(c, w_grad)

time: 272 us -> 262 us (0.963)
  starting transfers between devices: 75.6 us -> 62.2 us
  other arithmetic: 41.2 us -> 35.7 us
  waiting for transfers between devices: 104 us -> 109 us
  matrix products: 19.2 us -> 24.1 us
    ppermute x27, starting transfers between devices: 49 us -> 37.8 us  [swap_hi(): return lax.ppermute(v, 'ctx', perm)]
    ppermute x13, waiting for transfers between devices: 36 us -> 41.4 us  [swap_lo(): return lax.ppermute(v, 'ctx', lo_pair)]
    ppermute x4, waiting for transfers between devices: 7.14 us -> 12 us  [swap_mp(): return lax.ppermute(v, 'mp', pair)]
    ppermute x27, waiting for transfers between devices: 59.1 us -> 54.5 us  [swap_hi(): return lax.ppermute(v, 'ctx', perm)]
    another operation x5 -> x0, local copies, waits for them, and re-layouts: 3.67 us -> none  [the longest x3 1.9 us: local(): jnp.stack([jnp.pad(v.reshape(n_shards, -1), ((0, 0), (0, gain_cols - v.sh...]
    dot_general x6, matrix products: 4.56 us -> 8.08 us  [dot_tn(): lax.dot_general(a, b, (((0,), (0,)), ((), ())), preferred_element_type=f32)]
    unnamed x69 -> x108, local copies, waits for them, and re-layouts: 7.71 us -> 6.66 us
    another operation x5 -> x6, other arithmetic: 4.47 us -> 5.44 us  [by_mask(): got = jnp.stack(got)]
  transfers between devices with their start and end apart: 56 -> 56, of which waited for: 22 -> 24; matrix products, arithmetic and copies ran while one was open for 29% -> 27% of each run, Pallas kernels for 0% -> 0%
where the time goes in v3:
time: 262 us; the launch traced here: 261 us
  waiting for transfers between devices  109 us (42%)
  starting transfers between devices  62.2 us (24%)
  other arithmetic  35.7 us (14%)
  local copies, waits for them, and re-layouts  27.2 us (10%)
  matrix products  24.1 us (9%)
    ppermute x27, waiting for transfers between devices, swap_hi(): return lax.ppermute(v, 'ctx', perm)  54.5 us
    ppermute x13, waiting for transfers between devices, swap_lo(): return lax.ppermute(v, 'ctx', lo_pair)  41.4 us
    ppermute x27, starting transfers between devices, swap_hi(): return lax.ppermute(v, 'ctx', perm)  37.8 us
    ppermute x13, starting transfers between devices, swap_lo(): return lax.ppermute(v, 'ctx', lo_pair)  15 us
    ppermute x4, waiting for transfers between devices, swap_mp(): return lax.ppermute(v, 'mp', pair)  12 us
    dot_general x6, matrix products, dot_tn(): lax.dot_general(a, b, (((0,), (0,)), ((), ())), preferred_element_type=f32)  8.08 us
    dot_general x5, matrix products, dot_nn(): return jnp.dot(a, b, preferred_element_type=f32)  7.02 us
    unnamed x108, local copies, waits for them, and re-layouts  6.66 us
  transfers between devices with their start and end apart: 56, of which 24 were waited for; matrix products, arithmetic and copies ran while one was open for 27% of the time, Pallas kernels for 0%

profile of v3, /device:TPU:0, one launch (start us, length us, event | category | flops | bytes accessed | tf_op | source)
XLA Modules:
  0.0 260.7 jit_solution(14715130816151421881)
XLA Ops:
  2.2 5.1 %collective-permute-start.2 = (bf16[64,576]{1,0:T(8,128)(2,1)S(1)}, bf16[64,576]{1,0:T(8,128)(2,1)S(1)}, u32[]{:S(2)}, u32[]{:S(2)}) collective-permute-start(bf16[64,576]{1,0:T(8,128)(2,1)S(1)} %get-tuple-element.172), channel_id=1, source_target_pairs={{0,12},{2,14},{4,8},{6,10},{8,4},{10,6},{12,0},{14,2},{1,13},{3,15... | collective-permute-start | bytes 221192 | tf_op jit(solution)/shard_map/ppermute | solution.py:89
  8.0 3.7 %collective-permute-start.11 = (bf16[56,448]{1,0:T(8,128)(2,1)}, bf16[56,448]{1,0:T(8,128)(2,1)}, u32[]{:S(2)}, u32[]{:S(2)}) collective-permute-start(bf16[56,448]{1,0:T(8,128)(2,1)} %bitcast.30), channel_id=1, source_target_pairs={{0,12},{2,14},{4,8},{6,10},{8,4},{10,6},{12,0},{14,2},{1,13},{3,15... | collective-permute-start | bytes 150536 | tf_op jit(solution)/shard_map/ppermute | solution.py:89
  15.7 1.5 collective-permute-start.17
  20.6 8.1 %collective-permute-done.17 = bf16[2,56,1920]{2,1,0:T(8,128)(2,1)S(1)} collective-permute-done((bf16[2,56,1920]{2,1,0:T(8,128)(2,1)}, bf16[2,56,1920]{2,1,0:T(8,128)(2,1)S(1)}, u32[]{:S(2)}, u32[]{:S(2)}) %collective-permute-start.17) | collective-permute-done | bytes 430112 | tf_op jit(solution)/shard_map/ppermute | solution.py:85
  30.3 3.3 %collective-permute-done.3 = bf16[4,64,576]{2,1,0:T(8,128)(2,1)} collective-permute-done((bf16[4,64,576]{2,1,0:T(8,128)(2,1)}, bf16[4,64,576]{2,1,0:T(8,128)(2,1)}, u32[]{:S(2)}, u32[]{:S(2)}) %collective-permute-start.3) | collective-permute-done | bytes 294944 | tf_op jit(solution)/shard_map/ppermute | solution.py:85
  41.1 3.5 %collective-permute-start.7 = (bf16[128,128]{0,1:T(8,128)(2,1)S(1)}, bf16[128,128]{0,1:T(8,128)(2,1)S(1)}, u32[]{:S(2)}, u32[]{:S(2)}) collective-permute-start(bf16[128,128]{0,1:T(8,128)(2,1)S(1)} %get-tuple-element.177), channel_id=1, source_target_pairs={{0,12},{2,14},{4,8},{6,10},{8,4},{10,6},{12,0},{14,2},{1,13},{3,15... | collective-permute-start | bytes 98312 | tf_op jit(solution)/shard_map/ppermute | solution.py:89
  47.3 4.0 %collective-permute-done.7 = bf16[128,128]{0,1:T(8,128)(2,1)S(1)} collective-permute-done((bf16[128,128]{0,1:T(8,128)(2,1)S(1)}, bf16[128,128]{0,1:T(8,128)(2,1)S(1)}, u32[]{:S(2)}, u32[]{:S(2)}) %collective-permute-start.7) | collective-permute-done | bytes 32800 | tf_op jit(solution)/shard_map/ppermute | solution.py:89
  51.3 5.7 %collective-permute-start.20 = (bf16[2,2,56,1280]{3,2,1,0:T(8,128)(2,1)}, bf16[2,2,56,1280]{3,2,1,0:T(8,128)(2,1)}, u32[]{:S(2)}, u32[]{:S(2)}) collective-permute-start(bf16[2,2,56,1280]{3,2,1,0:T(8,128)(2,1)} %fusion.13), channel_id=1, source_target_pairs={{0,8},{2,10},{4,12},{6,14},{8,0},{10,2},{12,4},{14,6},{1,9},{3,11}... | collective-permute-start | bytes 1720328 | tf_op jit(solution)/shard_map/ppermute | solution.py:89
  57.0 1.5 collective-permute-start.22
  62.5 4.0 %collective-permute-done.8 = bf16[512,128]{0,1:T(8,128)(2,1)S(1)} collective-permute-done((bf16[512,128]{0,1:T(8,128)(2,1)S(1)}, bf16[512,128]{0,1:T(8,128)(2,1)S(1)}, u32[]{:S(2)}, u32[]{:S(2)}) %collective-permute-start.8) | collective-permute-done | bytes 131104 | tf_op jit(solution)/shard_map/ppermute | solution.py:85
  66.5 1.5 collective-permute-start.12
  68.6 1.7 fusion.102
  73.4 2.7 %fusion.11 = bf16[896,64]{0,1:T(8,128)(2,1)S(1)} fusion(f32[896,1024]{1,0:T(8,128)S(1)} %get-tuple-element.189, f32[896]{0:T(1024)S(1)} %get-tuple-element.188, s32[1024]{0:T(1024)S(1)} %bitcast.436, s32[896]{0:T(1024)S(1)} %copy-done.40, bf16[1024,128]{0,1:T(8,128)(2,1)S(1)} %copy-done.32, f32[896]{0:T(1024)S(1)} %fusion), kind=kOutput, calls=%fused_computation.39 | convolution fusion | flops 707510272 | bytes 3932160 | tf_op jit(solution)/shard_map/dot_general | solution.py:273
  79.3 1.6 collective-permute-start.14
  83.8 3.5 %collective-permute-done.14 = bf16[128,896]{1,0:T(8,128)(2,1)S(1)} collective-permute-done((bf16[128,896]{1,0:T(8,128)(2,1)S(1)}, bf16[128,896]{1,0:T(8,128)(2,1)S(1)}, u32[]{:S(2)}, u32[]{:S(2)}) %collective-permute-start.14) | collective-permute-done | bytes 229408 | tf_op jit(solution)/shard_map/ppermute | solution.py:82
  88.2 1.6 collective-permute-start.15
  89.7 7.3 %collective-permute-done.19 = bf16[2,2,56,1280]{3,2,1,0:T(8,128)(2,1)S(1)} collective-permute-done((bf16[2,2,56,1280]{3,2,1,0:T(8,128)(2,1)}, bf16[2,2,56,1280]{3,2,1,0:T(8,128)(2,1)S(1)}, u32[]{:S(2)}, u32[]{:S(2)}) %collective-permute-start.19) | collective-permute-done | bytes 573472 | tf_op jit(solution)/shard_map/ppermute | solution.py:89
  97.0 17.7 %collective-permute-done.21 = bf16[2,2,56,1280]{3,2,1,0:T(8,128)(2,1)S(1)} collective-permute-done((bf16[2,2,56,1280]{3,2,1,0:T(8,128)(2,1)}, bf16[2,2,56,1280]{3,2,1,0:T(8,128)(2,1)S(1)}, u32[]{:S(2)}, u32[]{:S(2)}) %collective-permute-start.21) | collective-permute-done | bytes 573472 | tf_op jit(solution)/shard_map/ppermute | solution.py:89
  118.0 1.5 fusion.26
  121.5 2.1 multiply_convert_fusion.2
  123.6 1.6 fusion.12
  129.2 3.1 %convolution_convert_fusion = bf16[896,1280]{1,0:T(8,128)(2,1)S(1)} fusion(bf16[512,640]{1,0:T(8,128)(2,1)} %copy-done.50, bf16[512,640]{1,0:T(8,128)(2,1)} %copy-done.49, bf16[256,896]{1,0:T(8,128)(2,1)} %copy-done.48, bf16[128,896]{1,0:T(8,128)(2,1)} %copy-done.29, bf16[128,896]{1,0:T(8,128)(2,1)} %copy-done.20), kind=kOutput, calls=%fused_computation.4 | convolution fusion | flops 1180925952 | bytes 4521984 | tf_op jit(solution)/shard_map/dot_general | solution.py:64
  133.5 1.6 collective-permute-start.28
  136.6 4.9 %collective-permute-done.28 = bf16[128,896]{1,0:T(8,128)(2,1)S(1)} collective-permute-done((bf16[128,896]{1,0:T(8,128)(2,1)S(1)}, bf16[128,896]{1,0:T(8,128)(2,1)S(1)}, u32[]{:S(2)}, u32[]{:S(2)}) %collective-permute-start.28) | collective-permute-done | bytes 229408 | tf_op jit(solution)/shard_map/ppermute | solution.py:85
  144.9 1.8 collective-permute-start.50
  147.0 5.2 %collective-permute-done.46 = bf16[2,2,56,1280]{3,2,1,0:T(8,128)(2,1)S(1)} collective-permute-done((bf16[2,2,56,1280]{3,2,1,0:T(8,128)(2,1)S(1)}, bf16[2,2,56,1280]{3,2,1,0:T(8,128)(2,1)S(1)}, u32[]{:S(2)}, u32[]{:S(2)}) %collective-permute-start.46) | collective-permute-done | bytes 573472 | tf_op jit(solution)/shard_map/ppermute | solution.py:89
  154.8 4.5 %collective-permute-done.30 = bf16[128,896]{1,0:T(8,128)(2,1)S(1)} collective-permute-done((bf16[128,896]{1,0:T(8,128)(2,1)S(1)}, bf16[128,896]{1,0:T(8,128)(2,1)S(1)}, u32[]{:S(2)}, u32[]{:S(2)}) %collective-permute-start.30) | collective-permute-done | bytes 229408 | tf_op jit(solution)/shard_map/ppermute | solution.py:85
  161.3 4.2 %collective-permute-done.31 = bf16[128,896]{1,0:T(8,128)(2,1)S(1)} collective-permute-done((bf16[128,896]{1,0:T(8,128)(2,1)S(1)}, bf16[128,896]{1,0:T(8,128)(2,1)S(1)}, u32[]{:S(2)}, u32[]{:S(2)}) %collective-permute-start.31) | collective-permute-done | bytes 229408 | tf_op jit(solution)/shard_map/ppermute | solution.py:82
  172.0 1.8 copy.205
  173.8 2.3 fusion.9
  179.8 1.6 convolution_convert_fusion.3
  182.3 1.8 add_convert_fusion.3
  184.5 1.9 collective-permute-start.36
  190.6 11.8 %collective-permute-done.35 = bf16[128,128]{0,1:T(8,128)(2,1)S(1)} collective-permute-done((bf16[128,128]{0,1:T(8,128)(2,1)S(1)}, bf16[128,128]{0,1:T(8,128)(2,1)S(1)}, u32[]{:S(2)}, u32[]{:S(2)}) %collective-permute-start.35) | collective-permute-done | bytes 32800 | tf_op jit(solution)/shard_map/ppermute | solution.py:89
  205.2 4.3 %collective-permute-done.37 = bf16[128,896]{1,0:T(8,128)(2,1)S(1)} collective-permute-done((bf16[128,896]{1,0:T(8,128)(2,1)S(1)}, bf16[128,896]{1,0:T(8,128)(2,1)S(1)}, u32[]{:S(2)}, u32[]{:S(2)}) %collective-permute-start.37) | collective-permute-done | bytes 229408 | tf_op jit(solution)/shard_map/ppermute | solution.py:82
  210.7 2.4 collective-permute-start.52
  214.3 1.6 collective-permute-start.41
  216.1 6.0 %collective-permute-done.41 = bf16[4,56,448]{2,1,0:T(8,128)(2,1)S(1)} collective-permute-done((bf16[4,56,448]{2,1,0:T(8,128)(2,1)S(1)}, bf16[4,56,448]{2,1,0:T(8,128)(2,1)S(1)}, u32[]{:S(2)}, u32[]{:S(2)}) %collective-permute-start.41) | collective-permute-done | bytes 200736 | tf_op jit(solution)/shard_map/ppermute | solution.py:85
  222.1 1.5 collective-permute-start.39
  224.7 3.5 %all-to-all-start = ((f32[16,8,128]{2,1,0:T(8,128)}), f32[16,8,128]{2,1,0:T(8,128)S(1)}, u32[]{:S(2)}, u32[]{:S(2)}) async-start(f32[16,8,128]{2,1,0:T(8,128)} %select_maximum_fusion), calls=%async_computation | async-start | bytes 131072 | tf_op jit(solution)/shard_map/all_to_all | solution.py:92
  228.2 2.0 collective-permute-done.39
  231.9 2.3 collective-permute-start.43
  234.1 2.0 collective-permute-start.44
  239.0 4.8 %collective-permute-done.43 = bf16[56,1024]{1,0:T(8,128)(2,1)S(1)} collective-permute-done((bf16[56,1024]{1,0:T(8,128)(2,1)S(1)}, bf16[56,1024]{1,0:T(8,128)(2,1)S(1)}, u32[]{:S(2)}, u32[]{:S(2)}) %collective-permute-start.43) | collective-permute-done | bytes 114720 | tf_op jit(solution)/shard_map/ppermute | solution.py:89
  246.4 1.6 collective-permute-start.54
  248.7 4.4 %collective-permute-done.54 = bf16[2,56,640]{2,1,0:T(8,128)(2,1)S(1)} collective-permute-done((bf16[2,56,640]{2,1,0:T(8,128)(2,1)S(1)}, bf16[2,56,640]{2,1,0:T(8,128)(2,1)S(1)}, u32[]{:S(2)}, u32[]{:S(2)}) %collective-permute-start.54) | collective-permute-done | bytes 143392 | tf_op jit(solution)/shard_map/ppermute | solution.py:85
  254.2 3.1 %collective-permute-done.49 = bf16[2,56,1280]{2,1,0:T(8,128)(2,1)S(1)} collective-permute-done((bf16[2,56,1280]{2,1,0:T(8,128)(2,1)S(1)}, bf16[2,56,1280]{2,1,0:T(8,128)(2,1)S(1)}, u32[]{:S(2)}, u32[]{:S(2)}) %collective-permute-start.49) | collective-permute-done | bytes 286752 | tf_op jit(solution)/shard_map/ppermute | solution.py:85
  258.7 2.0 maximum_bitcast_fusion.1
  (356 shorter events, 87.7 us)
Async XLA Ops:
  2.2 16.1 %collective-permute-start.2 = (bf16[64,576]{1,0:T(8,128)(2,1)S(1)}, bf16[64,576]{1,0:T(8,128)(2,1)S(1)}, u32[]{:S(2)}, u32[]{:S(2)}) collective-permute-start(bf16[64,576]{1,0:T(8,128)(2,1)S(1)} %get-tuple-element.172), channel_id=1, source_target_pairs={{0,12},{2,14},{4,8},{6,10},{8,4},{10,6},{12,0},{14,2},{1,13},{3,15... | collective-permute-start | bytes 221192 | tf_op jit(solution)/shard_map/ppermute | solution.py:89
  7.4 11.1 %collective-permute-start.1 = (bf16[64,576]{1,0:T(8,128)(2,1)S(1)}, bf16[64,576]{1,0:T(8,128)(2,1)S(1)}, u32[]{:S(2)}, u32[]{:S(2)}) collective-permute-start(bf16[64,576]{1,0:T(8,128)(2,1)S(1)} %get-tuple-element.172), channel_id=1, source_target_pairs={{0,8},{2,10},{4,12},{6,14},{8,0},{10,2},{12,4},{14,6},{1,9},{3,11}... | collective-permute-start | bytes 221192 | tf_op jit(solution)/shard_map/ppermute | solution.py:89
  7.4 11.9 %collective-permute-start = (bf16[64,576]{1,0:T(8,128)(2,1)S(1)}, bf16[64,576]{1,0:T(8,128)(2,1)S(1)}, u32[]{:S(2)}, u32[]{:S(2)}) collective-permute-start(bf16[64,576]{1,0:T(8,128)(2,1)S(1)} %get-tuple-element.172), channel_id=1, source_target_pairs={{0,4},{2,6},{4,0},{6,2},{8,12},{10,14},{12,8},{14,10},{1,5},{3,7},... | collective-permute-start | bytes 221192 | tf_op jit(solution)/shard_map/ppermute | solution.py:89
  8.0 36.5 %collective-permute-start.11 = (bf16[56,448]{1,0:T(8,128)(2,1)}, bf16[56,448]{1,0:T(8,128)(2,1)}, u32[]{:S(2)}, u32[]{:S(2)}) collective-permute-start(bf16[56,448]{1,0:T(8,128)(2,1)} %bitcast.30), channel_id=1, source_target_pairs={{0,12},{2,14},{4,8},{6,10},{8,4},{10,6},{12,0},{14,2},{1,13},{3,15... | collective-permute-start | bytes 150536 | tf_op jit(solution)/shard_map/ppermute | solution.py:89
  15.7 13.0 %collective-permute-start.17 = (bf16[2,56,1920]{2,1,0:T(8,128)(2,1)}, bf16[2,56,1920]{2,1,0:T(8,128)(2,1)S(1)}, u32[]{:S(2)}, u32[]{:S(2)}) collective-permute-start(bf16[2,56,1920]{2,1,0:T(8,128)(2,1)} %broadcast_select_fusion), channel_id=1, source_target_pairs={{0,2},{2,0},{4,6},{6,4},{8,10},{10,8},{12,14},{14,12},{1,3},{3,1},... | collective-permute-start | bytes 1290248 | tf_op jit(solution)/shard_map/ppermute | solution.py:85
  18.4 26.2 %collective-permute-start.10 = (bf16[56,448]{1,0:T(8,128)(2,1)}, bf16[56,448]{1,0:T(8,128)(2,1)}, u32[]{:S(2)}, u32[]{:S(2)}) collective-permute-start(bf16[56,448]{1,0:T(8,128)(2,1)} %bitcast.30), channel_id=1, source_target_pairs={{0,8},{2,10},{4,12},{6,14},{8,0},{10,2},{12,4},{14,6},{1,9},{3,11}... | collective-permute-start | bytes 150536 | tf_op jit(solution)/shard_map/ppermute | solution.py:89
  18.5 22.6 %collective-permute-start.9 = (bf16[56,448]{1,0:T(8,128)(2,1)}, bf16[56,448]{1,0:T(8,128)(2,1)}, u32[]{:S(2)}, u32[]{:S(2)}) collective-permute-start(bf16[56,448]{1,0:T(8,128)(2,1)} %bitcast.30), channel_id=1, source_target_pairs={{0,4},{2,6},{4,0},{6,2},{8,12},{10,14},{12,8},{14,10},{1,5},{3,7},... | collective-permute-start | bytes 150536 | tf_op jit(solution)/shard_map/ppermute | solution.py:89
  20.2 13.3 %collective-permute-start.3 = (bf16[4,64,576]{2,1,0:T(8,128)(2,1)}, bf16[4,64,576]{2,1,0:T(8,128)(2,1)}, u32[]{:S(2)}, u32[]{:S(2)}) collective-permute-start(bf16[4,64,576]{2,1,0:T(8,128)(2,1)} %pad_maximum_fusion.29), channel_id=1, source_target_pairs={{0,2},{2,0},{4,6},{6,4},{8,10},{10,8},{12,14},{14,12},{1,3},{3,1},... | collective-permute-start | bytes 884744 | tf_op jit(solution)/shard_map/ppermute | solution.py:85
  35.7 83.9 %collective-permute-start.24 = (bf16[2,2,56,640]{3,2,1,0:T(8,128)(2,1)}, bf16[2,2,56,640]{3,2,1,0:T(8,128)(2,1)}, u32[]{:S(2)}, u32[]{:S(2)}) collective-permute-start(bf16[2,2,56,640]{3,2,1,0:T(8,128)(2,1)} %pad_maximum_fusion.32), channel_id=1, source_target_pairs={{0,4},{2,6},{4,0},{6,2},{8,12},{10,14},{12,8},{14,10},{1,5},{3,7},... | collective-permute-start | bytes 860168 | tf_op jit(solution)/shard_map/ppermute | solution.py:89
  37.5 43.4 %collective-permute-start.25 = (bf16[2,2,56,640]{3,2,1,0:T(8,128)(2,1)}, bf16[2,2,56,640]{3,2,1,0:T(8,128)(2,1)}, u32[]{:S(2)}, u32[]{:S(2)}) collective-permute-start(bf16[2,2,56,640]{3,2,1,0:T(8,128)(2,1)} %pad_maximum_fusion.32), channel_id=1, source_target_pairs={{0,8},{2,10},{4,12},{6,14},{8,0},{10,2},{12,4},{14,6},{1,9},{3,11}... | collective-permute-start | bytes 860168 | tf_op jit(solution)/shard_map/ppermute | solution.py:89
  41.1 10.2 %collective-permute-start.7 = (bf16[128,128]{0,1:T(8,128)(2,1)S(1)}, bf16[128,128]{0,1:T(8,128)(2,1)S(1)}, u32[]{:S(2)}, u32[]{:S(2)}) collective-permute-start(bf16[128,128]{0,1:T(8,128)(2,1)S(1)} %get-tuple-element.177), channel_id=1, source_target_pairs={{0,12},{2,14},{4,8},{6,10},{8,4},{10,6},{12,0},{14,2},{1,13},{3,15... | collective-permute-start | bytes 98312 | tf_op jit(solution)/shard_map/ppermute | solution.py:89
  44.6 12.4 %collective-permute-start.6 = (bf16[128,128]{0,1:T(8,128)(2,1)S(1)}, bf16[128,128]{0,1:T(8,128)(2,1)S(1)}, u32[]{:S(2)}, u32[]{:S(2)}) collective-permute-start(bf16[128,128]{0,1:T(8,128)(2,1)S(1)} %get-tuple-element.177), channel_id=1, source_target_pairs={{0,8},{2,10},{4,12},{6,14},{8,0},{10,2},{12,4},{14,6},{1,9},{3,11}... | collective-permute-start | bytes 98312 | tf_op jit(solution)/shard_map/ppermute | solution.py:89
  44.6 13.9 %collective-permute-start.5 = (bf16[128,128]{0,1:T(8,128)(2,1)S(1)}, bf16[128,128]{0,1:T(8,128)(2,1)}, u32[]{:S(2)}, u32[]{:S(2)}) collective-permute-start(bf16[128,128]{0,1:T(8,128)(2,1)S(1)} %get-tuple-element.177), channel_id=1, source_target_pairs={{0,4},{2,6},{4,0},{6,2},{8,12},{10,14},{12,8},{14,10},{1,5},{3,7},... | collective-permute-start | bytes 98312 | tf_op jit(solution)/shard_map/ppermute | solution.py:89
  51.3 30.4 %collective-permute-start.20 = (bf16[2,2,56,1280]{3,2,1,0:T(8,128)(2,1)}, bf16[2,2,56,1280]{3,2,1,0:T(8,128)(2,1)}, u32[]{:S(2)}, u32[]{:S(2)}) collective-permute-start(bf16[2,2,56,1280]{3,2,1,0:T(8,128)(2,1)} %fusion.13), channel_id=1, source_target_pairs={{0,8},{2,10},{4,12},{6,14},{8,0},{10,2},{12,4},{14,6},{1,9},{3,11}... | collective-permute-start | bytes 1720328 | tf_op jit(solution)/shard_map/ppermute | solution.py:89
  57.0 19.7 %collective-permute-start.22 = (bf16[128,896]{1,0:T(8,128)(2,1)S(1)}, bf16[128,896]{1,0:T(8,128)(2,1)S(1)}, u32[]{:S(2)}, u32[]{:S(2)}) collective-permute-start(bf16[128,896]{1,0:T(8,128)(2,1)S(1)} %bitcast_convert_fusion.1), channel_id=1, source_target_pairs={{0,2},{2,0},{4,6},{6,4},{8,10},{10,8},{12,14},{14,12},{1,3},{3,1},... | collective-permute-start | bytes 688136 | tf_op jit(solution)/shard_map/ppermute | solution.py:85
  59.3 7.2 %collective-permute-start.8 = (bf16[512,128]{0,1:T(8,128)(2,1)S(1)}, bf16[512,128]{0,1:T(8,128)(2,1)S(1)}, u32[]{:S(2)}, u32[]{:S(2)}) collective-permute-start(bf16[512,128]{0,1:T(8,128)(2,1)S(1)} %pad_maximum_fusion.37), channel_id=1, source_target_pairs={{0,2},{2,0},{4,6},{6,4},{8,10},{10,8},{12,14},{14,12},{1,3},{3,1},... | collective-permute-start | bytes 393224 | tf_op jit(solution)/shard_map/ppermute | solution.py:85
  66.5 6.0 %collective-permute-start.12 = (bf16[4,56,448]{2,1,0:T(8,128)(2,1)S(1)}, bf16[4,56,448]{2,1,0:T(8,128)(2,1)S(1)}, u32[]{:S(2)}, u32[]{:S(2)}) collective-permute-start(bf16[4,56,448]{2,1,0:T(8,128)(2,1)S(1)} %pad_maximum_fusion.35), channel_id=1, source_target_pairs={{0,2},{2,0},{4,6},{6,4},{8,10},{10,8},{12,14},{14,12},{1,3},{3,1},... | collective-permute-start | bytes 602120 | tf_op jit(solution)/shard_map/ppermute | solution.py:85
  76.8 6.2 %collective-permute-start.23 = (bf16[256,896]{1,0:T(8,128)(2,1)S(1)}, bf16[256,896]{1,0:T(8,128)(2,1)S(1)}, u32[]{:S(2)}, u32[]{:S(2)}) collective-permute-start(bf16[256,896]{1,0:T(8,128)(2,1)S(1)} %pad_maximum_fusion.22), channel_id=1, source_target_pairs={{0,16},{16,0},{1,17},{17,1},{2,18},{18,2},{3,19},{19,3},{4,20},{20... | collective-permute-start | bytes 1376264 | tf_op jit(solution)/shard_map/ppermute | solution.py:79
  79.3 8.1 %collective-permute-start.14 = (bf16[128,896]{1,0:T(8,128)(2,1)S(1)}, bf16[128,896]{1,0:T(8,128)(2,1)S(1)}, u32[]{:S(2)}, u32[]{:S(2)}) collective-permute-start(bf16[128,896]{1,0:T(8,128)(2,1)S(1)} %convolution_convert_fusion.5), channel_id=1, source_target_pairs={{0,1},{1,0},{2,3},{3,2},{4,5},{5,4},{6,7},{7,6},{8,9},{9,8},{10,11... | collective-permute-start | bytes 688136 | tf_op jit(solution)/shard_map/ppermute | solution.py:82
  80.9 16.1 %collective-permute-start.19 = (bf16[2,2,56,1280]{3,2,1,0:T(8,128)(2,1)}, bf16[2,2,56,1280]{3,2,1,0:T(8,128)(2,1)S(1)}, u32[]{:S(2)}, u32[]{:S(2)}) collective-permute-start(bf16[2,2,56,1280]{3,2,1,0:T(8,128)(2,1)} %fusion.13), channel_id=1, source_target_pairs={{0,4},{2,6},{4,0},{6,2},{8,12},{10,14},{12,8},{14,10},{1,5},{3,7},... | collective-permute-start | bytes 1720328 | tf_op jit(solution)/shard_map/ppermute | solution.py:89
  81.7 37.8 %collective-permute-start.26 = (bf16[2,2,56,640]{3,2,1,0:T(8,128)(2,1)}, bf16[2,2,56,640]{3,2,1,0:T(8,128)(2,1)S(1)}, u32[]{:S(2)}, u32[]{:S(2)}) collective-permute-start(bf16[2,2,56,640]{3,2,1,0:T(8,128)(2,1)} %collective-permute-done.25), channel_id=1, source_target_pairs={{0,4},{2,6},{4,0},{6,2},{8,12},{10,14},{12,8},{14,10},{1,5},{3,7},... | collective-permute-start | bytes 860168 | tf_op jit(solution)/shard_map/ppermute | solution.py:89
  83.0 31.7 %collective-permute-start.21 = (bf16[2,2,56,1280]{3,2,1,0:T(8,128)(2,1)}, bf16[2,2,56,1280]{3,2,1,0:T(8,128)(2,1)S(1)}, u32[]{:S(2)}, u32[]{:S(2)}) collective-permute-start(bf16[2,2,56,1280]{3,2,1,0:T(8,128)(2,1)} %collective-permute-done.20), channel_id=1, source_target_pairs={{0,4},{2,6},{4,0},{6,2},{8,12},{10,14},{12,8},{14,10},{1,5},{3,7},... | collective-permute-start | bytes 1720328 | tf_op jit(solution)/shard_map/ppermute | solution.py:89
  88.2 27.9 %collective-permute-start.15 = (bf16[128,896]{1,0:T(8,128)(2,1)S(1)}, bf16[128,896]{1,0:T(8,128)(2,1)S(1)}, u32[]{:S(2)}, u32[]{:S(2)}) collective-permute-start(bf16[128,896]{1,0:T(8,128)(2,1)S(1)} %multiply_convert_fusion.4), channel_id=1, source_target_pairs={{0,2},{2,0},{4,6},{6,4},{8,10},{10,8},{12,14},{14,12},{1,3},{3,1},... | collective-permute-start | bytes 688136 | tf_op jit(solution)/shard_map/ppermute | solution.py:85
  133.5 8.0 %collective-permute-start.28 = (bf16[128,896]{1,0:T(8,128)(2,1)S(1)}, bf16[128,896]{1,0:T(8,128)(2,1)S(1)}, u32[]{:S(2)}, u32[]{:S(2)}) collective-permute-start(bf16[128,896]{1,0:T(8,128)(2,1)S(1)} %slice.677), channel_id=1, source_target_pairs={{0,2},{2,0},{4,6},{6,4},{8,10},{10,8},{12,14},{14,12},{1,3},{3,1},... | collective-permute-start | bytes 688136 | tf_op jit(solution)/shard_map/ppermute | solution.py:85
  136.3 15.9 %collective-permute-start.46 = (bf16[2,2,56,1280]{3,2,1,0:T(8,128)(2,1)S(1)}, bf16[2,2,56,1280]{3,2,1,0:T(8,128)(2,1)S(1)}, u32[]{:S(2)}, u32[]{:S(2)}) collective-permute-start(bf16[2,2,56,1280]{3,2,1,0:T(8,128)(2,1)S(1)} %get-tuple-element.89), channel_id=1, source_target_pairs={{0,4},{2,6},{4,0},{6,2},{8,12},{10,14},{12,8},{14,10},{1,5},{3,7},... | collective-permute-start | bytes 1720328 | tf_op jit(solution)/shard_map/ppermute | solution.py:89
  142.6 10.5 %collective-permute-start.29 = (bf16[256,896]{1,0:T(8,128)(2,1)S(1)}, bf16[256,896]{1,0:T(8,128)(2,1)S(1)}, u32[]{:S(2)}, u32[]{:S(2)}) collective-permute-start(bf16[256,896]{1,0:T(8,128)(2,1)S(1)} %slice.674), channel_id=1, source_target_pairs={{0,16},{16,0},{1,17},{17,1},{2,18},{18,2},{3,19},{19,3},{4,20},{20... | collective-permute-start | bytes 1376264 | tf_op jit(solution)/shard_map/ppermute | solution.py:79
  144.7 31.4 %collective-permute-start.51 = (bf16[2,2,56,640]{3,2,1,0:T(8,128)(2,1)}, bf16[2,2,56,640]{3,2,1,0:T(8,128)(2,1)}, u32[]{:S(2)}, u32[]{:S(2)}) collective-permute-start(bf16[2,2,56,640]{3,2,1,0:T(8,128)(2,1)} %get-tuple-element.103), channel_id=1, source_target_pairs={{0,4},{2,6},{4,0},{6,2},{8,12},{10,14},{12,8},{14,10},{1,5},{3,7},... | collective-permute-start | bytes 860168 | tf_op jit(solution)/shard_map/ppermute | solution.py:89
  144.9 85.3 %collective-permute-start.50 = (bf16[2,2,56,640]{3,2,1,0:T(8,128)(2,1)}, bf16[2,2,56,640]{3,2,1,0:T(8,128)(2,1)}, u32[]{:S(2)}, u32[]{:S(2)}) collective-permute-start(bf16[2,2,56,640]{3,2,1,0:T(8,128)(2,1)} %get-tuple-element.105), channel_id=1, source_target_pairs={{0,4},{2,6},{4,0},{6,2},{8,12},{10,14},{12,8},{14,10},{1,5},{3,7},... | collective-permute-start | bytes 860168 | tf_op jit(solution)/shard_map/ppermute | solution.py:89
  146.7 83.6 %collective-permute-start.45 = (bf16[2,2,56,1280]{3,2,1,0:T(8,128)(2,1)}, bf16[2,2,56,1280]{3,2,1,0:T(8,128)(2,1)}, u32[]{:S(2)}, u32[]{:S(2)}) collective-permute-start(bf16[2,2,56,1280]{3,2,1,0:T(8,128)(2,1)} %get-tuple-element.88), channel_id=1, source_target_pairs={{0,4},{2,6},{4,0},{6,2},{8,12},{10,14},{12,8},{14,10},{1,5},{3,7},... | collective-permute-start | bytes 1720328 | tf_op jit(solution)/shard_map/ppermute | solution.py:89
  152.1 8.4 %collective-permute-start.32 = (bf16[128,896]{1,0:T(8,128)(2,1)S(1)}, bf16[128,896]{1,0:T(8,128)(2,1)S(1)}, u32[]{:S(2)}, u32[]{:S(2)}) collective-permute-start(bf16[128,896]{1,0:T(8,128)(2,1)S(1)} %fusion.19), channel_id=1, source_target_pairs={{0,1},{1,0},{2,3},{3,2},{4,5},{5,4},{6,7},{7,6},{8,9},{9,8},{10,11... | collective-permute-start | bytes 688136 | tf_op jit(solution)/shard_map/ppermute | solution.py:82
  153.2 6.1 %collective-permute-start.30 = (bf16[128,896]{1,0:T(8,128)(2,1)S(1)}, bf16[128,896]{1,0:T(8,128)(2,1)S(1)}, u32[]{:S(2)}, u32[]{:S(2)}) collective-permute-start(bf16[128,896]{1,0:T(8,128)(2,1)S(1)} %slice.676), channel_id=1, source_target_pairs={{0,2},{2,0},{4,6},{6,4},{8,10},{10,8},{12,14},{14,12},{1,3},{3,1},... | collective-permute-start | bytes 688136 | tf_op jit(solution)/shard_map/ppermute | solution.py:85
  159.4 6.1 %collective-permute-start.31 = (bf16[128,896]{1,0:T(8,128)(2,1)S(1)}, bf16[128,896]{1,0:T(8,128)(2,1)S(1)}, u32[]{:S(2)}, u32[]{:S(2)}) collective-permute-start(bf16[128,896]{1,0:T(8,128)(2,1)S(1)} %fusion.18), channel_id=1, source_target_pairs={{0,1},{1,0},{2,3},{3,2},{4,5},{5,4},{6,7},{7,6},{8,9},{9,8},{10,11... | collective-permute-start | bytes 688136 | tf_op jit(solution)/shard_map/ppermute | solution.py:82
  184.5 6.1 %collective-permute-start.36 = (bf16[128,128]{0,1:T(8,128)(2,1)S(1)}, bf16[128,128]{0,1:T(8,128)(2,1)S(1)}, u32[]{:S(2)}, u32[]{:S(2)}) collective-permute-start(bf16[128,128]{0,1:T(8,128)(2,1)S(1)} %get-tuple-element.169), channel_id=1, source_target_pairs={{0,12},{2,14},{4,8},{6,10},{8,4},{10,6},{12,0},{14,2},{1,13},{3,15... | collective-permute-start | bytes 98312 | tf_op jit(solution)/shard_map/ppermute | solution.py:89
  186.4 16.0 %collective-permute-start.35 = (bf16[128,128]{0,1:T(8,128)(2,1)S(1)}, bf16[128,128]{0,1:T(8,128)(2,1)S(1)}, u32[]{:S(2)}, u32[]{:S(2)}) collective-permute-start(bf16[128,128]{0,1:T(8,128)(2,1)S(1)} %get-tuple-element.170), channel_id=1, source_target_pairs={{0,8},{2,10},{4,12},{6,14},{8,0},{10,2},{12,4},{14,6},{1,9},{3,11}... | collective-permute-start | bytes 98312 | tf_op jit(solution)/shard_map/ppermute | solution.py:89
  188.1 42.2 %collective-permute-start.47 = (bf16[2,2,56,1280]{3,2,1,0:T(8,128)(2,1)}, bf16[2,2,56,1280]{3,2,1,0:T(8,128)(2,1)S(1)}, u32[]{:S(2)}, u32[]{:S(2)}) collective-permute-start(bf16[2,2,56,1280]{3,2,1,0:T(8,128)(2,1)} %add_convert_fusion.1), channel_id=1, source_target_pairs={{0,8},{2,10},{4,12},{6,14},{8,0},{10,2},{12,4},{14,6},{1,9},{3,11}... | collective-permute-start | bytes 1720328 | tf_op jit(solution)/shard_map/ppermute | solution.py:89
  190.6 20.1 %collective-permute-start.40 = (bf16[4,2,56,448]{3,2,0,1:T(8,128)(2,1)}, bf16[4,2,56,448]{3,2,0,1:T(8,128)(2,1)}, u32[]{:S(2)}, u32[]{:S(2)}) collective-permute-start(bf16[4,2,56,448]{3,2,0,1:T(8,128)(2,1)} %select_bitcast_fusion.3), channel_id=1, source_target_pairs={{0,16},{16,0},{1,17},{17,1},{2,18},{18,2},{3,19},{19,3},{4,20},{20... | collective-permute-start | bytes 1204232 | tf_op jit(solution)/shard_map/ppermute | solution.py:79
  203.4 6.1 %collective-permute-start.37 = (bf16[128,896]{1,0:T(8,128)(2,1)S(1)}, bf16[128,896]{1,0:T(8,128)(2,1)S(1)}, u32[]{:S(2)}, u32[]{:S(2)}) collective-permute-start(bf16[128,896]{1,0:T(8,128)(2,1)S(1)} %convolution_convert_fusion.4), channel_id=1, source_target_pairs={{0,1},{1,0},{2,3},{3,2},{4,5},{5,4},{6,7},{7,6},{8,9},{9,8},{10,11... | collective-permute-start | bytes 688136 | tf_op jit(solution)/shard_map/ppermute | solution.py:82
  210.7 19.6 %collective-permute-start.52 = (bf16[2,2,56,640]{3,2,1,0:T(8,128)(2,1)}, bf16[2,2,56,640]{3,2,1,0:T(8,128)(2,1)S(1)}, u32[]{:S(2)}, u32[]{:S(2)}) collective-permute-start(bf16[2,2,56,640]{3,2,1,0:T(8,128)(2,1)} %add_convert_fusion.3), channel_id=1, source_target_pairs={{0,8},{2,10},{4,12},{6,14},{8,0},{10,2},{12,4},{14,6},{1,9},{3,11}... | collective-permute-start | bytes 860168 | tf_op jit(solution)/shard_map/ppermute | solution.py:89
  214.3 7.8 %collective-permute-start.41 = (bf16[4,56,448]{2,1,0:T(8,128)(2,1)S(1)}, bf16[4,56,448]{2,1,0:T(8,128)(2,1)S(1)}, u32[]{:S(2)}, u32[]{:S(2)}) collective-permute-start(bf16[4,56,448]{2,1,0:T(8,128)(2,1)S(1)} %fusion.33), channel_id=1, source_target_pairs={{0,2},{2,0},{4,6},{6,4},{8,10},{10,8},{12,14},{14,12},{1,3},{3,1},... | collective-permute-start | bytes 602120 | tf_op jit(solution)/shard_map/ppermute | solution.py:85
  222.1 8.1 %collective-permute-start.39 = (bf16[4,56,576]{2,1,0:T(8,128)(2,1)S(1)}, bf16[4,56,576]{2,1,0:T(8,128)(2,1)S(1)}, u32[]{:S(2)}, u32[]{:S(2)}) collective-permute-start(bf16[4,56,576]{2,1,0:T(8,128)(2,1)S(1)} %fusion.27), channel_id=1, source_target_pairs={{0,2},{2,0},{4,6},{6,4},{8,10},{10,8},{12,14},{14,12},{1,3},{3,1},... | collective-permute-start | bytes 774152 | tf_op jit(solution)/shard_map/ppermute | solution.py:85
  224.7 20.6 %all-to-all-start = ((f32[16,8,128]{2,1,0:T(8,128)}), f32[16,8,128]{2,1,0:T(8,128)S(1)}, u32[]{:S(2)}, u32[]{:S(2)}) async-start(f32[16,8,128]{2,1,0:T(8,128)} %select_maximum_fusion), calls=%async_computation | async-start | bytes 131072 | tf_op jit(solution)/shard_map/all_to_all | solution.py:92
  231.4 14.9 %collective-permute-start.53 = (bf16[2,56,640]{2,1,0:T(8,128)(2,1)S(1)}, bf16[2,56,640]{2,1,0:T(8,128)(2,1)S(1)}, u32[]{:S(2)}, u32[]{:S(2)}) collective-permute-start(bf16[2,56,640]{2,1,0:T(8,128)(2,1)S(1)} %select_bitcast_fusion.16), channel_id=1, source_target_pairs={{0,16},{16,0},{1,17},{17,1},{2,18},{18,2},{3,19},{19,3},{4,20},{20... | collective-permute-start | bytes 430088 | tf_op jit(solution)/shard_map/ppermute | solution.py:79
  231.6 7.3 %collective-permute-start.42 = (bf16[56,1024]{1,0:T(8,128)(2,1)S(1)}, bf16[56,1024]{1,0:T(8,128)(2,1)S(1)}, u32[]{:S(2)}, u32[]{:S(2)}) collective-permute-start(bf16[56,1024]{1,0:T(8,128)(2,1)S(1)} %get-tuple-element.132), channel_id=1, source_target_pairs={{0,4},{2,6},{4,0},{6,2},{8,12},{10,14},{12,8},{14,10},{1,5},{3,7},... | collective-permute-start | bytes 344072 | tf_op jit(solution)/shard_map/ppermute | solution.py:89
  231.9 11.9 %collective-permute-start.43 = (bf16[56,1024]{1,0:T(8,128)(2,1)S(1)}, bf16[56,1024]{1,0:T(8,128)(2,1)S(1)}, u32[]{:S(2)}, u32[]{:S(2)}) collective-permute-start(bf16[56,1024]{1,0:T(8,128)(2,1)S(1)} %get-tuple-element.133), channel_id=1, source_target_pairs={{0,8},{2,10},{4,12},{6,14},{8,0},{10,2},{12,4},{14,6},{1,9},{3,11}... | collective-permute-start | bytes 344072 | tf_op jit(solution)/shard_map/ppermute | solution.py:89
  234.1 9.6 %collective-permute-start.44 = (bf16[56,1024]{1,0:T(8,128)(2,1)S(1)}, bf16[56,1024]{1,0:T(8,128)(2,1)S(1)}, u32[]{:S(2)}, u32[]{:S(2)}) collective-permute-start(bf16[56,1024]{1,0:T(8,128)(2,1)S(1)} %get-tuple-element.134), channel_id=1, source_target_pairs={{0,12},{2,14},{4,8},{6,10},{8,4},{10,6},{12,0},{14,2},{1,13},{3,15... | collective-permute-start | bytes 344072 | tf_op jit(solution)/shard_map/ppermute | solution.py:89
  237.4 10.6 %collective-permute-start.48 = (bf16[2,56,1280]{2,1,0:T(8,128)(2,1)S(1)}, bf16[2,56,1280]{2,1,0:T(8,128)(2,1)S(1)}, u32[]{:S(2)}, u32[]{:S(2)}) collective-permute-start(bf16[2,56,1280]{2,1,0:T(8,128)(2,1)S(1)} %select_bitcast_fusion.12), channel_id=1, source_target_pairs={{0,16},{16,0},{1,17},{17,1},{2,18},{18,2},{3,19},{19,3},{4,20},{20... | collective-permute-start | bytes 860168 | tf_op jit(solution)/shard_map/ppermute | solution.py:79
  246.4 6.7 %collective-permute-start.54 = (bf16[2,56,640]{2,1,0:T(8,128)(2,1)S(1)}, bf16[2,56,640]{2,1,0:T(8,128)(2,1)S(1)}, u32[]{:S(2)}, u32[]{:S(2)}) collective-permute-start(bf16[2,56,640]{2,1,0:T(8,128)(2,1)S(1)} %select_bitcast_fusion.15), channel_id=1, source_target_pairs={{0,2},{2,0},{4,6},{6,4},{8,10},{10,8},{12,14},{14,12},{1,3},{3,1},... | collective-permute-start | bytes 430088 | tf_op jit(solution)/shard_map/ppermute | solution.py:85
  248.1 9.2 %collective-permute-start.49 = (bf16[2,56,1280]{2,1,0:T(8,128)(2,1)S(1)}, bf16[2,56,1280]{2,1,0:T(8,128)(2,1)S(1)}, u32[]{:S(2)}, u32[]{:S(2)}) collective-permute-start(bf16[2,56,1280]{2,1,0:T(8,128)(2,1)S(1)} %select_bitcast_fusion.11), channel_id=1, source_target_pairs={{0,2},{2,0},{4,6},{6,4},{8,10},{10,8},{12,14},{14,12},{1,3},{3,1},... | collective-permute-start | bytes 860168 | tf_op jit(solution)/shard_map/ppermute | solution.py:85
  (59 other events, 561.2 us)
